TPU v7x, 256 devices: a whole 4x4x8 slice. The times are simulated.
256 devices in a mesh: shot: 8 (over z_hi, core), brick: 32 (over y, x, z_lo).
Axes of the slice: x: 4, y: 4, z: 8 (z_hi: 4, z_lo: 2; z = z_hi * 2 + z_lo), core: 2. Of those that a mesh axis runs over, the one named last changes fastest.
Arguments:
- field_prev: float32 [8, 128, 256, 256], P('shot', 'brick'), may hold values from -6 to 6
- field_now: float32 [8, 128, 256, 256], P('shot', 'brick'), may hold values from -6 to 6
- diag_coef: float32 [3, 128, 256, 256], P(None, 'brick'), may hold values from 0.06 to 0.22
- cross_coef: float32 [3, 128, 256, 256], P(None, 'brick'), may hold values from -0.08 to 0.08
- green: bfloat16 [8, 4096, 4096], P('shot', None, 'brick'), may hold values from -0.09375 to 0.09375
- delays: int32 [8], replicated, may hold values from 0 to 8
- past: bfloat16 [8, 8, 4096], P(None, 'shot', 'brick'), may hold values from -6 to 6
- rec_cell: int32 [8, 4096], P('shot', 'brick'), may hold values from 0 to 262143
- emit_cell: int32 [8, 4096], P('shot', 'brick'), may hold values from 0 to 262143
Outputs:
- field_before: float32 [8, 128, 256, 256], P('shot', 'brick')
- field_after: float32 [8, 128, 256, 256], P('shot', 'brick')
- recorded: bfloat16 [3, 8, 4096], P(None, 'shot', 'brick')
Inputs may be any that keep to these rules, and one draw needn't show every extreme that they name: `rec_cell`: entries of block b (points b * 128 to (b + 1) * 128 - 1) index cells of brick b, counted within the brick. `emit_cell`: entries of block b (points b * 128 to (b + 1) * 128 - 1) index cells of brick b, counted within the brick.
All inputs are finite; a program needn't handle non-finite values.
Results may differ from a plain program's by a relative error of at most 0.001.
Values may be sent and summed in bfloat16 or wider, within the bound.
No kernel may reach another device: no remote copies, remote signals or barrier semaphores. Data moves between devices by JAX's collectives and lax.ppermute only.
A program may use at most 64 MiB of HBM per device.

v0:
```python
import jax
import jax.numpy as jnp
from jax import lax
from jax.sharding import PartitionSpec as P

STEPS = 3


def with_halo(array, sides, width):
    for axis, dim in sides:
        size, length = (lax.axis_size(axis), array.shape[dim])
        up = [(i, (i + 1) % size) for i in range(size - 1)]
        down = [(j, i) for i, j in up]
        last = lax.slice_in_dim(array, length - width, length, axis=dim)
        leading = lax.slice_in_dim(array, 0, width, axis=dim)
        before = lax.ppermute(last, axis, up)
        after = lax.ppermute(leading, axis, down)
        array = jnp.concatenate([before, array, after], axis=dim)
    return array


def operate(padded, centre, diag_coef, cross_coef):
    width_x = centre.shape[1]
    width_y = centre.shape[2]
    width_z = centre.shape[3]

    def shifted(offset_x, offset_y, offset_z):
        return padded[
            :,
            1 + offset_x : 1 + offset_x + width_x,
            1 + offset_y : 1 + offset_y + width_y,
            1 + offset_z : 1 + offset_z + width_z,
        ]

    second = diag_coef[0] * (shifted(1, 0, 0) - 2.0 * centre + shifted(-1, 0, 0))
    second = second + diag_coef[1] * (shifted(0, 1, 0) - 2.0 * centre + shifted(0, -1, 0))
    second = second + diag_coef[2] * (shifted(0, 0, 1) - 2.0 * centre + shifted(0, 0, -1))
    mixed = cross_coef[0] * (
        shifted(1, 1, 0) - shifted(1, -1, 0) - shifted(-1, 1, 0) + shifted(-1, -1, 0)
    )
    mixed = mixed + cross_coef[1] * (
        shifted(1, 0, 1) - shifted(1, 0, -1) - shifted(-1, 0, 1) + shifted(-1, 0, -1)
    )
    mixed = mixed + cross_coef[2] * (
        shifted(0, 1, 1) - shifted(0, 1, -1) - shifted(0, -1, 1) + shifted(0, -1, -1)
    )
    return second + 0.5 * mixed


def on_device(
    field_prev, field_now, diag_coef, cross_coef, green, delays, past, rec_cell, emit_cell
):
    lag_rank = lax.axis_index("shot")
    steps_total = STEPS
    history = past.shape[0]
    my_delay = lax.dynamic_index_in_dim(delays, lag_rank, 0, keepdims=False)
    series = [lax.all_gather(past, "shot", axis=1, tiled=True)]
    earlier, current = (field_prev, field_now)
    recorded = []
    for moment in range(steps_total):
        flat_now = current.reshape(1, -1)
        sample = jnp.take(flat_now[0], rec_cell[0]).astype(jnp.bfloat16).reshape(1, -1)
        recorded.append(sample)
        series.append(lax.all_gather(sample, "shot", axis=0, tiled=True)[None])
        stacked = jnp.concatenate(series, 0)
        where_at = history + moment - my_delay
        chosen = lax.dynamic_index_in_dim(stacked, where_at, 0, keepdims=False)
        partial_value = lax.dot_general(
            chosen, green[0], (((1,), (1,)), ((), ())), preferred_element_type=jnp.float32
        )
        grouped = lax.psum_scatter(partial_value, "brick", scatter_dimension=1, tiled=True)
        emitted = lax.psum_scatter(grouped, "shot", scatter_dimension=0, tiled=True)
        extended = with_halo(current, (("brick", 1),), 1)
        padded = jnp.pad(extended, ((0, 0), (0, 0), (1, 1), (1, 1)))
        following = 2.0 * current - earlier + operate(padded, current, diag_coef, cross_coef)
        flat_next = following.reshape(1, -1)
        flat_next = flat_next.at[0, emit_cell[0]].add(emitted.reshape(-1))
        earlier, current = (current, flat_next.reshape(current.shape))
    return (earlier, current, jnp.stack(recorded))


def solution(mesh):
    return jax.shard_map(
        on_device,
        mesh=mesh,
        in_specs=(
            P("shot", "brick", None, None),
            P("shot", "brick", None, None),
            P(None, "brick", None, None),
            P(None, "brick", None, None),
            P("shot", None, "brick"),
            P(),
            P(None, "shot", "brick"),
            P("shot", "brick"),
            P("shot", "brick"),
        ),
        out_specs=(
            P("shot", "brick", None, None),
            P("shot", "brick", None, None),
            P(None, "shot", "brick"),
        ),
        check_vma=False,
    )
```

profile of v0, /device:TPU:1, one launch (start us, length us, event | category | flops | bytes accessed | tf_op | source)
XLA Modules:
  0.0 637.2 jit_solution(8118385071217548182)
XLA Ops:
  7.2 0.0 copy-start
  7.2 0.0 copy-start.10
  7.2 0.0 copy-start.4
  7.2 0.0 copy-start.8
  7.2 0.0 reduce-scatter.4.cloned.1.call-start
  7.3 1.9 fusion.78
  9.2 4.4 collective-permute-start.1
  13.5 1.3 collective-permute-start
  14.8 1.2 dynamic_slice.16
  17.4 0.7 compare_select_fusion
  18.1 18.3 %all_gather.12 = bf16[8,8,128]{2,0,1:T(8,128)(2,1)S(1)} all-gather(bf16[8,1,128]{2,0,1:T(8,128)(2,1)} %param.17), channel_id=1, replica_groups=mesh['shot'=8,'brick'=32] {'shot'}, dimensions={1}, use_global_device_ids=true | all-gather | bytes 18432 | tf_op jit(solution)/shard_map/all_gather | solution.py:57
  36.4 1.8 copy.29
  38.1 1.3 gather_fusion
  39.4 10.2 %all-gather.3 = bf16[8,1,128]{2,1,0:T(2,128)(2,1)S(1)} all-gather(bf16[1,1,128]{2,1,0:T(2,128)(2,1)S(1)} %get-tuple-element.13), channel_id=2, replica_groups=mesh['shot'=8,'brick'=32] {'shot'}, dimensions={0}, use_global_device_ids=true | all-gather | bytes 2304 | tf_op jit(solution)/shard_map/all_gather | solution.py:64
  49.6 1.0 fusion.52
  50.6 0.0 reduce-scatter.4.cloned.1.call-update
  50.7 0.0 reduce-scatter.6.cloned.1.call-start
  52.0 0.6 dynamic-slice
  52.6 0.7 select_maximum_fusion.4
  53.4 1.1 copy-done.1
  54.5 5.1 fusion.37
  59.6 0.5 copy.28
  60.2 130.5 %reduce-scatter.4.cloned.1.call-done = f32[8,128]{1,0:T(8,128)} async-done(((f32[8,4096]{1,0:T(8,128)}), f32[8,128]{1,0:T(8,128)}) %reduce-scatter.4.cloned.1.call-update) | async-done | bytes 4112 | tf_op jit(solution)/shard_map/reduce_scatter | solution.py:71
  190.7 39.9 %all-reduce.4 = f32[8,128]{1,0:T(8,128)S(1)} all-reduce(f32[8,128]{1,0:T(8,128)} %reduce-scatter.4.cloned.1.call-done), channel_id=6, replica_groups=mesh['shot'=8,'brick'=32] {'shot'}, use_global_device_ids=true, to_apply=%region_1.3.clone | all-reduce | flops 1024 | bytes 8192
  230.6 0.6 fusion.66
  231.2 1.7 scatter_fusion
  232.9 0.0 copy-start.6
  232.9 1.0 copy-done.6
  233.9 1.1 gather_fusion.1
  235.0 1.5 reshape.130
  236.6 10.5 %all-gather.4 = bf16[8,1,128]{2,1,0:T(2,128)(2,1)S(1)} all-gather(bf16[1,1,128]{2,1,0:T(2,128)(2,1)S(1)} %fusion.71), channel_id=3, replica_groups=mesh['shot'=8,'brick'=32] {'shot'}, dimensions={0}, use_global_device_ids=true | all-gather | bytes 2304 | tf_op jit(solution)/shard_map/all_gather | solution.py:64
  247.1 1.0 fusion.50
  248.1 0.0 reduce-scatter.6.cloned.1.call-update
  248.1 0.0 reduce-scatter.8.cloned.1.call-start
  248.2 0.8 fusion.77
  249.0 1.3 collective-permute-start.3
  250.3 1.3 collective-permute-start.2
  252.9 128.3 %reduce-scatter.6.cloned.1.call-done = f32[8,128]{1,0:T(8,128)} async-done(((f32[8,4096]{1,0:T(8,128)}), f32[8,128]{1,0:T(8,128)}) %reduce-scatter.6.cloned.1.call-update) | async-done | bytes 4112 | tf_op jit(solution)/shard_map/reduce_scatter | solution.py:71
  381.2 39.9 %all-reduce.5 = f32[8,128]{1,0:T(8,128)S(1)} all-reduce(f32[8,128]{1,0:T(8,128)} %reduce-scatter.6.cloned.1.call-done), channel_id=8, replica_groups=mesh['shot'=8,'brick'=32] {'shot'}, use_global_device_ids=true, to_apply=%region_4.6.clone | all-reduce | flops 1024 | bytes 8192
  421.1 0.8 fusion.67
  421.9 1.8 select_maximum_fusion.2
  423.8 5.0 fusion.22
  428.8 0.5 copy.30
  429.4 1.7 scatter_fusion.1
  431.0 0.0 copy-start.7
  431.0 1.0 copy-done.7
  432.0 1.1 gather_fusion.2
  433.2 1.5 reshape.134
  434.7 0.0 copy-start.5
  434.7 10.7 %all-gather.5 = bf16[8,1,128]{2,1,0:T(2,128)(2,1)S(1)} all-gather(bf16[1,1,128]{2,1,0:T(2,128)(2,1)S(1)} %fusion.70), channel_id=4, replica_groups=mesh['shot'=8,'brick'=32] {'shot'}, dimensions={0}, use_global_device_ids=true | all-gather | bytes 2304 | tf_op jit(solution)/shard_map/all_gather | solution.py:64
  445.4 1.0 fusion.48
  446.4 0.0 reduce-scatter.8.cloned.1.call-update
  446.5 0.8 fusion.76
  447.3 1.3 collective-permute-start.5
  448.6 1.3 collective-permute-start.4
  449.9 0.6 copy.24
  450.4 129.1 %reduce-scatter.8.cloned.1.call-done = f32[8,128]{1,0:T(8,128)} async-done(((f32[8,4096]{1,0:T(8,128)}), f32[8,128]{1,0:T(8,128)}) %reduce-scatter.8.cloned.1.call-update) | async-done | bytes 4112 | tf_op jit(solution)/shard_map/reduce_scatter | solution.py:71
  579.6 39.9 %all-reduce.6 = f32[8,128]{1,0:T(8,128)S(1)} all-reduce(f32[8,128]{1,0:T(8,128)} %reduce-scatter.8.cloned.1.call-done), channel_id=10, replica_groups=mesh['shot'=8,'brick'=32] {'shot'}, use_global_device_ids=true, to_apply=%region_7.9.clone | all-reduce | flops 1024 | bytes 8192
  619.5 0.8 fusion.68
  620.3 1.8 select_maximum_fusion
  622.1 5.0 fusion.7
  627.2 0.5 copy.31
  627.7 1.7 scatter_fusion.2
  629.4 1.3 reshape.138
  (28 shorter events, 0.1 us)
Async XLA Ops:
  7.2 42.4 %copy-start = (bf16[1,4096,128]{2,1,0:T(8,128)(2,1)S(1)}, bf16[1,4096,128]{2,1,0:T(8,128)(2,1)}, u32[]{:S(2)}) copy-start(bf16[1,4096,128]{2,1,0:T(8,128)(2,1)} %param.15) | copy-start | bytes 3145732
  7.2 44.8 %copy-start.10 = (u32[256]{0:T(256)S(1)}, u32[256]{0:T(256)}, u32[]{:S(2)}) copy-start(u32[256]{0:T(256)} %constant.90) | copy-start | bytes 3076
  7.2 45.4 %copy-start.4 = (f32[1,4,256,256]{3,2,1,0:T(8,128)S(1)}, f32[1,4,256,256]{3,2,1,0:T(8,128)}, u32[]{:S(2)}) copy-start(f32[1,4,256,256]{3,2,1,0:T(8,128)} %param.12) | copy-start | bytes 3145732
  7.2 32.2 %copy-start.8 = (s32[1,128]{1,0:T(1,128)S(1)}, s32[1,128]{1,0:T(1,128)}, u32[]{:S(2)}) copy-start(s32[1,128]{1,0:T(1,128)} %param.18) | copy-start | bytes 1540
  7.2 45.4 %copy-start.9 = (s32[1,128]{1,0:T(1,128)S(1)}, s32[1,128]{1,0:T(1,128)}, u32[]{:S(2)}) copy-start(s32[1,128]{1,0:T(1,128)} %param.19) | copy-start | bytes 1540
  7.2 183.5 %reduce-scatter.4.cloned.1.call-start = ((), (), s32[]{:S(2)}) async-start(), calls=%async_computation.3 | async-start | bytes 135168 | tf_op jit(solution)/shard_map/reduce_scatter | solution.py:71
  9.2 43.5 %collective-permute-start.1 = (f32[1,1,256,256]{3,2,1,0:T(8,128)}, f32[1,1,256,256]{3,2,1,0:T(8,128)S(1)}, u32[]{:S(2)}, u32[]{:S(2)}) collective-permute-start(f32[1,1,256,256]{3,2,1,0:T(8,128)} %get-tuple-element.19), channel_id=1, source_target_pairs={{0,1},{1,2},{2,3},{3,4},{4,5},{5,6},{6,7},{7,8},{8,9},{9,10},{10,1... | collective-permute-start | bytes 786440 | tf_op jit(solution)/shard_map/ppermute | solution.py:16
  13.5 39.1 %collective-permute-start = (f32[1,1,256,256]{3,2,1,0:T(8,128)S(1)}, f32[1,1,256,256]{3,2,1,0:T(8,128)S(1)}, u32[]{:S(2)}, u32[]{:S(2)}) collective-permute-start(f32[1,1,256,256]{3,2,1,0:T(8,128)S(1)} %get-tuple-element.20), channel_id=1, source_target_pairs={{1,0},{2,1},{3,2},{4,3},{5,4},{6,5},{7,6},{8,7},{9,8},{10,9},{11,1... | collective-permute-start | bytes 786440 | tf_op jit(solution)/shard_map/ppermute | solution.py:17
  50.7 330.6 %reduce-scatter.6.cloned.1.call-start = ((), (), s32[]{:S(2)}) async-start(), calls=%async_computation.4 | async-start | bytes 135168 | tf_op jit(solution)/shard_map/reduce_scatter | solution.py:71
  52.6 1.9 copy-start.1
  232.9 1.0 copy-start.6
  248.1 331.4 %reduce-scatter.8.cloned.1.call-start = ((), (), s32[]{:S(2)}) async-start(), calls=%async_computation.5 | async-start | bytes 135168 | tf_op jit(solution)/shard_map/reduce_scatter | solution.py:71
  249.0 172.9 %collective-permute-start.3 = (f32[1,1,256,256]{3,2,1,0:T(8,128)}, f32[1,1,256,256]{3,2,1,0:T(8,128)S(1)}, u32[]{:S(2)}, u32[]{:S(2)}) collective-permute-start(f32[1,1,256,256]{3,2,1,0:T(8,128)} %get-tuple-element.17), channel_id=1, source_target_pairs={{0,1},{1,2},{2,3},{3,4},{4,5},{5,6},{6,7},{7,8},{8,9},{9,10},{10,1... | collective-permute-start | bytes 786440 | tf_op jit(solution)/shard_map/ppermute | solution.py:16
  250.3 171.6 %collective-permute-start.2 = (f32[1,1,256,256]{3,2,1,0:T(8,128)}, f32[1,1,256,256]{3,2,1,0:T(8,128)}, u32[]{:S(2)}, u32[]{:S(2)}) collective-permute-start(f32[1,1,256,256]{3,2,1,0:T(8,128)} %get-tuple-element.18), channel_id=1, source_target_pairs={{1,0},{2,1},{3,2},{4,3},{5,4},{6,5},{7,6},{8,7},{9,8},{10,9},{11,1... | collective-permute-start | bytes 786440 | tf_op jit(solution)/shard_map/ppermute | solution.py:17
  421.1 2.6 copy-start.2
  431.0 1.0 copy-start.7
  434.7 187.4 %copy-start.5 = (f32[1,4,256,256]{3,2,1,0:T(8,128)}, f32[1,4,256,256]{3,2,1,0:T(8,128)S(1)}, u32[]{:S(2)}) copy-start(f32[1,4,256,256]{3,2,1,0:T(8,128)S(1)} %reshape.134) | copy-start | bytes 3145732
  447.3 173.0 %collective-permute-start.5 = (f32[1,1,256,256]{3,2,1,0:T(8,128)}, f32[1,1,256,256]{3,2,1,0:T(8,128)S(1)}, u32[]{:S(2)}, u32[]{:S(2)}) collective-permute-start(f32[1,1,256,256]{3,2,1,0:T(8,128)} %get-tuple-element.15), channel_id=1, source_target_pairs={{0,1},{1,2},{2,3},{3,4},{4,5},{5,6},{6,7},{7,8},{8,9},{9,10},{10,1... | collective-permute-start | bytes 786440 | tf_op jit(solution)/shard_map/ppermute | solution.py:16
  448.6 171.7 %collective-permute-start.4 = (f32[1,1,256,256]{3,2,1,0:T(8,128)}, f32[1,1,256,256]{3,2,1,0:T(8,128)}, u32[]{:S(2)}, u32[]{:S(2)}) collective-permute-start(f32[1,1,256,256]{3,2,1,0:T(8,128)} %get-tuple-element.16), channel_id=1, source_target_pairs={{1,0},{2,1},{3,2},{4,3},{5,4},{6,5},{7,6},{8,7},{9,8},{10,9},{11,1... | collective-permute-start | bytes 786440 | tf_op jit(solution)/shard_map/ppermute | solution.py:17
  619.5 2.7 copy-start.3
Sparse Core Ops, SparseCore 0:
  50.8 139.8 reduce-scatter.3
  248.2 132.9 reduce-scatter.5
  446.6 132.9 reduce-scatter.7
where the time goes:
time: 638 us; the launch traced here: 637 us
  waiting for transfers between devices  388 us (61%)
  blocking collectives  169 us (26%)
  other arithmetic  25.3 us (4%)
  local copies, waits for them, and re-layouts  22.5 us (4%)
  between operations  18 us (3%)
  starting transfers between devices  10.9 us (2%)
    reduce_scatter x3, waiting for transfers between devices, on_device(): lax.psum_scatter(partial_value, 'brick', scatter_dimension=1, tiled=True)  388 us
    unnamed x3, blocking collectives  120 us
    all_gather x3, blocking collectives, on_device(): series.append(lax.all_gather(sample, 'shot', axis=0, tiled=True)[None])  31.3 us
    all_gather x1, blocking collectives, on_device(): series = [lax.all_gather(past, 'shot', axis=1, tiled=True)]  18.3 us
    add x3, other arithmetic, on_device(): 2.0 * current - earlier + operate(padded, current, diag_coef, cross_coef)  15.2 us
  transfers between devices with their start and end apart: 9, of which 3 were waited for; matrix products, arithmetic and copies ran while one was open for 3% of the time, Pallas kernels for 0%

commit v1 on v0

v1 whole, which is shorter than its diff:
```python
import functools

import jax
import jax.numpy as jnp
from jax import lax
from jax.experimental import pallas as pl
from jax.experimental.pallas import tpu as pltpu
from jax.sharding import PartitionSpec as P

STEPS = 3
VMEM = pltpu.VMEM
SMEM = pltpu.SMEM


def spec(space):
    return pl.BlockSpec(memory_space=space)


def sheet_of(row, width):
    tall = jnp.transpose(jnp.broadcast_to(row, (128, 128)))
    return jnp.concatenate([tall] * (width // 128), axis=1)


def lanes_of(cells):
    column = sheet_of((cells & 255).astype(jnp.float32), 256).astype(jnp.int32)
    return lax.broadcasted_iota(jnp.int32, (128, 256), 1) == column


def gather_row(read, cell_smem, cell_vec, rows_ref):
    for j in range(128):
        rows_ref[j : j + 1, :] = read(cell_smem[0, j] >> 8)
    picked = jnp.where(lanes_of(cell_vec), rows_ref[...], 0.0)
    return jnp.sum(jnp.transpose(picked[:, :128] + picked[:, 128:]), axis=0, keepdims=True)


def plane_row(ref):
    return lambda row: ref[row >> 8, pl.ds(row & 255, 1), :]


def first_kernel(cell_smem, cell_vec, emit_vec, past_ref, field_ref, out_ref, rows_ref):
    sample = gather_row(plane_row(field_ref), cell_smem, cell_vec[...], rows_ref)
    sample = sample.astype(jnp.bfloat16).astype(jnp.float32)
    out_ref[0:8, :] = past_ref[...].astype(jnp.float32)
    out_ref[8:9, :] = sample
    out_ref[9:10, :] = cell_vec[...].astype(jnp.float32)
    out_ref[10:11, :] = emit_vec[...].astype(jnp.float32)
    out_ref[11:16, :] = jnp.zeros((5, 128), jnp.float32)


def first_message(rec_cell, emit_cell, past, field):
    return pl.pallas_call(
        first_kernel,
        out_shape=jax.ShapeDtypeStruct((16, 128), jnp.float32),
        in_specs=[spec(SMEM), spec(VMEM), spec(VMEM), spec(VMEM), spec(VMEM)],
        out_specs=spec(VMEM),
        scratch_shapes=[pltpu.VMEM((128, 256), jnp.float32)],
        cost_estimate=pl.CostEstimate(flops=1 << 20, bytes_accessed=1 << 20, transcendentals=0),
        name="first_message",
    )(rec_cell, rec_cell, emit_cell, past, field)


def match_kernel(first_ref, out_ref):
    for s in range(8):
        rec = first_ref[s, 9:10, :]
        emit = first_ref[s, 10:11, :]
        same = sheet_of(emit, 128) == jnp.broadcast_to(rec, (128, 128))
        out_ref[s * 128 : (s + 1) * 128, :] = jnp.where(same, 1.0, 0.0).astype(jnp.bfloat16)


def matches(first):
    return pl.pallas_call(
        match_kernel,
        out_shape=jax.ShapeDtypeStruct((1024, 128), jnp.bfloat16),
        in_specs=[spec(VMEM)],
        out_specs=spec(VMEM),
        cost_estimate=pl.CostEstimate(flops=1 << 20, bytes_accessed=1 << 19, transcendentals=0),
        name="matches",
    )(first)


def multiply(chosen, green_ref, out_ref):
    left = chosen.astype(jnp.bfloat16)
    for b in range(32):
        out_ref[b] = lax.dot_general(
            left,
            green_ref[b * 128 : (b + 1) * 128, :],
            (((1,), (1,)), ((), ())),
            preferred_element_type=jnp.float32,
        )


def old_samples(first_ref, where):
    return jnp.concatenate([first_ref[s, pl.ds(where, 1), :] for s in range(8)], axis=0)


def start_kernel(delay, first_ref, green_ref, out_ref):
    multiply(old_samples(first_ref, 8 - delay[0]), green_ref, out_ref)


def emission_start(delay, first, green):
    return pl.pallas_call(
        start_kernel,
        out_shape=jax.ShapeDtypeStruct((32, 8, 128), jnp.float32),
        in_specs=[spec(SMEM), spec(VMEM), spec(VMEM)],
        out_specs=spec(VMEM),
        cost_estimate=pl.CostEstimate(flops=8 << 20, bytes_accessed=1 << 20, transcendentals=0),
        name="emission_start",
    )(delay, first, green)


def samples_kernel(moment, delay, *refs):
    message_ref, match_ref, first_ref, *newer_refs, green_ref, out_ref, emitted_ref, sample_ref = refs
    total = message_ref[0, 0:8, :]
    for lag in range(1, 8):
        total = total + message_ref[lag, 0:8, :]
    emitted_ref[...] = total
    values = jnp.concatenate([message_ref[s, 8:9, :] for s in range(8)], axis=0)
    wide = jnp.concatenate([total] * 8, axis=1)
    block = lax.broadcasted_iota(jnp.int32, (8, 1024), 1) >> 7
    wide = jnp.where(block == lax.broadcasted_iota(jnp.int32, (8, 1024), 0), wide, 0.0)
    high = wide.astype(jnp.bfloat16)
    rest = wide - high.astype(jnp.float32)
    middle = rest.astype(jnp.bfloat16)
    low = (rest - middle.astype(jnp.float32)).astype(jnp.bfloat16)
    parts = jnp.concatenate([high, middle, low], axis=0)
    added = jnp.dot(parts, match_ref[...], preferred_element_type=jnp.float32)
    values = values + ((added[16:24] + added[8:16]) + added[0:8])
    sample = values.astype(jnp.bfloat16).astype(jnp.float32)
    sample_ref[...] = sample
    where = 8 + moment - delay[0]
    chosen = old_samples(first_ref, jnp.minimum(where, 8))
    for k, newer_ref in enumerate(newer_refs):
        chosen = jnp.where(where == 9 + k, newer_ref[...], chosen)
    chosen = jnp.where(where == 8 + moment, sample, chosen)
    multiply(chosen, green_ref, out_ref)


def samples_and_emission(moment, delay, message, match, first, newer, green):
    return pl.pallas_call(
        functools.partial(samples_kernel, moment),
        out_shape=(
            jax.ShapeDtypeStruct((32, 8, 128), jnp.float32),
            jax.ShapeDtypeStruct((8, 128), jnp.float32),
            jax.ShapeDtypeStruct((8, 128), jnp.float32),
        ),
        in_specs=[spec(SMEM)] + [spec(VMEM)] * (4 + len(newer)),
        out_specs=(spec(VMEM),) * 3,
        cost_estimate=pl.CostEstimate(flops=8 << 20, bytes_accessed=1 << 20, transcendentals=0),
        name="samples",
    )(delay, message, match, first, *newer, green)


def stencil_kernel(
    take, cell_smem, cell_vec, field_ref, prev_ref, low_ref, high_ref, diag_ref, cross_ref, out_ref, *rest
):
    chunk = 32
    lane = lax.broadcasted_iota(jnp.int32, (chunk, 256), 1)
    sub = lax.broadcasted_iota(jnp.int32, (chunk, 256), 0)
    last = lane == 255
    first = lane == 0

    def right(a):
        return jnp.where(last, 0.0, pltpu.roll(a, 255, 1))

    def left(a):
        return jnp.where(first, 0.0, pltpu.roll(a, 1, 1))

    for x in range(4):

        def load(dx, a, b):
            if x + dx < 0:
                return low_ref[a:b, :]
            if x + dx > 3:
                return high_ref[a:b, :]
            return field_ref[x + dx, a:b, :]

        for k in range(256 // chunk):
            a = k * chunk
            b = a + chunk

            def up(dx):
                if b < 256:
                    return load(dx, a + 1, b + 1)
                whole = load(dx, a, b)
                return jnp.where(sub == chunk - 1, 0.0, pltpu.roll(whole, chunk - 1, 0))

            def down(dx):
                if a > 0:
                    return load(dx, a - 1, b - 1)
                whole = load(dx, a, b)
                return jnp.where(sub == 0, 0.0, pltpu.roll(whole, 1, 0))

            mid = load(0, a, b)
            ahead = load(1, a, b)
            behind = load(-1, a, b)
            mid_up, mid_down = up(0), down(0)
            twice = 2.0 * mid
            slope_x = ahead - behind
            slope_y = mid_up - mid_down
            mixed = cross_ref[0, x, a:b, :] * ((up(1) - up(-1)) - (down(1) - down(-1)))
            mixed = mixed + cross_ref[1, x, a:b, :] * (right(slope_x) - left(slope_x))
            mixed = mixed + cross_ref[2, x, a:b, :] * (right(slope_y) - left(slope_y))
            second = diag_ref[0, x, a:b, :] * (ahead - twice + behind)
            second = second + diag_ref[1, x, a:b, :] * (mid_up - twice + mid_down)
            second = second + diag_ref[2, x, a:b, :] * (right(mid) - twice + left(mid))
            out_ref[x, a:b, :] = (twice - prev_ref[x, a:b, :]) + (second + 0.5 * mixed)
    if take:
        value_ref, rows_ref = rest
        value_ref[...] = gather_row(plane_row(out_ref), cell_smem, cell_vec[...], rows_ref)


def stencil(take, rec_cell, field, prev, low, high, diag, cross):
    out_shape = [jax.ShapeDtypeStruct((4, 256, 256), jnp.float32)]
    scratch = []
    if take:
        out_shape.append(jax.ShapeDtypeStruct((1, 128), jnp.float32))
        scratch.append(pltpu.VMEM((128, 256), jnp.float32))
    return pl.pallas_call(
        functools.partial(stencil_kernel, take),
        out_shape=tuple(out_shape),
        in_specs=[spec(SMEM)] + [spec(VMEM)] * 7,
        out_specs=(spec(VMEM),) * len(out_shape),
        scratch_shapes=scratch,
        cost_estimate=pl.CostEstimate(flops=16 << 20, bytes_accessed=10 << 20, transcendentals=0),
        name="stencil",
    )(rec_cell, rec_cell, field, prev, low, high, diag, cross)


def scatter_kernel(cell_smem, cell_vec, value_ref, field_ref, out_ref, rows_ref):
    out_ref[...] = field_ref[...]
    value = value_ref[...]
    rows_ref[...] = jnp.where(lanes_of(cell_vec[...]), sheet_of(value, 256), 0.0)
    for j in range(128):
        row = cell_smem[0, j] >> 8
        at = (row >> 8, pl.ds(row & 255, 1), slice(None))
        out_ref[at] = out_ref[at] + rows_ref[j : j + 1, :]


def scatter(emit_cell, value, field):
    return pl.pallas_call(
        scatter_kernel,
        out_shape=jax.ShapeDtypeStruct((4, 256, 256), jnp.float32),
        in_specs=[spec(SMEM)] + [spec(VMEM)] * 3,
        out_specs=spec(VMEM),
        scratch_shapes=[pltpu.VMEM((128, 256), jnp.float32)],
        cost_estimate=pl.CostEstimate(flops=1 << 20, bytes_accessed=2 << 20, transcendentals=0),
        name="scatter",
    )(emit_cell, emit_cell, value, field)


def spread_kernel(parts_ref, value_ref, out_ref):
    sums = [parts_ref[b] for b in range(4)]
    for b in range(4, 32):
        sums[b % 4] = sums[b % 4] + parts_ref[b]
    total = (sums[0] + sums[1]) + (sums[2] + sums[3])
    for s in range(8):
        out_ref[s, 0:8, :] = total
        out_ref[s, 8:16, :] = jnp.broadcast_to(value_ref[...], (8, 128))


def spread(parts, value):
    return pl.pallas_call(
        spread_kernel,
        out_shape=jax.ShapeDtypeStruct((8, 16, 128), jnp.float32),
        in_specs=[spec(VMEM)] * 2,
        out_specs=spec(VMEM),
        cost_estimate=pl.CostEstimate(flops=1 << 15, bytes_accessed=1 << 18, transcendentals=0),
        name="spread",
    )(parts, value)


def exchange(array, axis):
    return lax.all_to_all(array, axis, 0, 0, tiled=True)


def halos(field):
    size = lax.axis_size("brick")
    up = [(i, i + 1) for i in range(size - 1)]
    down = [(i + 1, i) for i in range(size - 1)]
    return lax.ppermute(field[3], "brick", up), lax.ppermute(field[0], "brick", down)


def on_device(field_prev, field_now, diag, cross, green, delays, past, rec_cell, emit_cell):
    rank = lax.axis_index("shot")
    delay = lax.dynamic_slice_in_dim(delays, rank, 1)
    earlier, current, green, past = field_prev[0], field_now[0], green[0], past[:, 0]

    message = first_message(rec_cell, emit_cell, past, current)
    first = exchange(jnp.broadcast_to(message[None], (8, 16, 128)), "shot")
    low, high = halos(current)
    following, value = stencil(True, rec_cell, current, earlier, low, high, diag, cross)
    parts = exchange(emission_start(delay, first, green), "brick")
    match = matches(first)

    samples = []
    for moment in (1, 2):
        answer = exchange(spread(parts, value), "shot")
        partial, emitted, sample = samples_and_emission(moment, delay, answer, match, first, samples, green)
        samples.append(sample)
        parts = exchange(partial, "brick")
        mine = lax.dynamic_slice_in_dim(emitted, rank, 1)
        earlier, current = current, scatter(emit_cell, mine, following)
        low, high = halos(current)
        if moment == 1:
            following, value = stencil(True, rec_cell, current, earlier, low, high, diag, cross)
        else:
            (following,) = stencil(False, rec_cell, current, earlier, low, high, diag, cross)
    final = exchange(jnp.sum(parts, axis=0), "shot")
    after = scatter(emit_cell, jnp.sum(final, axis=0, keepdims=True), following)
    recorded = [message[8:9]] + [lax.dynamic_slice_in_dim(s, rank, 1) for s in samples]
    recorded = jnp.stack([r.astype(jnp.bfloat16) for r in recorded])
    return current[None], after[None], recorded


def solution(mesh):
    return jax.shard_map(
        on_device,
        mesh=mesh,
        in_specs=(
            P("shot", "brick", None, None),
            P("shot", "brick", None, None),
            P(None, "brick", None, None),
            P(None, "brick", None, None),
            P("shot", None, "brick"),
            P(),
            P(None, "shot", "brick"),
            P("shot", "brick"),
            P("shot", "brick"),
        ),
        out_specs=(
            P("shot", "brick", None, None),
            P("shot", "brick", None, None),
            P(None, "shot", "brick"),
        ),
        check_vma=False,
    )
```

time: 638 us -> 161 us (0.25)
  the two profiles are of different devices: /device:TPU:1 before, /device:TPU:38 now
where the time goes in v1:
time: 161 us; the launch traced here: 159 us
  starting transfers between devices  72.7 us (45%)
  Pallas kernels  46.5 us (29%)
  waiting for transfers between devices  20.7 us (13%)
  local copies, waits for them, and re-layouts  17.6 us (11%)
    all_to_all x7, starting transfers between devices, exchange(): return lax.all_to_all(array, axis, 0, 0, tiled=True)  46.1 us
    all_to_all x7, waiting for transfers between devices, exchange(): return lax.all_to_all(array, axis, 0, 0, tiled=True)  20.7 us
    pallas_call x3, Pallas kernels, stencil(): pl.pallas_call(functools.partial(stencil_kernel, take), out_shape=tuple(o...  20.4 us
    ppermute x3, starting transfers between devices, halos(): lax.ppermute(field[3], 'brick', up)  18.4 us
    pallas_call x3, Pallas kernels, scatter(): pl.pallas_call(scatter_kernel, out_shape=jax.ShapeDtypeStruct((4, 256, 25...  8.65 us
    ppermute x3, starting transfers between devices, halos(): lax.ppermute(field[0], 'brick', down)  8.16 us
    unnamed x23, local copies, waits for them, and re-layouts  7.31 us
    pallas_call x2, Pallas kernels, samples_and_emission(): pl.pallas_call(functools.partial(samples_kernel, moment), out_shape=(jax....  6.98 us
  transfers between devices with their start and end apart: 13, of which 3 were waited for; matrix products, arithmetic and copies ran while one was open for 4% of the time, Pallas kernels for 14%

profile of v1, /device:TPU:38, one launch (start us, length us, event | category | flops | bytes accessed | tf_op | source)
XLA Modules:
  0.0 159.4 jit_solution(17517814386820890428)
XLA Ops:
  0.6 2.3 %first_message.1 = f32[16,128]{1,0:T(8,128)} custom-call(s32[1,128]{1,0:T(1,128)} %cell_vec.12, s32[1,128]{1,0:T(1,128)} %cell_vec.12, s32[1,128]{1,0:T(1,128)} %cell_vec.13, bf16[8,128]{1,0:T(8,128)(2,1)} %bitcast.35, f32[4,256,256]{2,1,0:T(8,128)} %bitcast.26), custom_call_target="tpu_custom_call" | custom-call | flops 1048576 | bytes 1048576 | tf_op jit(solution)/shard_map/first_message/pallas_call | solution.py:51
  3.0 1.3 broadcast_in_dim.15
  4.3 7.6 %all-to-all-start = ((f32[8,16,128]{2,1,0:T(8,128)}), f32[8,16,128]{2,1,0:T(8,128)S(1)}, u32[]{:S(2)}, u32[]{:S(2)}) async-start(f32[8,16,128]{2,1,0:T(8,128)} %broadcast_in_dim.15), calls=%async_computation | async-start | bytes 131072 | tf_op jit(solution)/shard_map/all_to_all | solution.py:273
  11.9 1.1 slice_bitcast_fusion.4
  12.9 2.9 %collective-permute-start.1 = (f32[256,256]{1,0:T(8,128)S(1)}, f32[256,256]{1,0:T(8,128)S(1)}, u32[]{:S(2)}, u32[]{:S(2)}) collective-permute-start(f32[256,256]{1,0:T(8,128)S(1)} %get-tuple-element.33), channel_id=1, source_target_pairs={{1,0},{2,1},{3,2},{4,3},{5,4},{6,5},{7,6},{8,7},{9,8},{10,9},{11,1... | collective-permute-start | bytes 786440 | tf_op jit(solution)/shard_map/ppermute | solution.py:280
  15.9 5.9 %collective-permute-start = (f32[256,256]{1,0:T(8,128)S(1)}, f32[256,256]{1,0:T(8,128)S(1)}, u32[]{:S(2)}, u32[]{:S(2)}) collective-permute-start(f32[256,256]{1,0:T(8,128)S(1)} %get-tuple-element.34), channel_id=1, source_target_pairs={{0,1},{1,2},{2,3},{3,4},{4,5},{5,6},{6,7},{7,8},{8,9},{9,10},{10,1... | collective-permute-start | bytes 786440 | tf_op jit(solution)/shard_map/ppermute | solution.py:280
  21.8 1.2 dynamic_slice.15.delay
  23.0 0.0 all-to-all-done.first_ref.refs_2_
  23.1 0.6 copy-done
  23.7 3.2 %emission_start.1 = f32[32,8,128]{2,1,0:T(8,128)} custom-call(s32[1]{0:T(128)} %dynamic_slice.15.delay, f32[8,16,128]{2,1,0:T(8,128)} %copy-done, bf16[4096,128]{1,0:T(8,128)(2,1)} %bitcast.29), custom_call_target="tpu_custom_call" | custom-call | flops 8388608 | bytes 1048576 | tf_op jit(solution)/shard_map/emission_start/pallas_call | solution.py:101
  26.9 8.2 %all-to-all-start.1 = ((f32[32,8,128]{2,1,0:T(8,128)}), f32[32,8,128]{2,1,0:T(8,128)S(1)}, u32[]{:S(2)}, u32[]{:S(2)}) async-start(f32[32,8,128]{2,1,0:T(8,128)} %emission_start.1), calls=%async_computation.1 | async-start | bytes 262144 | tf_op jit(solution)/shard_map/all_to_all | solution.py:273
  35.1 0.0 collective-permute-done.1.high_ref
  35.1 0.0 collective-permute-done.low_ref
  35.1 0.0 copy-start.6
  35.2 0.7 copy-done.4
  35.8 0.1 copy-done.6
  35.9 6.9 %stencil.3 = (f32[4,256,256]{2,1,0:T(8,128)}, f32[1,128]{1,0:T(1,128)}) custom-call(s32[1,128]{1,0:T(1,128)} %cell_vec.12, s32[1,128]{1,0:T(1,128)} %cell_vec.12, f32[4,256,256]{2,1,0:T(8,128)} %bitcast.27, f32[4,256,256]{2,1,0:T(8,128)} %bitcast.33, f32[256,256]{1,0:T(8,128)} %copy-done.6, f32[256,256]{1,0:T(8,128)} %copy-done.4, ...), custom_call_target="tpu_custom_call" | custom-call | flops 16777216 | bytes 10485760 | tf_op jit(solution)/shard_map/stencil/pallas_call | solution.py:218
  42.8 0.0 all-to-all-done.1.parts_ref
  42.8 0.6 copy-done.1
  43.5 1.6 spread.2
  45.1 7.2 %all-to-all-start.2 = ((f32[8,16,128]{2,1,0:T(8,128)}), f32[8,16,128]{2,1,0:T(8,128)S(1)}, u32[]{:S(2)}, u32[]{:S(2)}) async-start(f32[8,16,128]{2,1,0:T(8,128)} %spread.2), calls=%async_computation.2 | async-start | bytes 131072 | tf_op jit(solution)/shard_map/all_to_all | solution.py:273
  52.3 1.7 %matches.1.refs_1_ = bf16[1024,128]{1,0:T(8,128)(2,1)} custom-call(f32[8,16,128]{2,1,0:T(8,128)} %copy-done), custom_call_target="tpu_custom_call" | custom-call | flops 1048576 | bytes 524288 | tf_op jit(solution)/shard_map/matches/pallas_call | solution.py:71
  54.0 6.5 %all-to-all-done.2.refs_0_ = f32[8,16,128]{2,1,0:T(8,128)S(1)} async-done(((f32[8,16,128]{2,1,0:T(8,128)}), f32[8,16,128]{2,1,0:T(8,128)S(1)}, u32[]{:S(2)}, u32[]{:S(2)}) %all-to-all-start.2) | async-done | bytes 65568 | tf_op jit(solution)/shard_map/all_to_all | solution.py:273
  60.5 0.6 copy-done.10
  61.1 3.5 %samples.2 = (f32[32,8,128]{2,1,0:T(8,128)}, f32[8,128]{1,0:T(8,128)}, f32[8,128]{1,0:T(8,128)}) custom-call(s32[1]{0:T(128)} %dynamic_slice.15.delay, f32[8,16,128]{2,1,0:T(8,128)} %copy-done.10, bf16[1024,128]{1,0:T(8,128)(2,1)} %matches.1.refs_1_, f32[8,16,128]{2,1,0:T(8,128)} %copy-done, bf16[4096,128]{1,0:T(8,128)(2,1)} %bitcast.30), custom_call_target="tpu_custom_call" | custom-call | flops 8388608 | bytes 1048576 | tf_op jit(solution)/shard_map/samples/pallas_call | solution.py:139
  64.6 1.3 constant_dynamic-slice_fusion.3.value_ref
  65.9 2.9 %scatter.3.field_ref.prev_ref = f32[4,256,256]{2,1,0:T(8,128)} custom-call(s32[1,128]{1,0:T(1,128)} %cell_vec.13, s32[1,128]{1,0:T(1,128)} %cell_vec.13, f32[1,128]{1,0:T(1,128)} %constant_dynamic-slice_fusion.3.value_ref, f32[4,256,256]{2,1,0:T(8,128)} %get-tuple-element.16.field_ref), custom_call_target="tpu_custom_call" | custom-call | flops 1048576 | bytes 2097152 | tf_op jit(solution)/shard_map/scatter/pallas_call | solution.py:240
  68.7 1.1 slice_bitcast_fusion.2
  69.8 2.8 %collective-permute-start.3 = (f32[256,256]{1,0:T(8,128)S(1)}, f32[256,256]{1,0:T(8,128)S(1)}, u32[]{:S(2)}, u32[]{:S(2)}) collective-permute-start(f32[256,256]{1,0:T(8,128)S(1)} %get-tuple-element.31), channel_id=1, source_target_pairs={{1,0},{2,1},{3,2},{4,3},{5,4},{6,5},{7,6},{8,7},{9,8},{10,9},{11,1... | collective-permute-start | bytes 786440 | tf_op jit(solution)/shard_map/ppermute | solution.py:280
  72.6 6.1 %collective-permute-start.2 = (f32[256,256]{1,0:T(8,128)S(1)}, f32[256,256]{1,0:T(8,128)S(1)}, u32[]{:S(2)}, u32[]{:S(2)}) collective-permute-start(f32[256,256]{1,0:T(8,128)S(1)} %get-tuple-element.32), channel_id=1, source_target_pairs={{0,1},{1,2},{2,3},{3,4},{4,5},{5,6},{6,7},{7,8},{8,9},{9,10},{10,1... | collective-permute-start | bytes 786440 | tf_op jit(solution)/shard_map/ppermute | solution.py:280
  78.7 8.0 %all-to-all-start.3 = ((f32[32,8,128]{2,1,0:T(8,128)}), f32[32,8,128]{2,1,0:T(8,128)S(1)}, u32[]{:S(2)}, u32[]{:S(2)}) async-start(f32[32,8,128]{2,1,0:T(8,128)} %get-tuple-element.14), calls=%async_computation.3 | async-start | bytes 262144 | tf_op jit(solution)/shard_map/all_to_all | solution.py:273
  86.7 0.0 collective-permute-done.3.high_ref
  86.7 0.0 collective-permute-done.2.low_ref
  86.7 0.7 copy-done.7
  87.4 0.7 copy-done.8
  88.1 6.9 %stencil.4 = (f32[4,256,256]{2,1,0:T(8,128)}, f32[1,128]{1,0:T(1,128)}) custom-call(s32[1,128]{1,0:T(1,128)} %cell_vec.12, s32[1,128]{1,0:T(1,128)} %cell_vec.12, f32[4,256,256]{2,1,0:T(8,128)} %scatter.3.field_ref.prev_ref, f32[4,256,256]{2,1,0:T(8,128)} %bitcast.28, f32[256,256]{1,0:T(8,128)} %copy-done.8, f32[256,256]{1,0:T(8,128)} %copy-done.7, ...), custom_call_target="tpu_custom_call" | custom-call | flops 16777216 | bytes 10485760 | tf_op jit(solution)/shard_map/stencil/pallas_call | solution.py:218
  95.0 0.0 all-to-all-done.3.parts_ref
  95.0 0.6 copy-done.2
  95.7 1.5 spread.3
  97.2 3.3 %all-to-all-start.4 = ((f32[8,16,128]{2,1,0:T(8,128)}), f32[8,16,128]{2,1,0:T(8,128)S(1)}, u32[]{:S(2)}, u32[]{:S(2)}) async-start(f32[8,16,128]{2,1,0:T(8,128)} %spread.3), calls=%async_computation.4 | async-start | bytes 131072 | tf_op jit(solution)/shard_map/all_to_all | solution.py:273
  100.6 0.7 fusion.4
  101.3 7.5 %all-to-all-done.4.refs_0_ = f32[8,16,128]{2,1,0:T(8,128)S(1)} async-done(((f32[8,16,128]{2,1,0:T(8,128)}), f32[8,16,128]{2,1,0:T(8,128)S(1)}, u32[]{:S(2)}, u32[]{:S(2)}) %all-to-all-start.4) | async-done | bytes 65568 | tf_op jit(solution)/shard_map/all_to_all | solution.py:273
  108.7 0.6 copy-done.9
  109.4 3.5 %samples.3 = (f32[32,8,128]{2,1,0:T(8,128)}, f32[8,128]{1,0:T(8,128)}, f32[8,128]{1,0:T(8,128)}) custom-call(s32[1]{0:T(128)} %dynamic_slice.15.delay, f32[8,16,128]{2,1,0:T(8,128)} %copy-done.9, bf16[1024,128]{1,0:T(8,128)(2,1)} %matches.1.refs_1_, f32[8,16,128]{2,1,0:T(8,128)} %copy-done, f32[8,128]{1,0:T(8,128)} %get-tuple-element.18.refs_3_, ...), custom_call_target="tpu_custom_call" | custom-call | flops 8388608 | bytes 1048576 | tf_op jit(solution)/shard_map/samples/pallas_call | solution.py:139
  112.8 1.2 constant_dynamic-slice_fusion.2.value_ref
  114.0 8.3 %all-to-all-start.5 = ((f32[32,8,128]{2,1,0:T(8,128)}), f32[32,8,128]{2,1,0:T(8,128)S(1)}, u32[]{:S(2)}, u32[]{:S(2)}) async-start(f32[32,8,128]{2,1,0:T(8,128)} %get-tuple-element.21), calls=%async_computation.5 | async-start | bytes 262144 | tf_op jit(solution)/shard_map/all_to_all | solution.py:273
  122.3 2.9 %scatter.4.field_ref = f32[4,256,256]{2,1,0:T(8,128)} custom-call(s32[1,128]{1,0:T(1,128)} %cell_vec.13, s32[1,128]{1,0:T(1,128)} %cell_vec.13, f32[1,128]{1,0:T(1,128)} %constant_dynamic-slice_fusion.2.value_ref, f32[4,256,256]{2,1,0:T(8,128)} %get-tuple-element.20.field_ref), custom_call_target="tpu_custom_call" | custom-call | flops 1048576 | bytes 2097152 | tf_op jit(solution)/shard_map/scatter/pallas_call | solution.py:240
  125.2 1.1 slice_bitcast_fusion
  126.3 2.5 %collective-permute-start.5 = (f32[256,256]{1,0:T(8,128)S(1)}, f32[256,256]{1,0:T(8,128)S(1)}, u32[]{:S(2)}, u32[]{:S(2)}) collective-permute-start(f32[256,256]{1,0:T(8,128)S(1)} %get-tuple-element.29), channel_id=1, source_target_pairs={{1,0},{2,1},{3,2},{4,3},{5,4},{6,5},{7,6},{8,7},{9,8},{10,9},{11,1... | collective-permute-start | bytes 786440 | tf_op jit(solution)/shard_map/ppermute | solution.py:280
  128.8 6.4 %collective-permute-start.4 = (f32[256,256]{1,0:T(8,128)S(1)}, f32[256,256]{1,0:T(8,128)S(1)}, u32[]{:S(2)}, u32[]{:S(2)}) collective-permute-start(f32[256,256]{1,0:T(8,128)S(1)} %get-tuple-element.30), channel_id=1, source_target_pairs={{0,1},{1,2},{2,3},{3,4},{4,5},{5,6},{6,7},{7,8},{8,9},{9,10},{10,1... | collective-permute-start | bytes 786440 | tf_op jit(solution)/shard_map/ppermute | solution.py:280
  135.1 0.7 fusion.1
  135.8 0.7 fusion.3
  136.5 0.0 all-to-all-done.5
  136.5 0.6 reduce_sum.18
  137.1 3.5 %all-to-all-start.6 = ((f32[8,1,128]{2,1,0:T(1,128)}), f32[8,1,128]{2,1,0:T(1,128)S(1)}, u32[]{:S(2)}, u32[]{:S(2)}) async-start(f32[8,1,128]{2,1,0:T(1,128)} %bitcast.9), calls=%async_computation.6 | async-start | bytes 8192 | tf_op jit(solution)/shard_map/all_to_all | solution.py:273
  140.7 0.6 copy.13
  141.2 6.8 %all-to-all-done.6 = f32[8,1,128]{2,1,0:T(1,128)S(1)} async-done(((f32[8,1,128]{2,1,0:T(1,128)}), f32[8,1,128]{2,1,0:T(1,128)S(1)}, u32[]{:S(2)}, u32[]{:S(2)}) %all-to-all-start.6) | async-done | bytes 4128 | tf_op jit(solution)/shard_map/all_to_all | solution.py:273
  148.0 0.5 reduce_sum.19
  148.5 0.0 collective-permute-done.5.high_ref
  148.5 0.0 collective-permute-done.4.low_ref
  148.5 0.7 copy-done.3
  149.3 0.7 copy-done.5
  150.0 6.6 %stencil.5.field_ref = f32[4,256,256]{2,1,0:T(8,128)} custom-call(s32[1,128]{1,0:T(1,128)} %cell_vec.12, s32[1,128]{1,0:T(1,128)} %cell_vec.12, f32[4,256,256]{2,1,0:T(8,128)} %scatter.4.field_ref, f32[4,256,256]{2,1,0:T(8,128)} %scatter.3.field_ref.prev_ref, f32[256,256]{1,0:T(8,128)} %copy-done.5, f32[256,256]{1,0:T(8,128)} %copy-done.3, ...), custom_call_target="tpu_custom_call" | custom-call | flops 16777216 | bytes 10485760 | tf_op jit(solution)/shard_map/stencil/pallas_call | solution.py:218
  156.6 2.9 %scatter.5 = f32[4,256,256]{2,1,0:T(8,128)} custom-call(s32[1,128]{1,0:T(1,128)} %cell_vec.13, s32[1,128]{1,0:T(1,128)} %cell_vec.13, f32[1,128]{1,0:T(1,128)} %bitcast.36, f32[4,256,256]{2,1,0:T(8,128)} %stencil.5.field_ref), custom_call_target="tpu_custom_call" | custom-call | flops 1048576 | bytes 2097152 | tf_op jit(solution)/shard_map/scatter/pallas_call | solution.py:240
  (11 shorter events, 0.0 us)
Async XLA Ops:
  4.3 18.8 %all-to-all-start = ((f32[8,16,128]{2,1,0:T(8,128)}), f32[8,16,128]{2,1,0:T(8,128)S(1)}, u32[]{:S(2)}, u32[]{:S(2)}) async-start(f32[8,16,128]{2,1,0:T(8,128)} %broadcast_in_dim.15), calls=%async_computation | async-start | bytes 131072 | tf_op jit(solution)/shard_map/all_to_all | solution.py:273
  12.9 22.2 %collective-permute-start.1 = (f32[256,256]{1,0:T(8,128)S(1)}, f32[256,256]{1,0:T(8,128)S(1)}, u32[]{:S(2)}, u32[]{:S(2)}) collective-permute-start(f32[256,256]{1,0:T(8,128)S(1)} %get-tuple-element.33), channel_id=1, source_target_pairs={{1,0},{2,1},{3,2},{4,3},{5,4},{6,5},{7,6},{8,7},{9,8},{10,9},{11,1... | collective-permute-start | bytes 786440 | tf_op jit(solution)/shard_map/ppermute | solution.py:280
  15.9 19.3 %collective-permute-start = (f32[256,256]{1,0:T(8,128)S(1)}, f32[256,256]{1,0:T(8,128)S(1)}, u32[]{:S(2)}, u32[]{:S(2)}) collective-permute-start(f32[256,256]{1,0:T(8,128)S(1)} %get-tuple-element.34), channel_id=1, source_target_pairs={{0,1},{1,2},{2,3},{3,4},{4,5},{5,6},{6,7},{7,8},{8,9},{9,10},{10,1... | collective-permute-start | bytes 786440 | tf_op jit(solution)/shard_map/ppermute | solution.py:280
  23.0 0.6 copy-start
  26.9 15.9 %all-to-all-start.1 = ((f32[32,8,128]{2,1,0:T(8,128)}), f32[32,8,128]{2,1,0:T(8,128)S(1)}, u32[]{:S(2)}, u32[]{:S(2)}) async-start(f32[32,8,128]{2,1,0:T(8,128)} %emission_start.1), calls=%async_computation.1 | async-start | bytes 262144 | tf_op jit(solution)/shard_map/all_to_all | solution.py:273
  35.1 0.7 copy-start.4
  35.1 0.8 copy-start.6
  42.8 0.7 copy-start.1
  45.1 15.4 %all-to-all-start.2 = ((f32[8,16,128]{2,1,0:T(8,128)}), f32[8,16,128]{2,1,0:T(8,128)S(1)}, u32[]{:S(2)}, u32[]{:S(2)}) async-start(f32[8,16,128]{2,1,0:T(8,128)} %spread.2), calls=%async_computation.2 | async-start | bytes 131072 | tf_op jit(solution)/shard_map/all_to_all | solution.py:273
  60.5 0.6 copy-start.10
  69.8 16.9 %collective-permute-start.3 = (f32[256,256]{1,0:T(8,128)S(1)}, f32[256,256]{1,0:T(8,128)S(1)}, u32[]{:S(2)}, u32[]{:S(2)}) collective-permute-start(f32[256,256]{1,0:T(8,128)S(1)} %get-tuple-element.31), channel_id=1, source_target_pairs={{1,0},{2,1},{3,2},{4,3},{5,4},{6,5},{7,6},{8,7},{9,8},{10,9},{11,1... | collective-permute-start | bytes 786440 | tf_op jit(solution)/shard_map/ppermute | solution.py:280
  72.6 14.1 %collective-permute-start.2 = (f32[256,256]{1,0:T(8,128)S(1)}, f32[256,256]{1,0:T(8,128)S(1)}, u32[]{:S(2)}, u32[]{:S(2)}) collective-permute-start(f32[256,256]{1,0:T(8,128)S(1)} %get-tuple-element.32), channel_id=1, source_target_pairs={{0,1},{1,2},{2,3},{3,4},{4,5},{5,6},{6,7},{7,8},{8,9},{9,10},{10,1... | collective-permute-start | bytes 786440 | tf_op jit(solution)/shard_map/ppermute | solution.py:280
  78.7 16.4 %all-to-all-start.3 = ((f32[32,8,128]{2,1,0:T(8,128)}), f32[32,8,128]{2,1,0:T(8,128)S(1)}, u32[]{:S(2)}, u32[]{:S(2)}) async-start(f32[32,8,128]{2,1,0:T(8,128)} %get-tuple-element.14), calls=%async_computation.3 | async-start | bytes 262144 | tf_op jit(solution)/shard_map/all_to_all | solution.py:273
  86.7 0.7 copy-start.7
  87.4 0.7 copy-start.8
  95.0 0.7 copy-start.2
  97.2 11.5 %all-to-all-start.4 = ((f32[8,16,128]{2,1,0:T(8,128)}), f32[8,16,128]{2,1,0:T(8,128)S(1)}, u32[]{:S(2)}, u32[]{:S(2)}) async-start(f32[8,16,128]{2,1,0:T(8,128)} %spread.3), calls=%async_computation.4 | async-start | bytes 131072 | tf_op jit(solution)/shard_map/all_to_all | solution.py:273
  108.7 0.6 copy-start.9
  114.0 22.5 %all-to-all-start.5 = ((f32[32,8,128]{2,1,0:T(8,128)}), f32[32,8,128]{2,1,0:T(8,128)S(1)}, u32[]{:S(2)}, u32[]{:S(2)}) async-start(f32[32,8,128]{2,1,0:T(8,128)} %get-tuple-element.21), calls=%async_computation.5 | async-start | bytes 262144 | tf_op jit(solution)/shard_map/all_to_all | solution.py:273
  126.3 22.3 %collective-permute-start.5 = (f32[256,256]{1,0:T(8,128)S(1)}, f32[256,256]{1,0:T(8,128)S(1)}, u32[]{:S(2)}, u32[]{:S(2)}) collective-permute-start(f32[256,256]{1,0:T(8,128)S(1)} %get-tuple-element.29), channel_id=1, source_target_pairs={{1,0},{2,1},{3,2},{4,3},{5,4},{6,5},{7,6},{8,7},{9,8},{10,9},{11,1... | collective-permute-start | bytes 786440 | tf_op jit(solution)/shard_map/ppermute | solution.py:280
  128.8 19.8 %collective-permute-start.4 = (f32[256,256]{1,0:T(8,128)S(1)}, f32[256,256]{1,0:T(8,128)S(1)}, u32[]{:S(2)}, u32[]{:S(2)}) collective-permute-start(f32[256,256]{1,0:T(8,128)S(1)} %get-tuple-element.30), channel_id=1, source_target_pairs={{0,1},{1,2},{2,3},{3,4},{4,5},{5,6},{6,7},{7,8},{8,9},{9,10},{10,1... | collective-permute-start | bytes 786440 | tf_op jit(solution)/shard_map/ppermute | solution.py:280
  137.1 10.9 %all-to-all-start.6 = ((f32[8,1,128]{2,1,0:T(1,128)}), f32[8,1,128]{2,1,0:T(1,128)S(1)}, u32[]{:S(2)}, u32[]{:S(2)}) async-start(f32[8,1,128]{2,1,0:T(1,128)} %bitcast.9), calls=%async_computation.6 | async-start | bytes 8192 | tf_op jit(solution)/shard_map/all_to_all | solution.py:273
  148.5 0.7 copy-start.3
  149.3 0.7 copy-start.5

commit v2 on v1

v2 whole, which is shorter than its diff:
```python
import functools

import jax
import jax.numpy as jnp
from jax import lax
from jax.experimental import pallas as pl
from jax.experimental.pallas import tpu as pltpu
from jax.sharding import PartitionSpec as P


VMEM = pltpu.VMEM
SMEM = pltpu.SMEM
HBM = pltpu.HBM
DMA = pltpu.SemaphoreType.DMA
f32 = jnp.float32


def spec(space):
    return pl.BlockSpec(memory_space=space)


def near(array):
    return pltpu.with_memory_space_constraint(array, pltpu.MemorySpace.VMEM)


def distant(array):
    return pltpu.with_memory_space_constraint(array, pltpu.MemorySpace.HBM)


def call(kernel, out_shape, work, scalars=(), arrays=(), far=(), free=(), scratch=(), aliases=None, room=2):
    flops, moved = work
    return pl.pallas_call(
        kernel,
        out_shape=out_shape,
        in_specs=[spec(SMEM)] * len(scalars) + [spec(VMEM)] * len(arrays) + [spec(HBM)] * len(far) + [spec(pl.ANY)] * len(free),
        out_specs=jax.tree.map(lambda _: spec(VMEM), out_shape),
        scratch_shapes=list(scratch),
        input_output_aliases=aliases or {},
        cost_estimate=pl.CostEstimate(flops=flops, bytes_accessed=moved, transcendentals=0),
        compiler_params=pltpu.CompilerParams(vmem_limit_bytes=room << 20),
    )(*scalars, *[near(a) for a in arrays], *[distant(a) for a in far], *free)


def sheet_of(row, width):
    tall = jnp.transpose(jnp.broadcast_to(row, (128, 128)))
    return jnp.concatenate([tall] * (width // 128), axis=1)


def lanes_of(cells):
    column = sheet_of((cells & 255).astype(f32), 256).astype(jnp.int32)
    return lax.broadcasted_iota(jnp.int32, (128, 256), 1) == column


def gather_row(field_ref, cell_smem, cell_vec, rows_ref):
    for j in range(128):
        row = cell_smem[0, j] >> 8
        rows_ref[j : j + 1, :] = field_ref[row >> 8, pl.ds(row & 255, 1), :]
    picked = jnp.where(lanes_of(cell_vec), rows_ref[...], 0.0)
    return jnp.sum(jnp.transpose(picked[:, :128] + picked[:, 128:]), axis=0, keepdims=True)


def copies(pairs, sems):
    started = [pltpu.make_async_copy(a, b, sems.at[k]) for k, (a, b) in enumerate(pairs)]
    for copy in started:
        copy.start()
    return started


def first_kernel(
    rank,
    delays,
    cell_smem,
    field_any,
    past_any,
    rec_any,
    emit_any,
    out_ref,
    field_ref,
    first_ref,
    last_ref,
    rec_ref,
    emit_ref,
    own_ref,
    delay_ref,
    rows_ref,
    past_ref,
    sems,
):
    pairs = [(field_any, field_ref), (past_any, past_ref), (rec_any, rec_ref), (emit_any, emit_ref)]
    pairs += [(field_any.at[0], first_ref), (field_any.at[3], last_ref)]
    started = copies(pairs, sems)
    own = lax.broadcasted_iota(jnp.int32, (8, 128), 0) == rank[0]
    own_ref[...] = jnp.where(own, 1.0, 0.0)
    delay_ref[...] = jnp.full((8, 128), delays[rank[0]], jnp.int32)
    for copy in started:
        copy.wait()
    sample = gather_row(field_ref, cell_smem, rec_ref[...], rows_ref)
    out_ref[0, 0:8, :] = past_ref[...].astype(f32)
    out_ref[0, 8:9, :] = sample.astype(jnp.bfloat16).astype(f32)
    out_ref[0, 9:10, :] = rec_ref[...].astype(f32)
    out_ref[0, 10:11, :] = emit_ref[...].astype(f32)
    out_ref[0, 11:16, :] = jnp.zeros((5, 128), f32)
    for s in range(1, 8):
        out_ref[s] = out_ref[0]


def first_message(rank, delays, rec_cell, emit_cell, past, field):
    plane = VMEM((256, 256), f32)
    row = VMEM((1, 128), jnp.int32)
    return call(
        first_kernel,
        (
            VMEM((8, 16, 128), f32),
            VMEM((4, 256, 256), f32),
            plane,
            plane,
            row,
            row,
            VMEM((8, 128), f32),
            VMEM((8, 128), jnp.int32),
        ),
        (1 << 20, 1 << 19),
        scalars=[rank, delays, rec_cell],
        far=[field, past, rec_cell, emit_cell],
        scratch=[VMEM((128, 256), f32), VMEM((8, 128), jnp.bfloat16), DMA((6,))],
    )


def turn_kernel(green_any, right_ref, green_ref, sems):
    for copy in copies([(green_any, green_ref)], sems):
        copy.wait()
    for b in range(32):
        at = slice(b * 128, (b + 1) * 128)
        right_ref[:, at] = jnp.transpose(green_ref[at, :])


def turn(green):
    return call(
        turn_kernel,
        VMEM((128, 4096), jnp.bfloat16),
        (1 << 20, 1 << 20),
        far=[green],
        scratch=[VMEM((4096, 128), jnp.bfloat16), DMA((1,))],
    )


def match_kernel(first_ref, delay_ref, out_ref, old_ref):
    for s in range(8):
        rec = first_ref[s, 9:10, :]
        emit = first_ref[s, 10:11, :]
        same = sheet_of(emit, 128) == jnp.broadcast_to(rec, (128, 128))
        out_ref[s * 128 : (s + 1) * 128, :] = jnp.where(same, 1.0, 0.0).astype(jnp.bfloat16)
    for moment in (1, 2):
        old_ref[moment - 1] = old_samples(first_ref, 8 + moment - delay_ref[...])


def matches(first, delay):
    return call(
        match_kernel,
        (VMEM((1024, 128), jnp.bfloat16), VMEM((2, 8, 128), f32)),
        (1 << 20, 1 << 18),
        arrays=[first, delay],
    )


def multiply(chosen, right_ref, out_ref):
    product = jnp.dot(chosen.astype(jnp.bfloat16), right_ref[...], preferred_element_type=f32)
    for b in range(32):
        out_ref[b] = product[:, b * 128 : (b + 1) * 128]


def old_samples(first_ref, where):
    chosen = jnp.zeros((8, 128), f32)
    for k in range(9):
        series = jnp.concatenate([first_ref[s, k : k + 1, :] for s in range(8)], axis=0)
        chosen = jnp.where(where == k, series, chosen)
    return chosen


def start_kernel(first_ref, delay_ref, right_ref, out_ref):
    multiply(old_samples(first_ref, 8 - delay_ref[...]), right_ref, out_ref)


def emission_start(first, delay, right):
    out = VMEM((32, 8, 128), f32)
    return call(start_kernel, out, (8 << 20, 1 << 20), arrays=[first, delay, right])


def samples_kernel(moment, message_ref, match_ref, old_ref, delay_ref, own_ref, *refs):
    *newer_refs, right_ref, out_ref, mine_ref, sample_ref = refs
    total = message_ref[0, 0:8, :]
    for lag in range(1, 8):
        total = total + message_ref[lag, 0:8, :]
    values = jnp.concatenate([message_ref[s, 8:9, :] for s in range(8)], axis=0)
    wide = jnp.concatenate([total] * 8, axis=1)
    block = lax.broadcasted_iota(jnp.int32, (8, 1024), 1) >> 7
    wide = jnp.where(block == lax.broadcasted_iota(jnp.int32, (8, 1024), 0), wide, 0.0)
    high = wide.astype(jnp.bfloat16)
    rest = wide - high.astype(f32)
    middle = rest.astype(jnp.bfloat16)
    low = (rest - middle.astype(f32)).astype(jnp.bfloat16)
    parts = jnp.concatenate([high, middle, low], axis=0)
    added = jnp.dot(parts, match_ref[...], preferred_element_type=f32)
    values = values + ((added[16:24] + added[8:16]) + added[0:8])
    sample = values.astype(jnp.bfloat16).astype(f32)
    delay = delay_ref[...]
    chosen = old_ref[moment - 1]
    for k, newer_ref in enumerate(newer_refs):
        chosen = jnp.where(delay == moment - 1 - k, newer_ref[...], chosen)
    chosen = jnp.where(delay == 0, sample, chosen)
    multiply(chosen, right_ref, out_ref)
    sample_ref[...] = sample
    mine_ref[...] = jnp.sum(jnp.where(own_ref[...] > 0.5, total, 0.0), axis=0, keepdims=True)


def samples_and_emission(moment, message, match, old, delay, own, newer, right):
    return call(
        functools.partial(samples_kernel, moment),
        (VMEM((32, 8, 128), f32), VMEM((1, 128), f32), VMEM((8, 128), f32)),
        (8 << 20, 1 << 20),
        arrays=[message, match, old, delay, own, *newer, right],
    )


def stencil_kernel(take, cell_smem, cell_vec, field_ref, prev_any, diag_any, cross_any, low_any, high_any, *refs):
    *outs, prev_ref, diag_ref, cross_ref, low_ref, high_ref, sems, edge_sems = refs
    out_ref, *outs = outs
    order = (1, 2, 0, 3)
    started = {}
    for x in order:
        pairs = [(diag_any.at[k, x], diag_ref.at[k, x]) for k in range(3)]
        pairs += [(cross_any.at[k, x], cross_ref.at[k, x]) for k in range(3)]
        started[x] = copies([(prev_any.at[x], prev_ref.at[x])] + pairs, sems.at[x])
    edges = copies([(low_any, low_ref), (high_any, high_ref)], edge_sems)
    chunk = 32
    lane = lax.broadcasted_iota(jnp.int32, (chunk, 256), 1)
    sub = lax.broadcasted_iota(jnp.int32, (chunk, 256), 0)
    last = lane == 255
    first = lane == 0

    def right(a):
        return jnp.where(last, 0.0, pltpu.roll(a, 255, 1))

    def left(a):
        return jnp.where(first, 0.0, pltpu.roll(a, 1, 1))

    for x in order:
        if x == 0:
            for copy in edges:
                copy.wait()
        for copy in started[x]:
            copy.wait()

        def load(dx, a, b):
            if x + dx < 0:
                return low_ref[a:b, :]
            if x + dx > 3:
                return high_ref[a:b, :]
            return field_ref[x + dx, a:b, :]

        for k in range(256 // chunk):
            a = k * chunk
            b = a + chunk

            def up(dx):
                if b < 256:
                    return load(dx, a + 1, b + 1)
                whole = load(dx, a, b)
                return jnp.where(sub == chunk - 1, 0.0, pltpu.roll(whole, chunk - 1, 0))

            def down(dx):
                if a > 0:
                    return load(dx, a - 1, b - 1)
                whole = load(dx, a, b)
                return jnp.where(sub == 0, 0.0, pltpu.roll(whole, 1, 0))

            mid = load(0, a, b)
            ahead = load(1, a, b)
            behind = load(-1, a, b)
            mid_up, mid_down = up(0), down(0)
            twice = 2.0 * mid
            slope_x = ahead - behind
            slope_y = mid_up - mid_down
            mixed = cross_ref[0, x, a:b, :] * ((up(1) - up(-1)) - (down(1) - down(-1)))
            mixed = mixed + cross_ref[1, x, a:b, :] * (right(slope_x) - left(slope_x))
            mixed = mixed + cross_ref[2, x, a:b, :] * (right(slope_y) - left(slope_y))
            second = diag_ref[0, x, a:b, :] * (ahead - twice + behind)
            second = second + diag_ref[1, x, a:b, :] * (mid_up - twice + mid_down)
            second = second + diag_ref[2, x, a:b, :] * (right(mid) - twice + left(mid))
            out_ref[x, a:b, :] = (twice - prev_ref[x, a:b, :]) + (second + 0.5 * mixed)
    if take:
        value_ref, rows_ref = outs
        value_ref[...] = gather_row(out_ref, cell_smem, cell_vec[...], rows_ref)


def stencil(take, rec_cell, rec, field, prev, diag, cross, low, high):
    out_shape = [VMEM((4, 256, 256), f32)]
    scratch = []
    if take:
        out_shape.append(VMEM((1, 128), f32))
        scratch.append(VMEM((128, 256), f32))
    plane = VMEM((256, 256), f32)
    coef = VMEM((3, 4, 256, 256), f32)
    return call(
        functools.partial(stencil_kernel, take),
        tuple(out_shape),
        (16 << 20, 10 << 20),
        scalars=[rec_cell],
        arrays=[rec, field],
        far=[prev, diag, cross],
        free=[low, high],
        scratch=scratch + [VMEM((4, 256, 256), f32), coef, coef, plane, plane, DMA((4, 7)), DMA((2,))],
        room=10,
    )


def add_at(cell_smem, cell_vec, value, target_ref, rows_ref):
    rows_ref[...] = jnp.where(lanes_of(cell_vec[...]), sheet_of(value, 256), 0.0)
    for j in range(128):
        row = cell_smem[0, j] >> 8
        at = (row >> 8, pl.ds(row & 255, 1), slice(None))
        target_ref[at] = target_ref[at] + rows_ref[j : j + 1, :]


def scatter_kernel(cell_smem, cell_vec, mine_ref, field_ref, *refs):
    *refs, rows_ref = refs
    old = refs[: len(refs) - 4] if len(refs) > 3 else []
    out_ref, low_ref, high_ref = refs[len(old) : len(old) + 3]
    del field_ref
    add_at(cell_smem, cell_vec, mine_ref[...], out_ref, rows_ref)
    low_ref[...] = out_ref[0]
    high_ref[...] = out_ref[3]
    if old:
        own_ref, first_ref, *sample_refs = old
        own = own_ref[...] > 0.5
        start = jnp.concatenate([first_ref[s, 8:9, :] for s in range(8)], axis=0)
        series = [start] + [s[...] for s in sample_refs]
        series = [jnp.sum(jnp.where(own, s, 0.0), axis=0, keepdims=True) for s in series]
        refs[-1][...] = jnp.concatenate(series, axis=0).astype(jnp.bfloat16)


def scatter(emit_cell, emit, mine, field, old=()):
    plane = VMEM((256, 256), f32)
    outs = (VMEM((4, 256, 256), f32), plane, plane)
    if old:
        outs += (VMEM((3, 128), jnp.bfloat16),)
    return call(
        scatter_kernel,
        outs,
        (1 << 20, 1 << 19),
        scalars=[emit_cell],
        arrays=[emit, mine, field, *old],
        scratch=[VMEM((128, 256), f32)],
        aliases={3: 0},
    )


def last_kernel(cell_smem, cell_vec, parts_ref, field_ref, out_ref, rows_ref):
    out_ref[...] = field_ref[...]
    value = parts_ref[0]
    for lag in range(1, 8):
        value = value + parts_ref[lag]
    add_at(cell_smem, cell_vec, value, out_ref, rows_ref)


def last_scatter(emit_cell, emit, parts, field):
    return call(
        last_kernel,
        jax.ShapeDtypeStruct((4, 256, 256), f32),
        (1 << 20, 2 << 20),
        scalars=[emit_cell],
        arrays=[emit, parts, field],
        scratch=[VMEM((128, 256), f32)],
    )


def spread_kernel(parts_ref, *refs):
    *value_refs, out_ref = refs
    sums = [parts_ref[b] for b in range(4)]
    for b in range(4, 32):
        sums[b % 4] = sums[b % 4] + parts_ref[b]
    total = (sums[0] + sums[1]) + (sums[2] + sums[3])
    if not value_refs:
        for s in range(8):
            out_ref[s] = total[s : s + 1, :]
        return
    value = jnp.broadcast_to(value_refs[0][...], (8, 128))
    for s in range(8):
        out_ref[s, 0:8, :] = total
        out_ref[s, 8:16, :] = value


def spread(parts, *value):
    out = VMEM((8, 16 if value else 1, 128), f32)
    return call(spread_kernel, out, (1 << 15, 1 << 17), arrays=[parts, *value])


def exchange(array, axis):
    return lax.all_to_all(array, axis, 0, 0, tiled=True)


def halos(first_plane, last_plane):
    size = lax.axis_size("brick")
    up = [(i, i + 1) for i in range(size - 1)]
    down = [(i + 1, i) for i in range(size - 1)]
    low = lax.ppermute(last_plane, "brick", up)
    high = lax.ppermute(first_plane, "brick", down)
    return low, high


def steps(field_prev, field_now, diag, cross, green, delays, past, rec_cell, emit_cell):
    rank = lax.axis_index("shot").reshape(1)
    past = past[:, 0]

    message, current, *planes, rec, emit, own, delay = first_message(
        rank, delays, rec_cell, emit_cell, past, field_now[0]
    )
    first = exchange(message, "shot")
    low, high = halos(*planes)
    right = turn(green[0])
    following, value = stencil(True, rec_cell, rec, current, field_prev[0], diag, cross, low, high)
    partial = emission_start(first, delay, right)
    parts = exchange(partial, "brick")
    match, old = matches(first, delay)
    message = spread(parts, value)

    answer = exchange(message, "shot")
    partial, mine, sample1 = samples_and_emission(1, answer, match, old, delay, own, [], right)
    earlier = current
    current, *planes = scatter(emit_cell, emit, mine, following)
    low, high = halos(*planes)
    parts = exchange(partial, "brick")
    following, value = stencil(True, rec_cell, rec, current, earlier, diag, cross, low, high)
    message = spread(parts, value)

    answer = exchange(message, "shot")
    partial, mine, sample2 = samples_and_emission(2, answer, match, old, delay, own, [sample1], right)
    parts = exchange(partial, "brick")
    earlier = current
    current, *planes, recorded = scatter(emit_cell, emit, mine, following, (own, first, sample1, sample2))
    low, high = halos(*planes)
    (following,) = stencil(False, rec_cell, rec, current, earlier, diag, cross, low, high)
    message = spread(parts)
    parts = exchange(message, "shot")
    after = last_scatter(emit_cell, emit, parts, following)
    return current[None], after[None], recorded[:, None]


def solution(mesh):
    return jax.shard_map(
        steps,
        mesh=mesh,
        in_specs=(
            P("shot", "brick", None, None),
            P("shot", "brick", None, None),
            P(None, "brick", None, None),
            P(None, "brick", None, None),
            P("shot", None, "brick"),
            P(),
            P(None, "shot", "brick"),
            P("shot", "brick"),
            P("shot", "brick"),
        ),
        out_specs=(
            P("shot", "brick", None, None),
            P("shot", "brick", None, None),
            P(None, "shot", "brick"),
        ),
        check_vma=False,
    )
```

time: 161 us -> 132 us (0.82)
  the two profiles are of different devices: /device:TPU:38 before, /device:TPU:1 now
where the time goes in v2:
time: 132 us; the launch traced here: 131 us
  starting transfers between devices  53 us (40%)
  Pallas kernels  28.2 us (21%)
  blocking collectives  28.1 us (21%)
  waiting for transfers between devices  11.9 us (9%)
  local copies, waits for them, and re-layouts  8.79 us (7%)
    all_to_all x5, starting transfers between devices, exchange(): return lax.all_to_all(array, axis, 0, 0, tiled=True)  40.6 us
    pallas_call x15, Pallas kernels, call(): pl.pallas_call(kernel, out_shape=out_shape, in_specs=[spec(SMEM)] * len(s...  28.2 us
    all_to_all x2, blocking collectives, exchange(): return lax.all_to_all(array, axis, 0, 0, tiled=True)  28.1 us
    all_to_all x5, waiting for transfers between devices, exchange(): return lax.all_to_all(array, axis, 0, 0, tiled=True)  10.5 us
    unnamed x28, local copies, waits for them, and re-layouts  8.79 us
    ppermute x3, starting transfers between devices, halos(): low = lax.ppermute(last_plane, 'brick', up)  8.5 us
    ppermute x3, starting transfers between devices, halos(): high = lax.ppermute(first_plane, 'brick', down)  3.88 us
  transfers between devices with their start and end apart: 11, of which 4 were waited for; matrix products, arithmetic and copies ran while one was open for 1% of the time, Pallas kernels for 13%

profile of v2, /device:TPU:1, one launch (start us, length us, event | category | flops | bytes accessed | tf_op | source)
XLA Modules:
  0.0 130.9 jit_solution(2438779819339281644)
XLA Ops:
  0.6 0.0 copy-start.10
  0.6 0.0 copy-start.12
  0.7 0.6 copy-done.12
  1.3 3.2 %shard_map.112 = (f32[8,16,128]{2,1,0:T(8,128)}, f32[4,256,256]{2,1,0:T(8,128)S(1)}, f32[256,256]{1,0:T(8,128)S(1)}, f32[256,256]{1,0:T(8,128)S(1)}, s32[1,128]{...) custom-call(s32[1]{0:T(128)} %bitcast.rank, s32[8]{0:T(128)S(1)} %copy-done.12, ...), custom_call_target="tpu_custom_call" | custom-call | flops 1048576 | bytes 524288 | tf_op jit(solution)/shard_map/pallas_call | solution.py:32
  4.5 0.0 copy-start.1
  4.5 10.0 %all-to-all-start = ((f32[8,16,128]{2,1,0:T(8,128)}), f32[8,16,128]{2,1,0:T(8,128)S(1)}, u32[]{:S(2)}, u32[]{:S(2)}) async-start(f32[8,16,128]{2,1,0:T(8,128)} %get-tuple-element.31), calls=%async_computation | async-start | bytes 131072 | tf_op jit(solution)/shard_map/all_to_all | solution.py:399
  14.5 2.6 %collective-permute-start = (f32[256,256]{1,0:T(8,128)S(1)}, f32[256,256]{1,0:T(8,128)S(1)}, u32[]{:S(2)}, u32[]{:S(2)}) collective-permute-start(f32[256,256]{1,0:T(8,128)S(1)} %get-tuple-element.35), channel_id=1, source_target_pairs={{0,1},{1,2},{2,3},{3,4},{4,5},{5,6},{6,7},{7,8},{8,9},{9,10},{10,1... | collective-permute-start | bytes 786440 | tf_op jit(solution)/shard_map/ppermute | solution.py:406
  17.2 1.3 collective-permute-start.1
  18.5 1.6 %shard_map.113.right_ref.refs_0_.refs_1_ = bf16[128,4096]{1,0:T(8,128)(2,1)S(1)} custom-call(bf16[4096,128]{1,0:T(8,128)(2,1)} %bitcast.12), custom_call_target="tpu_custom_call" | custom-call | flops 1048576 | bytes 1048576 | tf_op jit(solution)/shard_map/pallas_call | solution.py:32
  20.0 2.0 %all-to-all-done.first_ref.refs_1_ = f32[8,16,128]{2,1,0:T(8,128)S(1)} async-done(((f32[8,16,128]{2,1,0:T(8,128)}), f32[8,16,128]{2,1,0:T(8,128)S(1)}, u32[]{:S(2)}, u32[]{:S(2)}) %all-to-all-start) | async-done | bytes 65568 | tf_op jit(solution)/shard_map/all_to_all | solution.py:399
  22.1 0.9 shard_map.114
  23.0 7.2 %all-to-all-start.1 = ((f32[32,8,128]{2,1,0:T(8,128)}), f32[32,8,128]{2,1,0:T(8,128)S(1)}, u32[]{:S(2)}, u32[]{:S(2)}) async-start(f32[32,8,128]{2,1,0:T(8,128)} %shard_map.114), calls=%async_computation.1 | async-start | bytes 262144 | tf_op jit(solution)/shard_map/all_to_all | solution.py:399
  30.2 0.0 collective-permute-done.low_any
  30.2 0.0 copy-start.2
  30.2 0.7 copy-done.2
  30.9 0.0 collective-permute-done.1.high_any
  30.9 0.0 copy-start.4
  30.9 0.7 copy-done.4
  31.6 0.0 copy-done.10
  31.6 0.0 copy-start.3
  31.6 0.9 copy-done.3
  32.6 0.0 copy-start.5
  32.6 0.9 copy-done.5
  33.5 4.8 %shard_map.115 = (f32[4,256,256]{2,1,0:T(8,128)S(1)}, f32[1,128]{1,0:T(1,128)S(1)}) custom-call(s32[1,128]{1,0:T(1,128)S(1)} %copy-done.10, s32[1,128]{1,0:T(1,128)S(1)} %get-tuple-element.33.cell_vec, f32[4,256,256]{2,1,0:T(8,128)S(1)} %get-tuple-element.34.field_ref.prev_any, f32[4,256,256]{2,1,0:T(8,128)} %bitcast.10, f32[3,4,256,256]{3,2,1,0:T(8,128)} %diag_any.5, ...), custom_call_target="tpu_custom_call" | custom-call | flops 16777216 | bytes 10485760 | tf_op jit(solution)/shard_map/pallas_call | solution.py:32
  38.4 0.0 copy-done.1
  38.4 0.0 all-to-all-done.1.parts_ref
  38.4 0.6 shard_map.116
  39.0 8.6 %all-to-all-start.2 = ((f32[8,16,128]{2,1,0:T(8,128)}), f32[8,16,128]{2,1,0:T(8,128)S(1)}, u32[]{:S(2)}, u32[]{:S(2)}) async-start(f32[8,16,128]{2,1,0:T(8,128)} %shard_map.116), calls=%async_computation.2 | async-start | bytes 131072 | tf_op jit(solution)/shard_map/all_to_all | solution.py:399
  47.6 0.2 shard_map.117
  47.8 7.4 %all-to-all-done.2.message_ref = f32[8,16,128]{2,1,0:T(8,128)S(1)} async-done(((f32[8,16,128]{2,1,0:T(8,128)}), f32[8,16,128]{2,1,0:T(8,128)S(1)}, u32[]{:S(2)}, u32[]{:S(2)}) %all-to-all-start.2) | async-done | bytes 65568 | tf_op jit(solution)/shard_map/all_to_all | solution.py:399
  55.3 1.1 shard_map.118
  56.3 0.0 copy-done.11
  56.3 1.2 shard_map.119
  57.5 0.0 copy-start
  57.5 2.8 %collective-permute-start.2 = (f32[256,256]{1,0:T(8,128)S(1)}, f32[256,256]{1,0:T(8,128)S(1)}, u32[]{:S(2)}, u32[]{:S(2)}) collective-permute-start(f32[256,256]{1,0:T(8,128)S(1)} %get-tuple-element.45), channel_id=1, source_target_pairs={{0,1},{1,2},{2,3},{3,4},{4,5},{5,6},{6,7},{7,8},{8,9},{9,10},{10,1... | collective-permute-start | bytes 786440 | tf_op jit(solution)/shard_map/ppermute | solution.py:406
  60.3 1.3 collective-permute-start.3
  61.6 8.7 %all-to-all-start.3 = ((f32[32,8,128]{2,1,0:T(8,128)}), f32[32,8,128]{2,1,0:T(8,128)}, u32[]{:S(2)}, u32[]{:S(2)}) async-start(f32[32,8,128]{2,1,0:T(8,128)} %get-tuple-element.41), calls=%async_computation.3 | async-start | bytes 262144 | tf_op jit(solution)/shard_map/all_to_all | solution.py:399
  70.4 0.0 collective-permute-done.2.low_any
  70.4 0.0 copy-start.6
  70.4 0.7 copy-done.6
  71.1 1.5 %collective-permute-done.3.high_any = f32[256,256]{1,0:T(8,128)S(1)} collective-permute-done((f32[256,256]{1,0:T(8,128)S(1)}, f32[256,256]{1,0:T(8,128)S(1)}, u32[]{:S(2)}, u32[]{:S(2)}) %collective-permute-start.3) | collective-permute-done | bytes 262176 | tf_op jit(solution)/shard_map/ppermute | solution.py:407
  72.6 0.0 copy-start.8
  72.6 0.7 copy-done.8
  73.3 0.9 copy-done.7
  74.2 0.9 copy-done.9
  75.2 4.8 %shard_map.120 = (f32[4,256,256]{2,1,0:T(8,128)S(1)}, f32[1,128]{1,0:T(1,128)S(1)}) custom-call(s32[1,128]{1,0:T(1,128)S(1)} %copy-done.10, s32[1,128]{1,0:T(1,128)S(1)} %get-tuple-element.33.cell_vec, f32[4,256,256]{2,1,0:T(8,128)S(1)} %get-tuple-element.44.field_ref.prev_any, f32[4,256,256]{2,1,0:T(8,128)} %copy-done.1, f32[3,4,256,256]{3,2,1,0:T(8,128)} %diag_any.5, ...), custom_call_target="tpu_custom_call" | custom-call | flops 16777216 | bytes 10485760 | tf_op jit(solution)/shard_map/pallas_call | solution.py:32
  80.0 0.0 copy-done
  80.0 0.0 all-to-all-done.3.parts_ref
  80.0 0.9 shard_map.121
  80.9 12.3 %all_to_all.35.message_ref = f32[8,16,128]{2,1,0:T(8,128)S(1)} all-to-all(f32[8,16,128]{2,1,0:T(8,128)S(1)} %shard_map.121), channel_id=1, replica_groups=mesh['shot'=8,'brick'=32] {'shot'}, dimensions={0} | all-to-all | bytes 131072 | tf_op jit(solution)/shard_map/all_to_all | solution.py:399
  93.2 0.4 shard_map.122
  93.6 1.2 shard_map.123
  94.9 3.1 %collective-permute-start.4 = (f32[256,256]{1,0:T(8,128)S(1)}, f32[256,256]{1,0:T(8,128)S(1)}, u32[]{:S(2)}, u32[]{:S(2)}) collective-permute-start(f32[256,256]{1,0:T(8,128)S(1)} %get-tuple-element.54), channel_id=1, source_target_pairs={{0,1},{1,2},{2,3},{3,4},{4,5},{5,6},{6,7},{7,8},{8,9},{9,10},{10,1... | collective-permute-start | bytes 786440 | tf_op jit(solution)/shard_map/ppermute | solution.py:406
  98.0 1.3 collective-permute-start.5
  99.2 15.9 %all_to_all.36.parts_ref = f32[32,8,128]{2,1,0:T(8,128)S(1)} all-to-all(f32[32,8,128]{2,1,0:T(8,128)S(1)} %get-tuple-element.53), channel_id=1, replica_groups=mesh['shot'=8,'brick'=32] {'brick'}, dimensions={0} | all-to-all | bytes 262144 | tf_op jit(solution)/shard_map/all_to_all | solution.py:399
  115.1 0.6 shard_map.124
  115.7 6.1 %all-to-all-start.6 = ((f32[8,1,128]{2,1,0:T(1,128)}), f32[8,1,128]{2,1,0:T(1,128)S(1)}, u32[]{:S(2)}, u32[]{:S(2)}) async-start(f32[8,1,128]{2,1,0:T(1,128)} %shard_map.124), calls=%async_computation.6 | async-start | bytes 8192 | tf_op jit(solution)/shard_map/all_to_all | solution.py:399
  121.8 0.6 copy.17
  122.4 1.0 copy.16
  123.3 0.0 collective-permute-done.4.low_any
  123.3 0.0 collective-permute-done.5.high_any
  123.3 4.4 %shard_map.125.field_ref = f32[4,256,256]{2,1,0:T(8,128)S(1)} custom-call(s32[1,128]{1,0:T(1,128)S(1)} %copy-done.10, s32[1,128]{1,0:T(1,128)S(1)} %get-tuple-element.33.cell_vec, f32[4,256,256]{2,1,0:T(8,128)S(1)} %get-tuple-element.52.field_ref, f32[4,256,256]{2,1,0:T(8,128)} %copy-done, f32[3,4,256,256]{3,2,1,0:T(8,128)} %diag_any.5, ...), custom_call_target="tpu_custom_call" | custom-call | flops 16777216 | bytes 10485760 | tf_op jit(solution)/shard_map/pallas_call | solution.py:32
  127.8 1.0 all-to-all-done.6.parts_ref
  128.8 2.1 %shard_map.126 = f32[4,256,256]{2,1,0:T(8,128)} custom-call(s32[1,128]{1,0:T(1,128)S(1)} %copy-done.11, s32[1,128]{1,0:T(1,128)S(1)} %get-tuple-element.30.cell_vec, f32[8,1,128]{2,1,0:T(1,128)S(1)} %all-to-all-done.6.parts_ref, f32[4,256,256]{2,1,0:T(8,128)S(1)} %shard_map.125.field_ref), custom_call_target="tpu_custom_call" | custom-call | flops 1048576 | bytes 2097152 | tf_op jit(solution)/shard_map/pallas_call | solution.py:32
  (3 shorter events, 0.0 us)
Async XLA Ops:
  0.6 31.0 %copy-start.10 = (s32[1,128]{1,0:T(1,128)S(1)}, s32[1,128]{1,0:T(1,128)}, u32[]{:S(2)}) copy-start(s32[1,128]{1,0:T(1,128)} %cell_smem.12) | copy-start | bytes 1540
  0.6 0.7 copy-start.12
  4.5 33.9 %copy-start.1 = (f32[4,256,256]{2,1,0:T(8,128)}, f32[4,256,256]{2,1,0:T(8,128)S(1)}, u32[]{:S(2)}) copy-start(f32[4,256,256]{2,1,0:T(8,128)S(1)} %get-tuple-element.34.field_ref.prev_any) | copy-start | bytes 3145732
  4.5 17.5 %all-to-all-start = ((f32[8,16,128]{2,1,0:T(8,128)}), f32[8,16,128]{2,1,0:T(8,128)S(1)}, u32[]{:S(2)}, u32[]{:S(2)}) async-start(f32[8,16,128]{2,1,0:T(8,128)} %get-tuple-element.31), calls=%async_computation | async-start | bytes 131072 | tf_op jit(solution)/shard_map/all_to_all | solution.py:399
  14.5 15.7 %collective-permute-start = (f32[256,256]{1,0:T(8,128)S(1)}, f32[256,256]{1,0:T(8,128)S(1)}, u32[]{:S(2)}, u32[]{:S(2)}) collective-permute-start(f32[256,256]{1,0:T(8,128)S(1)} %get-tuple-element.35), channel_id=1, source_target_pairs={{0,1},{1,2},{2,3},{3,4},{4,5},{5,6},{6,7},{7,8},{8,9},{9,10},{10,1... | collective-permute-start | bytes 786440 | tf_op jit(solution)/shard_map/ppermute | solution.py:406
  17.2 13.8 %collective-permute-start.1 = (f32[256,256]{1,0:T(8,128)S(1)}, f32[256,256]{1,0:T(8,128)S(1)}, u32[]{:S(2)}, u32[]{:S(2)}) collective-permute-start(f32[256,256]{1,0:T(8,128)S(1)} %get-tuple-element.36), channel_id=1, source_target_pairs={{1,0},{2,1},{3,2},{4,3},{5,4},{6,5},{7,6},{8,7},{9,8},{10,9},{11,1... | collective-permute-start | bytes 786440 | tf_op jit(solution)/shard_map/ppermute | solution.py:407
  23.0 15.4 %all-to-all-start.1 = ((f32[32,8,128]{2,1,0:T(8,128)}), f32[32,8,128]{2,1,0:T(8,128)S(1)}, u32[]{:S(2)}, u32[]{:S(2)}) async-start(f32[32,8,128]{2,1,0:T(8,128)} %shard_map.114), calls=%async_computation.1 | async-start | bytes 262144 | tf_op jit(solution)/shard_map/all_to_all | solution.py:399
  30.2 0.7 copy-start.2
  30.9 0.7 copy-start.4
  31.6 1.0 copy-start.3
  32.6 0.9 copy-start.5
  33.5 22.8 %copy-start.11 = (s32[1,128]{1,0:T(1,128)S(1)}, s32[1,128]{1,0:T(1,128)}, u32[]{:S(2)}) copy-start(s32[1,128]{1,0:T(1,128)} %cell_smem.13) | copy-start | bytes 1540
  39.0 16.2 %all-to-all-start.2 = ((f32[8,16,128]{2,1,0:T(8,128)}), f32[8,16,128]{2,1,0:T(8,128)S(1)}, u32[]{:S(2)}, u32[]{:S(2)}) async-start(f32[8,16,128]{2,1,0:T(8,128)} %shard_map.116), calls=%async_computation.2 | async-start | bytes 131072 | tf_op jit(solution)/shard_map/all_to_all | solution.py:399
  57.5 22.5 %copy-start = (f32[4,256,256]{2,1,0:T(8,128)}, f32[4,256,256]{2,1,0:T(8,128)S(1)}, u32[]{:S(2)}) copy-start(f32[4,256,256]{2,1,0:T(8,128)S(1)} %get-tuple-element.44.field_ref.prev_any) | copy-start | bytes 3145732
  57.5 12.8 %collective-permute-start.2 = (f32[256,256]{1,0:T(8,128)S(1)}, f32[256,256]{1,0:T(8,128)S(1)}, u32[]{:S(2)}, u32[]{:S(2)}) collective-permute-start(f32[256,256]{1,0:T(8,128)S(1)} %get-tuple-element.45), channel_id=1, source_target_pairs={{0,1},{1,2},{2,3},{3,4},{4,5},{5,6},{6,7},{7,8},{8,9},{9,10},{10,1... | collective-permute-start | bytes 786440 | tf_op jit(solution)/shard_map/ppermute | solution.py:406
  60.3 12.2 %collective-permute-start.3 = (f32[256,256]{1,0:T(8,128)S(1)}, f32[256,256]{1,0:T(8,128)S(1)}, u32[]{:S(2)}, u32[]{:S(2)}) collective-permute-start(f32[256,256]{1,0:T(8,128)S(1)} %get-tuple-element.46), channel_id=1, source_target_pairs={{1,0},{2,1},{3,2},{4,3},{5,4},{6,5},{7,6},{8,7},{9,8},{10,9},{11,1... | collective-permute-start | bytes 786440 | tf_op jit(solution)/shard_map/ppermute | solution.py:407
  61.6 18.4 %all-to-all-start.3 = ((f32[32,8,128]{2,1,0:T(8,128)}), f32[32,8,128]{2,1,0:T(8,128)}, u32[]{:S(2)}, u32[]{:S(2)}) async-start(f32[32,8,128]{2,1,0:T(8,128)} %get-tuple-element.41), calls=%async_computation.3 | async-start | bytes 262144 | tf_op jit(solution)/shard_map/all_to_all | solution.py:399
  70.4 0.7 copy-start.6
  72.6 0.7 copy-start.8
  73.3 0.9 copy-start.7
  74.2 0.9 copy-start.9
  94.9 28.5 %collective-permute-start.4 = (f32[256,256]{1,0:T(8,128)S(1)}, f32[256,256]{1,0:T(8,128)S(1)}, u32[]{:S(2)}, u32[]{:S(2)}) collective-permute-start(f32[256,256]{1,0:T(8,128)S(1)} %get-tuple-element.54), channel_id=1, source_target_pairs={{0,1},{1,2},{2,3},{3,4},{4,5},{5,6},{6,7},{7,8},{8,9},{9,10},{10,1... | collective-permute-start | bytes 786440 | tf_op jit(solution)/shard_map/ppermute | solution.py:406
  98.0 25.4 %collective-permute-start.5 = (f32[256,256]{1,0:T(8,128)S(1)}, f32[256,256]{1,0:T(8,128)S(1)}, u32[]{:S(2)}, u32[]{:S(2)}) collective-permute-start(f32[256,256]{1,0:T(8,128)S(1)} %get-tuple-element.55), channel_id=1, source_target_pairs={{1,0},{2,1},{3,2},{4,3},{5,4},{6,5},{7,6},{8,7},{9,8},{10,9},{11,1... | collective-permute-start | bytes 786440 | tf_op jit(solution)/shard_map/ppermute | solution.py:407
  115.7 13.0 %all-to-all-start.6 = ((f32[8,1,128]{2,1,0:T(1,128)}), f32[8,1,128]{2,1,0:T(1,128)S(1)}, u32[]{:S(2)}, u32[]{:S(2)}) async-start(f32[8,1,128]{2,1,0:T(1,128)} %shard_map.124), calls=%async_computation.6 | async-start | bytes 8192 | tf_op jit(solution)/shard_map/all_to_all | solution.py:399

commit v3 on v2

v3 whole, which is shorter than its diff:
```python
import functools

import jax
import jax.numpy as jnp
from jax import lax
from jax.experimental import pallas as pl
from jax.experimental.pallas import tpu as pltpu
from jax.sharding import PartitionSpec as P


VMEM = pltpu.VMEM
SMEM = pltpu.SMEM
HBM = pltpu.HBM
DMA = pltpu.SemaphoreType.DMA
f32 = jnp.float32


def spec(space):
    return pl.BlockSpec(memory_space=space)


def near(array):
    return pltpu.with_memory_space_constraint(array, pltpu.MemorySpace.VMEM)


def distant(array):
    return pltpu.with_memory_space_constraint(array, pltpu.MemorySpace.HBM)


def call(kernel, out_shape, work, scalars=(), arrays=(), far=(), free=(), scratch=(), aliases=None, room=2, result=VMEM):
    flops, moved = work
    return pl.pallas_call(
        kernel,
        out_shape=out_shape,
        in_specs=[spec(SMEM)] * len(scalars) + [spec(VMEM)] * len(arrays) + [spec(HBM)] * len(far) + [spec(pl.ANY)] * len(free),
        out_specs=jax.tree.map(lambda _: spec(result), out_shape),
        scratch_shapes=list(scratch),
        input_output_aliases=aliases or {},
        cost_estimate=pl.CostEstimate(flops=flops, bytes_accessed=moved, transcendentals=0),
        compiler_params=pltpu.CompilerParams(vmem_limit_bytes=room << 20),
    )(*scalars, *[near(a) for a in arrays], *[distant(a) for a in far], *free)


def sheet_of(row, width):
    tall = jnp.transpose(jnp.broadcast_to(row, (128, 128)))
    return jnp.concatenate([tall] * (width // 128), axis=1)


def lanes_of(cells):
    column = sheet_of((cells & 255).astype(f32), 256).astype(jnp.int32)
    return lax.broadcasted_iota(jnp.int32, (128, 256), 1) == column


def gather_row(field_ref, cell_smem, cell_vec, rows_ref):
    for j in range(128):
        row = cell_smem[0, j] >> 8
        rows_ref[j : j + 1, :] = field_ref[row >> 8, pl.ds(row & 255, 1), :]
    picked = jnp.where(lanes_of(cell_vec), rows_ref[...], 0.0)
    return jnp.sum(jnp.transpose(picked[:, :128] + picked[:, 128:]), axis=0, keepdims=True)


def copies(pairs, sems):
    started = [pltpu.make_async_copy(a, b, sems.at[k]) for k, (a, b) in enumerate(pairs)]
    for copy in started:
        copy.start()
    return started


def first_kernel(
    rank,
    odd_brick,
    field_any,
    past_any,
    rec_any,
    emit_any,
    delays_any,
    out_ref,
    even_ref,
    odd_ref,
    rec_ref,
    emit_ref,
    own_ref,
    delay_ref,
    field_ref,
    rows_ref,
    past_ref,
    cell_smem,
    delays,
    sems,
):
    pairs = [(rec_any, cell_smem), (delays_any, delays), (field_any, field_ref), (past_any, past_ref)]
    started = copies(pairs + [(rec_any, rec_ref), (emit_any, emit_ref)], sems)
    own = lax.broadcasted_iota(jnp.int32, (8, 128), 0) == rank[0]
    own_ref[...] = jnp.where(own, 1.0, 0.0)
    for copy in started:
        copy.wait()
    delay_ref[...] = jnp.full((8, 128), delays[rank[0]], jnp.int32)
    sample = gather_row(field_ref, cell_smem, rec_ref[...], rows_ref)
    rows = [past_ref[...].astype(f32), sample.astype(jnp.bfloat16).astype(f32)]
    rows += [rec_ref[...].astype(f32), emit_ref[...].astype(f32), jnp.zeros((5, 128), f32)]
    message = jnp.concatenate(rows, axis=0)
    for s in range(8):
        out_ref[s] = message
    edges(odd_brick, field_ref, even_ref, odd_ref)


def edges(odd_brick, field_ref, even_ref, odd_ref):
    even_ref[...] = field_ref[3 - 3 * odd_brick[0]]
    odd_ref[...] = field_ref[3 * odd_brick[0]]


def first_message(rank, odd_brick, delays, rec_cell, emit_cell, past, field):
    plane = VMEM((256, 256), f32)
    row = VMEM((1, 128), jnp.int32)
    return call(
        first_kernel,
        (VMEM((8, 16, 128), f32), plane, plane, row, row, VMEM((8, 128), f32), VMEM((8, 128), jnp.int32)),
        (1 << 20, 1 << 19),
        scalars=[rank, odd_brick],
        far=[field, past, rec_cell, emit_cell, delays],
        scratch=[
            VMEM((4, 256, 256), f32),
            VMEM((128, 256), f32),
            VMEM((8, 128), jnp.bfloat16),
            SMEM((1, 128), jnp.int32),
            SMEM((8,), jnp.int32),
            DMA((6,)),
        ],
        room=3,
    )


def turn_kernel(green_any, right_ref, green_ref, sems):
    for copy in copies([(green_any, green_ref)], sems):
        copy.wait()
    for b in range(32):
        at = slice(b * 128, (b + 1) * 128)
        right_ref[:, at] = jnp.transpose(green_ref[at, :])


def turn(green):
    return call(
        turn_kernel,
        VMEM((128, 4096), jnp.bfloat16),
        (1 << 20, 1 << 20),
        far=[green],
        scratch=[VMEM((4096, 128), jnp.bfloat16), DMA((1,))],
    )


def older_kernel(first_ref, delay_ref, old_ref):
    for moment in (1, 2):
        old_ref[moment - 1] = old_samples(first_ref, 8 + moment - delay_ref[...])


def older(first, delay):
    out = VMEM((2, 8, 128), f32)
    return call(older_kernel, out, (1 << 20, 1 << 18), arrays=[first, delay])


def matches(first_ref):
    blocks = []
    for s in range(8):
        rec = first_ref[s, 9:10, :]
        emit = first_ref[s, 10:11, :]
        same = sheet_of(emit, 128) == jnp.broadcast_to(rec, (128, 128))
        blocks.append(jnp.where(same, 1.0, 0.0).astype(jnp.bfloat16))
    return jnp.concatenate(blocks, axis=0)


def multiply(chosen, right_ref, out_ref):
    product = jnp.dot(chosen.astype(jnp.bfloat16), right_ref[...], preferred_element_type=f32)
    for b in range(32):
        out_ref[b] = product[:, b * 128 : (b + 1) * 128]


def old_samples(first_ref, where):
    chosen = jnp.zeros((8, 128), f32)
    for k in range(9):
        series = jnp.concatenate([first_ref[s, k : k + 1, :] for s in range(8)], axis=0)
        chosen = jnp.where(where == k, series, chosen)
    return chosen


def start_kernel(first_ref, delay_ref, right_ref, out_ref):
    multiply(old_samples(first_ref, 8 - delay_ref[...]), right_ref, out_ref)


def emission_start(first, delay, right):
    out = VMEM((32, 8, 128), f32)
    return call(start_kernel, out, (8 << 20, 1 << 20), arrays=[first, delay, right])


def samples_kernel(moment, message_ref, first_ref, old_ref, delay_ref, own_ref, *refs):
    *newer_refs, right_ref, out_ref, mine_ref, sample_ref = refs
    total = message_ref[0, 0:8, :]
    for lag in range(1, 8):
        total = total + message_ref[lag, 0:8, :]
    values = jnp.concatenate([message_ref[s, 8:9, :] for s in range(8)], axis=0)
    wide = jnp.concatenate([total] * 8, axis=1)
    block = lax.broadcasted_iota(jnp.int32, (8, 1024), 1) >> 7
    wide = jnp.where(block == lax.broadcasted_iota(jnp.int32, (8, 1024), 0), wide, 0.0)
    high = wide.astype(jnp.bfloat16)
    rest = wide - high.astype(f32)
    middle = rest.astype(jnp.bfloat16)
    low = (rest - middle.astype(f32)).astype(jnp.bfloat16)
    parts = jnp.concatenate([high, middle, low], axis=0)
    added = jnp.dot(parts, matches(first_ref), preferred_element_type=f32)
    values = values + ((added[16:24] + added[8:16]) + added[0:8])
    sample = values.astype(jnp.bfloat16).astype(f32)
    delay = delay_ref[...]
    chosen = old_ref[moment - 1]
    for k, newer_ref in enumerate(newer_refs):
        chosen = jnp.where(delay == moment - 1 - k, newer_ref[...], chosen)
    chosen = jnp.where(delay == 0, sample, chosen)
    multiply(chosen, right_ref, out_ref)
    sample_ref[...] = sample
    mine_ref[...] = jnp.sum(jnp.where(own_ref[...] > 0.5, total, 0.0), axis=0, keepdims=True)


def samples_and_emission(moment, message, first, old, delay, own, newer, right):
    return call(
        functools.partial(samples_kernel, moment),
        (VMEM((32, 8, 128), f32), VMEM((1, 128), f32), VMEM((8, 128), f32)),
        (8 << 20, 1 << 20),
        arrays=[message, first, old, delay, own, *newer, right],
    )


def stencil_kernel(take, inside, odd_brick, cell_smem, cell_vec, *refs):
    field_in, prev_any, diag_any, cross_any, even_any, odd_any, *refs = refs
    *outs, field_ref, prev_ref, diag_ref, cross_ref, low_ref, high_ref, sems, edge_sems = refs
    out_ref, *outs = outs
    order = (1, 2, 0, 3)
    started = {}
    begun = {}
    if inside:
        field_ref = field_in
    else:
        begun = {x: copies([(field_in.at[x], field_ref.at[x])], sems.at[x, pl.ds(7, 1)]) for x in (0, 1, 2, 3)}
    for x in order:
        pairs = [(diag_any.at[k, x], diag_ref.at[k, x]) for k in range(3)]
        pairs += [(cross_any.at[k, x], cross_ref.at[k, x]) for k in range(3)]
        started[x] = copies([(prev_any.at[x], prev_ref.at[x])] + pairs, sems.at[x])

    @pl.when(odd_brick[0] == 0)
    def _():
        copies([(even_any, high_ref), (odd_any, low_ref)], edge_sems)

    @pl.when(odd_brick[0] == 1)
    def _():
        copies([(even_any, low_ref), (odd_any, high_ref)], edge_sems)

    lane = lax.broadcasted_iota(jnp.int32, (8, 128), 1)
    sub = lax.broadcasted_iota(jnp.int32, (8, 128), 0)
    zero = jnp.zeros((8, 128), f32)

    def after_z(pair):
        a, b = (pltpu.roll(v, 127, 1) for v in pair)
        return jnp.where(lane == 127, b, a), jnp.where(lane == 127, 0.0, b)

    def before_z(pair):
        a, b = (pltpu.roll(v, 1, 1) for v in pair)
        return jnp.where(lane == 0, 0.0, a), jnp.where(lane == 0, a, b)

    def at(ref, where, t):
        rows = slice(8 * t, 8 * t + 8)
        return ref[(*where, rows, slice(0, 128))], ref[(*where, rows, slice(128, 256))]

    def each(f, *pairs):
        return tuple(f(*vs) for vs in zip(*pairs))

    for x in order:
        need = {1: (0, 1, 2), 2: (3,)}.get(x, ())
        for k in need:
            for copy in begun.get(k, ()):
                copy.wait()
        if x == 0:
            for copy in [pltpu.make_async_copy(odd_any, low_ref, edge_sems.at[k]) for k in (0, 1)]:
                copy.wait()
        for copy in started[x]:
            copy.wait()

        def plane(dx):
            if x + dx < 0:
                return low_ref, ()
            if x + dx > 3:
                return high_ref, ()
            return field_ref, (x + dx,)

        def turned(pair):
            return tuple(pltpu.roll(v, 7, 0) for v in pair), tuple(pltpu.roll(v, 1, 0) for v in pair)

        edge = ((zero, zero), (zero, zero))
        tiles = {}
        turns = {-1: (edge, edge), 32: (edge, edge)}

        def fetch(t):
            mid = at(*plane(0), t)
            ahead = at(*plane(1), t)
            behind = at(*plane(-1), t)
            slope = each(lambda a, b: a - b, ahead, behind)
            tiles[t] = mid, each(lambda a, b: a + b, ahead, behind), slope
            turns[t] = turned(mid), turned(slope)

        def after_y(t, k):
            return each(lambda a, b: jnp.where(sub == 7, b, a), turns[t][k][0], turns[t + 1][k][0])

        def before_y(t, k):
            return each(lambda a, b: jnp.where(sub == 0, b, a), turns[t][k][1], turns[t - 1][k][1])

        fetch(0)
        for t in range(32):
            if t < 31:
                fetch(t + 1)
            mid, sum_x, slope_x = tiles.pop(t)
            up, down = after_y(t, 0), before_y(t, 0)
            twist = each(lambda a, b: a - b, after_y(t, 1), before_y(t, 1))
            slope_y = each(lambda a, b: a - b, up, down)
            sum_y = each(lambda a, b: a + b, up, down)
            sum_z = each(lambda a, b: a + b, after_z(mid), before_z(mid))
            twist_x = each(lambda a, b: a - b, after_z(slope_x), before_z(slope_x))
            twist_y = each(lambda a, b: a - b, after_z(slope_y), before_z(slope_y))
            diag = [at(diag_ref, (k, x), t) for k in range(3)]
            cross = [at(cross_ref, (k, x), t) for k in range(3)]
            prev = at(prev_ref, (x,), t)
            for h in range(2):
                d0, d1, d2 = (d[h] for d in diag)
                c0, c1, c2 = (c[h] for c in cross)
                twice = mid[h] + mid[h]
                second = d0 * (sum_x[h] - twice) + d1 * (sum_y[h] - twice) + d2 * (sum_z[h] - twice)
                mixed = c0 * twist[h] + c1 * twist_x[h] + c2 * twist_y[h]
                value = (twice - prev[h]) + (second + 0.5 * mixed)
                out_ref[x, 8 * t : 8 * t + 8, 128 * h : 128 * h + 128] = value
    if take:
        value_ref, rows_ref = outs
        value_ref[...] = gather_row(out_ref, cell_smem, cell_vec[...], rows_ref)


def stencil(take, inside, odd_brick, rec_cell, rec, field, prev, diag, cross, even, odd):
    out_shape = [VMEM((4, 256, 256), f32)]
    scratch = []
    if take:
        out_shape.append(VMEM((1, 128), f32))
        scratch.append(VMEM((128, 256), f32))
    plane = VMEM((256, 256), f32)
    coef = VMEM((3, 4, 256, 256), f32)
    whole = VMEM((4, 256, 256), f32)
    scratch += [VMEM((8, 128), f32) if inside else whole, whole, coef, coef, plane, plane, DMA((4, 8)), DMA((2,))]
    return call(
        functools.partial(stencil_kernel, take, inside),
        tuple(out_shape),
        (16 << 20, 10 << 20),
        scalars=[odd_brick, rec_cell],
        arrays=[rec] + [field] * inside,
        far=[field] * (not inside) + [prev, diag, cross],
        free=[even, odd],
        scratch=scratch,
        room=11,
    )


def add_at(cell_smem, cell_vec, value, target_ref, rows_ref):
    rows_ref[...] = jnp.where(lanes_of(cell_vec[...]), sheet_of(value, 256), 0.0)
    for j in range(128):
        row = cell_smem[0, j] >> 8
        at = (row >> 8, pl.ds(row & 255, 1), slice(None))
        target_ref[at] = target_ref[at] + rows_ref[j : j + 1, :]


def scatter_kernel(odd_brick, cell_smem, cell_vec, mine_ref, field_ref, *refs):
    *refs, rows_ref = refs
    old = refs[: len(refs) - 4] if len(refs) > 3 else []
    out_ref, even_ref, odd_ref = refs[len(old) : len(old) + 3]
    del field_ref
    add_at(cell_smem, cell_vec, mine_ref[...], out_ref, rows_ref)
    edges(odd_brick, out_ref, even_ref, odd_ref)
    if old:
        own_ref, first_ref, *sample_refs = old
        own = own_ref[...] > 0.5
        start = jnp.concatenate([first_ref[s, 8:9, :] for s in range(8)], axis=0)
        series = [start] + [s[...] for s in sample_refs]
        series = [jnp.sum(jnp.where(own, s, 0.0), axis=0, keepdims=True) for s in series]
        refs[-1][...] = jnp.concatenate(series, axis=0).astype(jnp.bfloat16)


def scatter(odd_brick, emit_cell, emit, mine, field, old=()):
    plane = VMEM((256, 256), f32)
    outs = (VMEM((4, 256, 256), f32), plane, plane)
    if old:
        outs += (VMEM((3, 128), jnp.bfloat16),)
    return call(
        scatter_kernel,
        outs,
        (1 << 20, 1 << 19),
        scalars=[odd_brick, emit_cell],
        arrays=[emit, mine, field, *old],
        scratch=[VMEM((128, 256), f32)],
        aliases={4: 0},
    )


def last_kernel(cell_smem, cell_vec, parts_ref, field_ref, out_any, rows_ref, sem):
    value = parts_ref[0]
    for lag in range(1, 8):
        value = value + parts_ref[lag]
    add_at(cell_smem, cell_vec, value, field_ref, rows_ref)
    copy = pltpu.make_async_copy(field_ref, out_any, sem)
    copy.start()
    copy.wait()


def last_scatter(emit_cell, emit, parts, field):
    return call(
        last_kernel,
        jax.ShapeDtypeStruct((4, 256, 256), f32),
        (1 << 20, 2 << 20),
        scalars=[emit_cell],
        arrays=[emit, parts, field],
        scratch=[VMEM((128, 256), f32), DMA],
        result=HBM,
    )


def spread_kernel(parts_ref, *refs):
    *value_refs, out_ref = refs
    sums = [parts_ref[b] for b in range(4)]
    for b in range(4, 32):
        sums[b % 4] = sums[b % 4] + parts_ref[b]
    total = (sums[0] + sums[1]) + (sums[2] + sums[3])
    if not value_refs:
        for s in range(8):
            out_ref[s] = total[s : s + 1, :]
        return
    value = jnp.broadcast_to(value_refs[0][...], (8, 128))
    for s in range(8):
        out_ref[s, 0:8, :] = total
        out_ref[s, 8:16, :] = value


def spread(parts, *value):
    out = VMEM((8, 16 if value else 1, 128), f32)
    return call(spread_kernel, out, (1 << 15, 1 << 17), arrays=[parts, *value])


def exchange(array, axis):
    return lax.all_to_all(array, axis, 0, 0, tiled=True)


def halos(even_plane, odd_plane):
    size = lax.axis_size("brick")
    even = lax.ppermute(even_plane, "brick", [(i, i ^ 1) for i in range(size)])
    odd = lax.ppermute(odd_plane, "brick", [(i, ((i + 1) ^ 1) - 1) for i in range(1, size - 1)])
    return even, odd


def steps(field_prev, field_now, diag, cross, green, delays, past, rec_cell, emit_cell):
    rank = lax.axis_index("shot").reshape(1)
    odd_brick = (lax.axis_index("brick") & 1).reshape(1)
    past = past[:, 0]

    current = field_now[0]
    message, *planes, rec, emit, own, delay = first_message(rank, odd_brick, delays, rec_cell, emit_cell, past, current)
    first = exchange(message, "shot")
    even, odd = halos(*planes)
    right = turn(green[0])
    following, value = stencil(True, False, odd_brick, rec_cell, rec, current, field_prev[0], diag, cross, even, odd)
    partial = emission_start(first, delay, right)
    parts = exchange(partial, "brick")
    old = older(first, delay)
    message = spread(parts, value)

    answer = exchange(message, "shot")
    partial, mine, sample1 = samples_and_emission(1, answer, first, old, delay, own, [], right)
    earlier = current
    current, *planes = scatter(odd_brick, emit_cell, emit, mine, following)
    even, odd = halos(*planes)
    parts = exchange(partial, "brick")
    following, value = stencil(True, True, odd_brick, rec_cell, rec, current, earlier, diag, cross, even, odd)
    message = spread(parts, value)

    answer = exchange(message, "shot")
    partial, mine, sample2 = samples_and_emission(2, answer, first, old, delay, own, [sample1], right)
    parts = exchange(partial, "brick")
    earlier = current
    current, *planes, recorded = scatter(odd_brick, emit_cell, emit, mine, following, (own, first, sample1, sample2))
    even, odd = halos(*planes)
    (following,) = stencil(False, True, odd_brick, rec_cell, rec, current, earlier, diag, cross, even, odd)
    message = spread(parts)
    parts = exchange(message, "shot")
    after = last_scatter(emit_cell, emit, parts, following)
    return current[None], after[None], recorded[:, None]


def solution(mesh):
    return jax.shard_map(
        steps,
        mesh=mesh,
        in_specs=(
            P("shot", "brick", None, None),
            P("shot", "brick", None, None),
            P(None, "brick", None, None),
            P(None, "brick", None, None),
            P("shot", None, "brick"),
            P(),
            P(None, "shot", "brick"),
            P("shot", "brick"),
            P("shot", "brick"),
        ),
        out_specs=(
            P("shot", "brick", None, None),
            P("shot", "brick", None, None),
            P(None, "shot", "brick"),
        ),
        check_vma=False,
    )
```

time: 132 us -> 123 us (0.932)
  starting transfers between devices: 53 us -> 45.6 us
  waiting for transfers between devices: 11.9 us -> 15.9 us
  local copies, waits for them, and re-layouts: 8.79 us -> 4.84 us
  Pallas kernels: 28.2 us -> 26.8 us
    all_to_all x5, waiting for transfers between devices: 10.5 us -> 15.8 us  [exchange(): return lax.all_to_all(array, axis, 0, 0, tiled=True)]
    ppermute x6, starting transfers between devices: 12.4 us -> 7.26 us  [the longest x3 5.26 us: halos(): even = lax.ppermute(even_plane, 'brick', [(i, i ^ 1) for i in range(size)])]
    unnamed x28 -> x16, local copies, waits for them, and re-layouts: 8.79 us -> 4.84 us
    all_to_all x5, starting transfers between devices: 40.6 us -> 38.4 us  [exchange(): return lax.all_to_all(array, axis, 0, 0, tiled=True)]
    ppermute x6, waiting for transfers between devices: 1.49 us -> 0.02 us  [the longest x3 0.01 us: halos(): even = lax.ppermute(even_plane, 'brick', [(i, i ^ 1) for i in range(size)])]
  transfers between devices with their start and end apart: 11 -> 11, of which waited for: 4 -> 4; matrix products, arithmetic and copies ran while one was open for 1% -> 1% of each run, Pallas kernels for 13% -> 14%
where the time goes in v3:
time: 123 us; the launch traced here: 122 us
  starting transfers between devices  45.6 us (37%)
  blocking collectives  28.1 us (23%)
  Pallas kernels  26.8 us (22%)
  waiting for transfers between devices  15.9 us (13%)
  local copies, waits for them, and re-layouts  4.84 us (4%)
    all_to_all x5, starting transfers between devices, exchange(): return lax.all_to_all(array, axis, 0, 0, tiled=True)  38.4 us
    all_to_all x2, blocking collectives, exchange(): return lax.all_to_all(array, axis, 0, 0, tiled=True)  28.1 us
    pallas_call x15, Pallas kernels, call(): pl.pallas_call(kernel, out_shape=out_shape, in_specs=[spec(SMEM)] * len(s...  26.8 us
    all_to_all x5, waiting for transfers between devices, exchange(): return lax.all_to_all(array, axis, 0, 0, tiled=True)  15.8 us
    ppermute x3, starting transfers between devices, halos(): even = lax.ppermute(even_plane, 'brick', [(i, i ^ 1) for i in range(size)])  5.26 us
    unnamed x16, local copies, waits for them, and re-layouts  4.84 us
  transfers between devices with their start and end apart: 11, of which 4 were waited for; matrix products, arithmetic and copies ran while one was open for 1% of the time, Pallas kernels for 14%

profile of v3, /device:TPU:1, one launch (start us, length us, event | category | flops | bytes accessed | tf_op | source)
XLA Modules:
  0.0 122.2 jit_solution(3738510529987878930)
XLA Ops:
  0.6 0.0 copy-start.6
  0.6 2.4 %shard_map.112 = (f32[8,16,128]{2,1,0:T(8,128)}, f32[256,256]{1,0:T(8,128)S(1)}, f32[256,256]{1,0:T(8,128)S(1)}, s32[1,128]{1,0:T(1,128)S(1)}, s32[1,128]{1,0:T(...) custom-call(s32[1]{0:T(128)} %bitcast.1.rank, s32[1]{0:T(128)} %bitcast.odd_brick, f32[4,256,256]{2,1,0:T(8,128)} %bitcast.11, ...), custom_call_target="tpu_custom_call" | custom-call | flops 1048576 | bytes 524288 | tf_op jit(solution)/shard_map/pallas_call | solution.py:32
  3.1 10.0 %all-to-all-start = ((f32[8,16,128]{2,1,0:T(8,128)}), f32[8,16,128]{2,1,0:T(8,128)S(1)}, u32[]{:S(2)}, u32[]{:S(2)}) async-start(f32[8,16,128]{2,1,0:T(8,128)} %get-tuple-element.28), calls=%async_computation | async-start | bytes 131072 | tf_op jit(solution)/shard_map/all_to_all | solution.py:447
  13.0 0.7 collective-permute-start
  13.8 0.7 collective-permute-start.1
  14.4 1.6 %shard_map.113.right_ref.refs_0_.refs_1_ = bf16[128,4096]{1,0:T(8,128)(2,1)S(1)} custom-call(bf16[4096,128]{1,0:T(8,128)(2,1)} %bitcast.15), custom_call_target="tpu_custom_call" | custom-call | flops 1048576 | bytes 1048576 | tf_op jit(solution)/shard_map/pallas_call | solution.py:32
  16.0 4.8 %all-to-all-done.first_ref.refs_1_ = f32[8,16,128]{2,1,0:T(8,128)S(1)} async-done(((f32[8,16,128]{2,1,0:T(8,128)}), f32[8,16,128]{2,1,0:T(8,128)S(1)}, u32[]{:S(2)}, u32[]{:S(2)}) %all-to-all-start) | async-done | bytes 65568 | tf_op jit(solution)/shard_map/all_to_all | solution.py:447
  20.8 0.9 shard_map.114
  21.8 7.5 %all-to-all-start.1 = ((f32[32,8,128]{2,1,0:T(8,128)}), f32[32,8,128]{2,1,0:T(8,128)S(1)}, u32[]{:S(2)}, u32[]{:S(2)}) async-start(f32[32,8,128]{2,1,0:T(8,128)} %shard_map.114), calls=%async_computation.1 | async-start | bytes 262144 | tf_op jit(solution)/shard_map/all_to_all | solution.py:447
  29.3 0.0 collective-permute-done.refs_4_
  29.3 0.0 collective-permute-done.1.refs_5_
  29.3 0.0 copy-done.6
  29.3 0.0 copy-start.5
  29.3 5.1 %shard_map.115 = (f32[4,256,256]{2,1,0:T(8,128)S(1)}, f32[1,128]{1,0:T(1,128)S(1)}) custom-call(s32[1]{0:T(128)} %bitcast.odd_brick, s32[1,128]{1,0:T(1,128)S(1)} %copy-done.6, s32[1,128]{1,0:T(1,128)S(1)} %get-tuple-element.30.cell_vec, f32[4,256,256]{2,1,0:T(8,128)} %bitcast.12, f32[4,256,256]{2,1,0:T(8,128)} %bitcast.14, f32[3,4,256,256]{3,2,1,0:T(8,128)} %refs_2_.5, ...), custom_call_target="tpu_custom_call" | custom-call | flops 16777216 | bytes 10485760 | tf_op jit(solution)/shard_map/pallas_call | solution.py:32
  34.4 2.4 %all-to-all-done.1.parts_ref = f32[32,8,128]{2,1,0:T(8,128)S(1)} async-done(((f32[32,8,128]{2,1,0:T(8,128)}), f32[32,8,128]{2,1,0:T(8,128)S(1)}, u32[]{:S(2)}, u32[]{:S(2)}) %all-to-all-start.1) | async-done | bytes 131104 | tf_op jit(solution)/shard_map/all_to_all | solution.py:447
  36.8 0.6 shard_map.116
  37.5 7.0 %all-to-all-start.2 = ((f32[8,16,128]{2,1,0:T(8,128)}), f32[8,16,128]{2,1,0:T(8,128)S(1)}, u32[]{:S(2)}, u32[]{:S(2)}) async-start(f32[8,16,128]{2,1,0:T(8,128)} %shard_map.116), calls=%async_computation.2 | async-start | bytes 131072 | tf_op jit(solution)/shard_map/all_to_all | solution.py:447
  44.5 7.5 %all-to-all-done.2.message_ref = f32[8,16,128]{2,1,0:T(8,128)S(1)} async-done(((f32[8,16,128]{2,1,0:T(8,128)}), f32[8,16,128]{2,1,0:T(8,128)S(1)}, u32[]{:S(2)}, u32[]{:S(2)}) %all-to-all-start.2) | async-done | bytes 65568 | tf_op jit(solution)/shard_map/all_to_all | solution.py:447
  51.9 1.2 shard_map.118
  53.1 0.0 copy-done.5
  53.1 1.3 %shard_map.119 = (f32[4,256,256]{2,1,0:T(8,128)S(1)}, f32[256,256]{1,0:T(8,128)S(1)}, f32[256,256]{1,0:T(8,128)S(1)}) custom-call(s32[1]{0:T(128)} %bitcast.odd_brick, s32[1,128]{1,0:T(1,128)S(1)} %copy-done.5, s32[1,128]{1,0:T(1,128)S(1)} %get-tuple-element.27.cell_vec, f32[1,128]{1,0:T(1,128)S(1)} %get-tuple-element.36.mine_ref, ...), custom_call_target="tpu_custom_call", output_to_operand_aliasing={{0}: (4, {})} | custom-call | flops 1048576 | bytes 524288 | tf_op jit(solution)/shard_map/pallas_call | solution.py:32
  54.4 0.0 copy-start
  54.4 0.7 collective-permute-start.2
  55.1 0.7 collective-permute-start.3
  55.8 8.0 %all-to-all-start.3 = ((f32[32,8,128]{2,1,0:T(8,128)}), f32[32,8,128]{2,1,0:T(8,128)S(1)}, u32[]{:S(2)}, u32[]{:S(2)}) async-start(f32[32,8,128]{2,1,0:T(8,128)} %get-tuple-element.35), calls=%async_computation.3 | async-start | bytes 262144 | tf_op jit(solution)/shard_map/all_to_all | solution.py:447
  63.8 0.0 collective-permute-done.2.refs_4_
  63.8 0.0 copy-start.1
  63.8 0.7 copy-done.1
  64.5 0.0 collective-permute-done.3.refs_5_
  64.5 0.0 copy-start.3
  64.5 0.7 copy-done.3
  65.2 0.0 copy-start.2
  65.2 0.9 copy-done.2
  66.2 0.0 copy-start.4
  66.2 0.9 copy-done.4
  67.1 4.8 %shard_map.120 = (f32[4,256,256]{2,1,0:T(8,128)S(1)}, f32[1,128]{1,0:T(1,128)S(1)}) custom-call(s32[1]{0:T(128)} %bitcast.odd_brick, s32[1,128]{1,0:T(1,128)S(1)} %copy-done.6, s32[1,128]{1,0:T(1,128)S(1)} %get-tuple-element.30.cell_vec, f32[4,256,256]{2,1,0:T(8,128)S(1)} %get-tuple-element.38.refs_0_.refs_1_, f32[4,256,256]{2,1,0:T(8,128)} %bitcast.13, ...), custom_call_target="tpu_custom_call" | custom-call | flops 16777216 | bytes 10485760 | tf_op jit(solution)/shard_map/pallas_call | solution.py:32
  71.9 0.0 copy-done
  71.9 0.0 all-to-all-done.3.parts_ref
  72.0 11.7 %all_to_all.35.message_ref = f32[8,16,128]{2,1,0:T(8,128)S(1)} all-to-all(f32[8,16,128]{2,1,0:T(8,128)S(1)} %shard_map.121), channel_id=1, replica_groups=mesh['shot'=8,'brick'=32] {'shot'}, dimensions={0} | all-to-all | bytes 131072 | tf_op jit(solution)/shard_map/all_to_all | solution.py:447
  83.7 0.5 shard_map.122
  84.2 1.2 %shard_map.123 = (f32[4,256,256]{2,1,0:T(8,128)S(1)}, f32[256,256]{1,0:T(8,128)S(1)}, f32[256,256]{1,0:T(8,128)S(1)}, bf16[3,128]{1,0:T(4,128)(2,1)S(1)}) custom-call(s32[1]{0:T(128)} %bitcast.odd_brick, s32[1,128]{1,0:T(1,128)S(1)} %copy-done.5, s32[1,128]{1,0:T(1,128)S(1)} %get-tuple-element.27.cell_vec, ...), custom_call_target="tpu_custom_call", output_to_operand_aliasing={{0}: (4, {})} | custom-call | flops 1048576 | bytes 524288 | tf_op jit(solution)/shard_map/pallas_call | solution.py:32
  85.5 3.8 %collective-permute-start.4 = (f32[256,256]{1,0:T(8,128)S(1)}, f32[256,256]{1,0:T(8,128)S(1)}, u32[]{:S(2)}, u32[]{:S(2)}) collective-permute-start(f32[256,256]{1,0:T(8,128)S(1)} %get-tuple-element.48), channel_id=1, source_target_pairs={{0,1},{1,0},{2,3},{3,2},{4,5},{5,4},{6,7},{7,6},{8,9},{9,8},{10,11... | collective-permute-start | bytes 786440 | tf_op jit(solution)/shard_map/ppermute | solution.py:452
  89.3 0.7 collective-permute-start.5
  90.0 16.3 %all_to_all.36.parts_ref = f32[32,8,128]{2,1,0:T(8,128)S(1)} all-to-all(f32[32,8,128]{2,1,0:T(8,128)S(1)} %get-tuple-element.47), channel_id=1, replica_groups=mesh['shot'=8,'brick'=32] {'brick'}, dimensions={0} | all-to-all | bytes 262144 | tf_op jit(solution)/shard_map/all_to_all | solution.py:447
  106.3 0.6 shard_map.124
  106.9 5.9 %all-to-all-start.6 = ((f32[8,1,128]{2,1,0:T(1,128)}), f32[8,1,128]{2,1,0:T(1,128)S(1)}, u32[]{:S(2)}, u32[]{:S(2)}) async-start(f32[8,1,128]{2,1,0:T(1,128)} %shard_map.124), calls=%async_computation.6 | async-start | bytes 8192 | tf_op jit(solution)/shard_map/all_to_all | solution.py:447
  112.8 0.6 copy.17
  113.4 1.0 copy.16
  114.4 0.0 collective-permute-done.4.refs_4_
  114.4 0.0 collective-permute-done.5.refs_5_
  114.4 4.4 %shard_map.125.field_ref = f32[4,256,256]{2,1,0:T(8,128)S(1)} custom-call(s32[1]{0:T(128)} %bitcast.odd_brick, s32[1,128]{1,0:T(1,128)S(1)} %copy-done.6, s32[1,128]{1,0:T(1,128)S(1)} %get-tuple-element.30.cell_vec, f32[4,256,256]{2,1,0:T(8,128)S(1)} %get-tuple-element.46.refs_0_, f32[4,256,256]{2,1,0:T(8,128)} %copy-done, f32[3,4,256,256]{3,2,1,0:T(8,128)} %refs_2_.5, ...), custom_call_target="tpu_custom_call" | custom-call | flops 16777216 | bytes 10485760 | tf_op jit(solution)/shard_map/pallas_call | solution.py:32
  118.8 1.1 all-to-all-done.6.parts_ref
  119.9 2.2 %shard_map.126 = f32[4,256,256]{2,1,0:T(8,128)} custom-call(s32[1,128]{1,0:T(1,128)S(1)} %copy-done.5, s32[1,128]{1,0:T(1,128)S(1)} %get-tuple-element.27.cell_vec, f32[8,1,128]{2,1,0:T(1,128)S(1)} %all-to-all-done.6.parts_ref, f32[4,256,256]{2,1,0:T(8,128)S(1)} %shard_map.125.field_ref), custom_call_target="tpu_custom_call" | custom-call | flops 1048576 | bytes 2097152 | tf_op jit(solution)/shard_map/pallas_call | solution.py:32
  (2 shorter events, 0.0 us)
Async XLA Ops:
  0.6 28.7 %copy-start.6 = (s32[1,128]{1,0:T(1,128)S(1)}, s32[1,128]{1,0:T(1,128)}, u32[]{:S(2)}) copy-start(s32[1,128]{1,0:T(1,128)} %cell_smem.10) | copy-start | bytes 1540
  3.1 17.8 %all-to-all-start = ((f32[8,16,128]{2,1,0:T(8,128)}), f32[8,16,128]{2,1,0:T(8,128)S(1)}, u32[]{:S(2)}, u32[]{:S(2)}) async-start(f32[8,16,128]{2,1,0:T(8,128)} %get-tuple-element.28), calls=%async_computation | async-start | bytes 131072 | tf_op jit(solution)/shard_map/all_to_all | solution.py:447
  13.0 16.2 %collective-permute-start = (f32[256,256]{1,0:T(8,128)S(1)}, f32[256,256]{1,0:T(8,128)S(1)}, u32[]{:S(2)}, u32[]{:S(2)}) collective-permute-start(f32[256,256]{1,0:T(8,128)S(1)} %get-tuple-element.31), channel_id=1, source_target_pairs={{0,1},{1,0},{2,3},{3,2},{4,5},{5,4},{6,7},{7,6},{8,9},{9,8},{10,11... | collective-permute-start | bytes 786440 | tf_op jit(solution)/shard_map/ppermute | solution.py:452
  13.8 15.5 %collective-permute-start.1 = (f32[256,256]{1,0:T(8,128)S(1)}, f32[256,256]{1,0:T(8,128)S(1)}, u32[]{:S(2)}, u32[]{:S(2)}) collective-permute-start(f32[256,256]{1,0:T(8,128)S(1)} %get-tuple-element.32), channel_id=1, source_target_pairs={{1,2},{2,1},{3,4},{4,3},{5,6},{6,5},{7,8},{8,7},{9,10},{10,9},{11,... | collective-permute-start | bytes 786440 | tf_op jit(solution)/shard_map/ppermute | solution.py:453
  21.8 15.1 %all-to-all-start.1 = ((f32[32,8,128]{2,1,0:T(8,128)}), f32[32,8,128]{2,1,0:T(8,128)S(1)}, u32[]{:S(2)}, u32[]{:S(2)}) async-start(f32[32,8,128]{2,1,0:T(8,128)} %shard_map.114), calls=%async_computation.1 | async-start | bytes 262144 | tf_op jit(solution)/shard_map/all_to_all | solution.py:447
  29.3 23.8 %copy-start.5 = (s32[1,128]{1,0:T(1,128)S(1)}, s32[1,128]{1,0:T(1,128)}, u32[]{:S(2)}) copy-start(s32[1,128]{1,0:T(1,128)} %cell_smem.11) | copy-start | bytes 1540
  37.5 14.4 %all-to-all-start.2 = ((f32[8,16,128]{2,1,0:T(8,128)}), f32[8,16,128]{2,1,0:T(8,128)S(1)}, u32[]{:S(2)}, u32[]{:S(2)}) async-start(f32[8,16,128]{2,1,0:T(8,128)} %shard_map.116), calls=%async_computation.2 | async-start | bytes 131072 | tf_op jit(solution)/shard_map/all_to_all | solution.py:447
  54.4 17.5 %copy-start = (f32[4,256,256]{2,1,0:T(8,128)}, f32[4,256,256]{2,1,0:T(8,128)S(1)}, u32[]{:S(2)}) copy-start(f32[4,256,256]{2,1,0:T(8,128)S(1)} %get-tuple-element.38.refs_0_.refs_1_) | copy-start | bytes 3145732
  54.4 9.4 %collective-permute-start.2 = (f32[256,256]{1,0:T(8,128)S(1)}, f32[256,256]{1,0:T(8,128)S(1)}, u32[]{:S(2)}, u32[]{:S(2)}) collective-permute-start(f32[256,256]{1,0:T(8,128)S(1)} %get-tuple-element.39), channel_id=1, source_target_pairs={{0,1},{1,0},{2,3},{3,2},{4,5},{5,4},{6,7},{7,6},{8,9},{9,8},{10,11... | collective-permute-start | bytes 786440 | tf_op jit(solution)/shard_map/ppermute | solution.py:452
  55.1 9.4 %collective-permute-start.3 = (f32[256,256]{1,0:T(8,128)S(1)}, f32[256,256]{1,0:T(8,128)S(1)}, u32[]{:S(2)}, u32[]{:S(2)}) collective-permute-start(f32[256,256]{1,0:T(8,128)S(1)} %get-tuple-element.40), channel_id=1, source_target_pairs={{1,2},{2,1},{3,4},{4,3},{5,6},{6,5},{7,8},{8,7},{9,10},{10,9},{11,... | collective-permute-start | bytes 786440 | tf_op jit(solution)/shard_map/ppermute | solution.py:453
  55.8 16.1 %all-to-all-start.3 = ((f32[32,8,128]{2,1,0:T(8,128)}), f32[32,8,128]{2,1,0:T(8,128)S(1)}, u32[]{:S(2)}, u32[]{:S(2)}) async-start(f32[32,8,128]{2,1,0:T(8,128)} %get-tuple-element.35), calls=%async_computation.3 | async-start | bytes 262144 | tf_op jit(solution)/shard_map/all_to_all | solution.py:447
  63.8 0.7 copy-start.1
  64.5 0.7 copy-start.3
  65.2 0.9 copy-start.2
  66.2 0.9 copy-start.4
  85.5 28.9 %collective-permute-start.4 = (f32[256,256]{1,0:T(8,128)S(1)}, f32[256,256]{1,0:T(8,128)S(1)}, u32[]{:S(2)}, u32[]{:S(2)}) collective-permute-start(f32[256,256]{1,0:T(8,128)S(1)} %get-tuple-element.48), channel_id=1, source_target_pairs={{0,1},{1,0},{2,3},{3,2},{4,5},{5,4},{6,7},{7,6},{8,9},{9,8},{10,11... | collective-permute-start | bytes 786440 | tf_op jit(solution)/shard_map/ppermute | solution.py:452
  89.3 25.1 %collective-permute-start.5 = (f32[256,256]{1,0:T(8,128)S(1)}, f32[256,256]{1,0:T(8,128)S(1)}, u32[]{:S(2)}, u32[]{:S(2)}) collective-permute-start(f32[256,256]{1,0:T(8,128)S(1)} %get-tuple-element.49), channel_id=1, source_target_pairs={{1,2},{2,1},{3,4},{4,3},{5,6},{6,5},{7,8},{8,7},{9,10},{10,9},{11,... | collective-permute-start | bytes 786440 | tf_op jit(solution)/shard_map/ppermute | solution.py:453
  106.9 13.0 %all-to-all-start.6 = ((f32[8,1,128]{2,1,0:T(1,128)}), f32[8,1,128]{2,1,0:T(1,128)S(1)}, u32[]{:S(2)}, u32[]{:S(2)}) async-start(f32[8,1,128]{2,1,0:T(1,128)} %shard_map.124), calls=%async_computation.6 | async-start | bytes 8192 | tf_op jit(solution)/shard_map/all_to_all | solution.py:447

commit v4 on v3

--- a/solution.py
+++ b/solution.py
@@ -11,6 +11,7 @@
 VMEM = pltpu.VMEM
 SMEM = pltpu.SMEM
 HBM = pltpu.HBM
+FAR = True
 DMA = pltpu.SemaphoreType.DMA
 f32 = jnp.float32
 
@@ -54,7 +55,7 @@
 def gather_row(field_ref, cell_smem, cell_vec, rows_ref):
     for j in range(128):
         row = cell_smem[0, j] >> 8
-        rows_ref[j : j + 1, :] = field_ref[row >> 8, pl.ds(row & 255, 1), :]
+        rows_ref[j : j + 1, :] = field_ref[pl.ds(row, 1), :]
     picked = jnp.where(lanes_of(cell_vec), rows_ref[...], 0.0)
     return jnp.sum(jnp.transpose(picked[:, :128] + picked[:, 128:]), axis=0, keepdims=True)
 
@@ -105,8 +106,8 @@
 
 
 def edges(odd_brick, field_ref, even_ref, odd_ref):
-    even_ref[...] = field_ref[3 - 3 * odd_brick[0]]
-    odd_ref[...] = field_ref[3 * odd_brick[0]]
+    even_ref[...] = field_ref[pl.ds(pl.multiple_of(768 - 768 * odd_brick[0], 256), 256), :]
+    odd_ref[...] = field_ref[pl.ds(pl.multiple_of(768 * odd_brick[0], 256), 256), :]
 
 
 def first_message(rank, odd_brick, delays, rec_cell, emit_cell, past, field):
@@ -119,7 +120,7 @@
         scalars=[rank, odd_brick],
         far=[field, past, rec_cell, emit_cell, delays],
         scratch=[
-            VMEM((4, 256, 256), f32),
+            VMEM((1024, 256), f32),
             VMEM((128, 256), f32),
             VMEM((8, 128), jnp.bfloat16),
             SMEM((1, 128), jnp.int32),
@@ -130,22 +131,14 @@
     )
 
 
-def turn_kernel(green_any, right_ref, green_ref, sems):
-    for copy in copies([(green_any, green_ref)], sems):
-        copy.wait()
+def turn_kernel(green_ref, right_ref):
     for b in range(32):
         at = slice(b * 128, (b + 1) * 128)
         right_ref[:, at] = jnp.transpose(green_ref[at, :])
 
 
 def turn(green):
-    return call(
-        turn_kernel,
-        VMEM((128, 4096), jnp.bfloat16),
-        (1 << 20, 1 << 20),
-        far=[green],
-        scratch=[VMEM((4096, 128), jnp.bfloat16), DMA((1,))],
-    )
+    return call(turn_kernel, VMEM((128, 4096), jnp.bfloat16), (1 << 20, 1 << 20), arrays=[green])
 
 
 def older_kernel(first_ref, delay_ref, old_ref):
@@ -229,19 +222,24 @@
 
 def stencil_kernel(take, inside, odd_brick, cell_smem, cell_vec, *refs):
     field_in, prev_any, diag_any, cross_any, even_any, odd_any, *refs = refs
-    *outs, field_ref, prev_ref, diag_ref, cross_ref, low_ref, high_ref, sems, edge_sems = refs
+    *outs, field_ref, prev_ref, diag_ref, cross_ref, low_ref, high_ref, skew_ref, sum_ref, sems, edge_sems = refs
     out_ref, *outs = outs
     order = (1, 2, 0, 3)
-    started = {}
+
+    def part(x):
+        return pl.ds(256 * x, 256)
+
     begun = {}
     if inside:
         field_ref = field_in
     else:
-        begun = {x: copies([(field_in.at[x], field_ref.at[x])], sems.at[x, pl.ds(7, 1)]) for x in (0, 1, 2, 3)}
+        for x in (0, 1, 2, 3):
+            begun[x] = copies([(field_in.at[part(x)], field_ref.at[part(x)])], sems.at[x, pl.ds(7, 1)])
+    started = {}
     for x in order:
         pairs = [(diag_any.at[k, x], diag_ref.at[k, x]) for k in range(3)]
         pairs += [(cross_any.at[k, x], cross_ref.at[k, x]) for k in range(3)]
-        started[x] = copies([(prev_any.at[x], prev_ref.at[x])] + pairs, sems.at[x])
+        started[x] = copies([(prev_any.at[part(x)], prev_ref.at[part(x)])] + pairs, sems.at[x])
 
     @pl.when(odd_brick[0] == 0)
     def _():
@@ -254,109 +252,126 @@
     lane = lax.broadcasted_iota(jnp.int32, (8, 128), 1)
     sub = lax.broadcasted_iota(jnp.int32, (8, 128), 0)
     zero = jnp.zeros((8, 128), f32)
-
-    def after_z(pair):
-        a, b = (pltpu.roll(v, 127, 1) for v in pair)
-        return jnp.where(lane == 127, b, a), jnp.where(lane == 127, 0.0, b)
-
-    def before_z(pair):
-        a, b = (pltpu.roll(v, 1, 1) for v in pair)
-        return jnp.where(lane == 0, 0.0, a), jnp.where(lane == 0, a, b)
-
-    def at(ref, where, t):
-        rows = slice(8 * t, 8 * t + 8)
+    first_lane, last_lane = lane == 0, lane == 127
+    first_sub, last_sub = sub == 0, sub == 7
+
+    def at(ref, where, row):
+        rows = slice(row, row + 8)
         return ref[(*where, rows, slice(0, 128))], ref[(*where, rows, slice(128, 256))]
+
+    def put(ref, row, pair):
+        for h in range(2):
+            ref[row : row + 8, 128 * h : 128 * h + 128] = pair[h]
 
     def each(f, *pairs):
         return tuple(f(*vs) for vs in zip(*pairs))
 
+    def plus(a, b):
+        return each(lambda v, w: v + w, a, b)
+
+    def minus(a, b):
+        return each(lambda v, w: v - w, a, b)
+
+    def source(x):
+        if x < 0:
+            return low_ref, 0
+        if x > 3:
+            return high_ref, 0
+        return field_ref, 256 * x
+
+    def along_z(x):
+        ref, base = source(x)
+        for t in range(32):
+            a, b = at(ref, (), base + 8 * t)
+            up_a, up_b = pltpu.roll(a, 127, 1), pltpu.roll(b, 127, 1)
+            down_a, down_b = pltpu.roll(a, 1, 1), pltpu.roll(b, 1, 1)
+            ahead = (jnp.where(last_lane, up_b, up_a), jnp.where(last_lane, 0.0, up_b))
+            behind = (jnp.where(first_lane, 0.0, down_a), jnp.where(first_lane, down_a, down_b))
+            put(skew_ref, 256 * (x + 1) + 8 * t, minus(ahead, behind))
+            if 0 <= x < 4:
+                put(sum_ref, 256 * x + 8 * t, plus(ahead, behind))
+
+    ready = {1: (0, 1, 2), 2: (3,), 0: (-1,), 3: (4,)}
     for x in order:
-        need = {1: (0, 1, 2), 2: (3,)}.get(x, ())
-        for k in need:
+        if x == 0:
+            for k in (0, 1):
+                pltpu.make_async_copy(odd_any, low_ref, edge_sems.at[k]).wait()
+        for k in ready[x]:
             for copy in begun.get(k, ()):
                 copy.wait()
-        if x == 0:
-            for copy in [pltpu.make_async_copy(odd_any, low_ref, edge_sems.at[k]) for k in (0, 1)]:
-                copy.wait()
+            along_z(k)
         for copy in started[x]:
             copy.wait()
 
-        def plane(dx):
-            if x + dx < 0:
-                return low_ref, ()
-            if x + dx > 3:
-                return high_ref, ()
-            return field_ref, (x + dx,)
-
         def turned(pair):
             return tuple(pltpu.roll(v, 7, 0) for v in pair), tuple(pltpu.roll(v, 1, 0) for v in pair)
 
         edge = ((zero, zero), (zero, zero))
         tiles = {}
-        turns = {-1: (edge, edge), 32: (edge, edge)}
+        turns = {-1: (edge, edge, edge), 32: (edge, edge, edge)}
 
         def fetch(t):
-            mid = at(*plane(0), t)
-            ahead = at(*plane(1), t)
-            behind = at(*plane(-1), t)
-            slope = each(lambda a, b: a - b, ahead, behind)
-            tiles[t] = mid, each(lambda a, b: a + b, ahead, behind), slope
-            turns[t] = turned(mid), turned(slope)
+            mid, ahead, behind = (at(ref, (), base + 8 * t) for ref, base in map(source, (x, x + 1, x - 1)))
+            slope = minus(ahead, behind)
+            skew = at(skew_ref, (), 256 * (x + 1) + 8 * t)
+            tiles[t] = mid, plus(ahead, behind)
+            turns[t] = turned(mid), turned(slope), turned(skew)
 
         def after_y(t, k):
-            return each(lambda a, b: jnp.where(sub == 7, b, a), turns[t][k][0], turns[t + 1][k][0])
+            return each(lambda a, b: jnp.where(last_sub, b, a), turns[t][k][0], turns[t + 1][k][0])
 
         def before_y(t, k):
-            return each(lambda a, b: jnp.where(sub == 0, b, a), turns[t][k][1], turns[t - 1][k][1])
+            return each(lambda a, b: jnp.where(first_sub, b, a), turns[t][k][1], turns[t - 1][k][1])
 
         fetch(0)
         for t in range(32):
             if t < 31:
                 fetch(t + 1)
-            mid, sum_x, slope_x = tiles.pop(t)
-            up, down = after_y(t, 0), before_y(t, 0)
-            twist = each(lambda a, b: a - b, after_y(t, 1), before_y(t, 1))
-            slope_y = each(lambda a, b: a - b, up, down)
-            sum_y = each(lambda a, b: a + b, up, down)
-            sum_z = each(lambda a, b: a + b, after_z(mid), before_z(mid))
-            twist_x = each(lambda a, b: a - b, after_z(slope_x), before_z(slope_x))
-            twist_y = each(lambda a, b: a - b, after_z(slope_y), before_z(slope_y))
-            diag = [at(diag_ref, (k, x), t) for k in range(3)]
-            cross = [at(cross_ref, (k, x), t) for k in range(3)]
-            prev = at(prev_ref, (x,), t)
+            row = 8 * t
+            mid, sum_x = tiles.pop(t)
+            sum_y = plus(after_y(t, 0), before_y(t, 0))
+            sum_z = at(sum_ref, (), 256 * x + row)
+            skew_xy = minus(after_y(t, 1), before_y(t, 1))
+            skew_xz = minus(at(skew_ref, (), 256 * (x + 2) + row), at(skew_ref, (), 256 * x + row))
+            skew_yz = minus(after_y(t, 2), before_y(t, 2))
+            diag = [at(diag_ref, (k, x), row) for k in range(3)]
+            cross = [at(cross_ref, (k, x), row) for k in range(3)]
+            prev = at(prev_ref, (), 256 * x + row)
+            values = []
             for h in range(2):
                 d0, d1, d2 = (d[h] for d in diag)
                 c0, c1, c2 = (c[h] for c in cross)
                 twice = mid[h] + mid[h]
                 second = d0 * (sum_x[h] - twice) + d1 * (sum_y[h] - twice) + d2 * (sum_z[h] - twice)
-                mixed = c0 * twist[h] + c1 * twist_x[h] + c2 * twist_y[h]
-                value = (twice - prev[h]) + (second + 0.5 * mixed)
-                out_ref[x, 8 * t : 8 * t + 8, 128 * h : 128 * h + 128] = value
+                mixed = c0 * skew_xy[h] + c1 * skew_xz[h] + c2 * skew_yz[h]
+                values.append((twice - prev[h]) + (second + 0.5 * mixed))
+            put(out_ref, 256 * x + row, values)
     if take:
         value_ref, rows_ref = outs
         value_ref[...] = gather_row(out_ref, cell_smem, cell_vec[...], rows_ref)
 
 
 def stencil(take, inside, odd_brick, rec_cell, rec, field, prev, diag, cross, even, odd):
-    out_shape = [VMEM((4, 256, 256), f32)]
+    out_shape = [VMEM((1024, 256), f32)]
     scratch = []
     if take:
         out_shape.append(VMEM((1, 128), f32))
         scratch.append(VMEM((128, 256), f32))
     plane = VMEM((256, 256), f32)
     coef = VMEM((3, 4, 256, 256), f32)
-    whole = VMEM((4, 256, 256), f32)
-    scratch += [VMEM((8, 128), f32) if inside else whole, whole, coef, coef, plane, plane, DMA((4, 8)), DMA((2,))]
+    whole = VMEM((1024, 256), f32)
+    scratch += [VMEM((8, 128), f32) if inside else whole, whole, coef, coef, plane, plane]
+    scratch += [VMEM((1536, 256), f32), whole, DMA((4, 8)), DMA((2,))]
     return call(
         functools.partial(stencil_kernel, take, inside),
         tuple(out_shape),
         (16 << 20, 10 << 20),
         scalars=[odd_brick, rec_cell],
         arrays=[rec] + [field] * inside,
-        far=[field] * (not inside) + [prev, diag, cross],
-        free=[even, odd],
+        far=[field] * (not inside) + [prev, diag, cross] + ([even, odd] if FAR and take and inside else []),
+        free=[] if FAR and take and inside else [even, odd],
         scratch=scratch,
-        room=11,
+        room=14,
     )
 
 
@@ -364,8 +379,7 @@
     rows_ref[...] = jnp.where(lanes_of(cell_vec[...]), sheet_of(value, 256), 0.0)
     for j in range(128):
         row = cell_smem[0, j] >> 8
-        at = (row >> 8, pl.ds(row & 255, 1), slice(None))
-        target_ref[at] = target_ref[at] + rows_ref[j : j + 1, :]
+        target_ref[pl.ds(row, 1), :] = target_ref[pl.ds(row, 1), :] + rows_ref[j : j + 1, :]
 
 
 def scatter_kernel(odd_brick, cell_smem, cell_vec, mine_ref, field_ref, *refs):
@@ -386,7 +400,7 @@
 
 def scatter(odd_brick, emit_cell, emit, mine, field, old=()):
     plane = VMEM((256, 256), f32)
-    outs = (VMEM((4, 256, 256), f32), plane, plane)
+    outs = (VMEM((1024, 256), f32), plane, plane)
     if old:
         outs += (VMEM((3, 128), jnp.bfloat16),)
     return call(
@@ -413,7 +427,7 @@
 def last_scatter(emit_cell, emit, parts, field):
     return call(
         last_kernel,
-        jax.ShapeDtypeStruct((4, 256, 256), f32),
+        jax.ShapeDtypeStruct((1024, 256), f32),
         (1 << 20, 2 << 20),
         scalars=[emit_cell],
         arrays=[emit, parts, field],
@@ -459,12 +473,13 @@
     odd_brick = (lax.axis_index("brick") & 1).reshape(1)
     past = past[:, 0]
 
-    current = field_now[0]
+    current = field_now.reshape(1024, 256)
+    before = field_prev.reshape(1024, 256)
     message, *planes, rec, emit, own, delay = first_message(rank, odd_brick, delays, rec_cell, emit_cell, past, current)
     first = exchange(message, "shot")
     even, odd = halos(*planes)
     right = turn(green[0])
-    following, value = stencil(True, False, odd_brick, rec_cell, rec, current, field_prev[0], diag, cross, even, odd)
+    following, value = stencil(True, False, odd_brick, rec_cell, rec, current, before, diag, cross, even, odd)
     partial = emission_start(first, delay, right)
     parts = exchange(partial, "brick")
     old = older(first, delay)
@@ -489,7 +504,8 @@
     message = spread(parts)
     parts = exchange(message, "shot")
     after = last_scatter(emit_cell, emit, parts, following)
-    return current[None], after[None], recorded[:, None]
+    shape = field_now.shape
+    return current.reshape(shape), after.reshape(shape), recorded[:, None]
 
 
 def solution(mesh):

time: 123 us -> 121 us (0.984)
  Pallas kernels: 26.8 us -> 24.9 us
  starting transfers between devices: 45.6 us -> 43.7 us
    pallas_call x15, Pallas kernels: 26.8 us -> 24.9 us  [call(): pl.pallas_call(kernel, out_shape=out_shape, in_specs=[spec(SMEM)] * len(s...]
    ppermute x3, starting transfers between devices: 5.26 us -> 3.34 us  [halos(): even = lax.ppermute(even_plane, 'brick', [(i, i ^ 1) for i in range(size)])]
    all_to_all x5, waiting for transfers between devices: 15.8 us -> 17.1 us  [exchange(): return lax.all_to_all(array, axis, 0, 0, tiled=True)]
    unnamed x16 -> x14, local copies, waits for them, and re-layouts: 4.84 us -> 4.17 us
  transfers between devices with their start and end apart: 11 -> 11, of which waited for: 4 -> 5; matrix products, arithmetic and copies ran while one was open for 1% -> 1% of each run, Pallas kernels for 14% -> 13%
where the time goes in v4:
time: 121 us; the launch traced here: 120 us
  starting transfers between devices  43.7 us (36%)
  blocking collectives  29 us (24%)
  Pallas kernels  24.9 us (21%)
  waiting for transfers between devices  17.1 us (14%)
  local copies, waits for them, and re-layouts  4.17 us (3%)
    all_to_all x5, starting transfers between devices, exchange(): return lax.all_to_all(array, axis, 0, 0, tiled=True)  38.3 us
    all_to_all x2, blocking collectives, exchange(): return lax.all_to_all(array, axis, 0, 0, tiled=True)  29 us
    pallas_call x15, Pallas kernels, call(): pl.pallas_call(kernel, out_shape=out_shape, in_specs=[spec(SMEM)] * len(s...  24.9 us
    all_to_all x5, waiting for transfers between devices, exchange(): return lax.all_to_all(array, axis, 0, 0, tiled=True)  17.1 us
    unnamed x14, local copies, waits for them, and re-layouts  4.17 us
    ppermute x3, starting transfers between devices, halos(): even = lax.ppermute(even_plane, 'brick', [(i, i ^ 1) for i in range(size)])  3.34 us
  transfers between devices with their start and end apart: 11, of which 5 were waited for; matrix products, arithmetic and copies ran while one was open for 1% of the time, Pallas kernels for 13%

profile of v4, /device:TPU:1, one launch (start us, length us, event | category | flops | bytes accessed | tf_op | source)
XLA Modules:
  0.0 119.9 jit_solution(14407763175662719146)
XLA Ops:
  0.6 0.0 copy-start.3
  0.6 2.3 %shard_map.112 = (f32[8,16,128]{2,1,0:T(8,128)}, f32[256,256]{1,0:T(8,128)}, f32[256,256]{1,0:T(8,128)S(1)}, s32[1,128]{1,0:T(1,128)S(1)}, s32[1,128]{1,0:T(1,12...) custom-call(s32[1]{0:T(128)} %bitcast.1.rank, s32[1]{0:T(128)} %bitcast.odd_brick, f32[1024,256]{1,0:T(8,128)} %bitcast.12, ...), custom_call_target="tpu_custom_call" | custom-call | flops 1048576 | bytes 524288 | tf_op jit(solution)/shard_map/pallas_call | solution.py:33
  2.9 10.0 %all-to-all-start = ((f32[8,16,128]{2,1,0:T(8,128)}), f32[8,16,128]{2,1,0:T(8,128)S(1)}, u32[]{:S(2)}, u32[]{:S(2)}) async-start(f32[8,16,128]{2,1,0:T(8,128)} %get-tuple-element.28), calls=%async_computation | async-start | bytes 131072 | tf_op jit(solution)/shard_map/all_to_all | solution.py:461
  12.9 0.7 collective-permute-start
  13.6 0.7 collective-permute-start.1
  14.3 0.0 copy-start.1
  14.3 1.2 %copy-done.1 = bf16[1,4096,128]{2,1,0:T(8,128)(2,1)S(1)} copy-done((bf16[1,4096,128]{2,1,0:T(8,128)(2,1)S(1)}, bf16[1,4096,128]{2,1,0:T(8,128)(2,1)}, u32[]{:S(2)}) %copy-start.1) | copy-done | bytes 1048600
  15.5 0.3 shard_map.113.right_ref.refs_0_.refs_1_
  15.9 4.7 %all-to-all-done.first_ref.refs_1_ = f32[8,16,128]{2,1,0:T(8,128)S(1)} async-done(((f32[8,16,128]{2,1,0:T(8,128)}), f32[8,16,128]{2,1,0:T(8,128)S(1)}, u32[]{:S(2)}, u32[]{:S(2)}) %all-to-all-start) | async-done | bytes 65568 | tf_op jit(solution)/shard_map/all_to_all | solution.py:461
  20.6 0.9 shard_map.114
  21.5 7.5 %all-to-all-start.1 = ((f32[32,8,128]{2,1,0:T(8,128)}), f32[32,8,128]{2,1,0:T(8,128)S(1)}, u32[]{:S(2)}, u32[]{:S(2)}) async-start(f32[32,8,128]{2,1,0:T(8,128)} %shard_map.114), calls=%async_computation.1 | async-start | bytes 262144 | tf_op jit(solution)/shard_map/all_to_all | solution.py:461
  29.0 0.0 collective-permute-done.refs_4_
  29.0 0.0 collective-permute-done.1.refs_5_
  29.0 0.0 copy-done.3
  29.0 0.0 copy-start.2
  29.1 4.8 %shard_map.115 = (f32[1024,256]{1,0:T(8,128)S(1)}, f32[1,128]{1,0:T(1,128)S(1)}) custom-call(s32[1]{0:T(128)} %bitcast.odd_brick, s32[1,128]{1,0:T(1,128)S(1)} %copy-done.3, s32[1,128]{1,0:T(1,128)S(1)} %get-tuple-element.30.cell_vec, f32[1024,256]{1,0:T(8,128)} %bitcast.13, f32[1024,256]{1,0:T(8,128)} %bitcast.15, f32[3,4,256,256]{3,2,1,0:T(8,128)} %refs_2_.5, ...), custom_call_target="tpu_custom_call" | custom-call | flops 16777216 | bytes 10485760 | tf_op jit(solution)/shard_map/pallas_call | solution.py:33
  33.9 2.7 %all-to-all-done.1.parts_ref = f32[32,8,128]{2,1,0:T(8,128)S(1)} async-done(((f32[32,8,128]{2,1,0:T(8,128)}), f32[32,8,128]{2,1,0:T(8,128)S(1)}, u32[]{:S(2)}, u32[]{:S(2)}) %all-to-all-start.1) | async-done | bytes 131104 | tf_op jit(solution)/shard_map/all_to_all | solution.py:461
  36.6 0.6 shard_map.116
  37.2 7.1 %all-to-all-start.2 = ((f32[8,16,128]{2,1,0:T(8,128)}), f32[8,16,128]{2,1,0:T(8,128)S(1)}, u32[]{:S(2)}, u32[]{:S(2)}) async-start(f32[8,16,128]{2,1,0:T(8,128)} %shard_map.116), calls=%async_computation.2 | async-start | bytes 131072 | tf_op jit(solution)/shard_map/all_to_all | solution.py:461
  44.3 7.5 %all-to-all-done.2.message_ref = f32[8,16,128]{2,1,0:T(8,128)S(1)} async-done(((f32[8,16,128]{2,1,0:T(8,128)}), f32[8,16,128]{2,1,0:T(8,128)S(1)}, u32[]{:S(2)}, u32[]{:S(2)}) %all-to-all-start.2) | async-done | bytes 65568 | tf_op jit(solution)/shard_map/all_to_all | solution.py:461
  51.8 1.2 %shard_map.118 = (f32[32,8,128]{2,1,0:T(8,128)}, f32[1,128]{1,0:T(1,128)S(1)}, f32[8,128]{1,0:T(8,128)S(1)}) custom-call(f32[8,16,128]{2,1,0:T(8,128)S(1)} %all-to-all-done.2.message_ref, f32[8,16,128]{2,1,0:T(8,128)S(1)} %all-to-all-done.first_ref.refs_1_, f32[2,8,128]{2,1,0:T(8,128)S(1)} %shard_map.117.old_ref, s32[8,128]{1,0:T(8,128)S(1)} %get-tuple-element.29.delay_ref, ...), custom_call_target="tpu_custom_call" | custom-call | flops 8388608 | bytes 1048576 | tf_op jit(solution)/shard_map/pallas_call | solution.py:33
  53.0 0.0 copy-done.2
  53.0 1.1 shard_map.119
  54.1 0.0 copy-start
  54.1 0.7 collective-permute-start.2
  54.8 0.7 collective-permute-start.3
  55.5 7.8 %all-to-all-start.3 = ((f32[32,8,128]{2,1,0:T(8,128)}), f32[32,8,128]{2,1,0:T(8,128)S(1)}, u32[]{:S(2)}, u32[]{:S(2)}) async-start(f32[32,8,128]{2,1,0:T(8,128)} %get-tuple-element.35), calls=%async_computation.3 | async-start | bytes 262144 | tf_op jit(solution)/shard_map/all_to_all | solution.py:461
  63.3 0.0 collective-permute-done.2.refs_4_
  63.3 0.0 copy-start.4
  63.3 0.0 collective-permute-done.3.refs_5_
  63.3 0.7 copy-done.4
  64.0 0.0 copy-start.5
  64.0 0.7 copy-done.5
  64.7 5.1 %shard_map.120 = (f32[1024,256]{1,0:T(8,128)S(1)}, f32[1,128]{1,0:T(1,128)S(1)}) custom-call(s32[1]{0:T(128)} %bitcast.odd_brick, s32[1,128]{1,0:T(1,128)S(1)} %copy-done.3, s32[1,128]{1,0:T(1,128)S(1)} %get-tuple-element.30.cell_vec, f32[1024,256]{1,0:T(8,128)S(1)} %get-tuple-element.38.refs_0_.refs_1_, f32[1024,256]{1,0:T(8,128)} %bitcast.14, ...), custom_call_target="tpu_custom_call" | custom-call | flops 16777216 | bytes 10485760 | tf_op jit(solution)/shard_map/pallas_call | solution.py:33
  69.8 0.0 copy-done
  69.9 1.0 all-to-all-done.3.parts_ref
  70.9 12.9 %all_to_all.35.message_ref = f32[8,16,128]{2,1,0:T(8,128)S(1)} all-to-all(f32[8,16,128]{2,1,0:T(8,128)S(1)} %shard_map.121), channel_id=1, replica_groups=mesh['shot'=8,'brick'=32] {'shot'}, dimensions={0} | all-to-all | bytes 131072 | tf_op jit(solution)/shard_map/all_to_all | solution.py:461
  83.7 0.5 shard_map.122
  84.3 1.1 shard_map.123
  85.4 1.9 %collective-permute-start.4 = (f32[256,256]{1,0:T(8,128)S(1)}, f32[256,256]{1,0:T(8,128)S(1)}, u32[]{:S(2)}, u32[]{:S(2)}) collective-permute-start(f32[256,256]{1,0:T(8,128)S(1)} %get-tuple-element.48), channel_id=1, source_target_pairs={{0,1},{1,0},{2,3},{3,2},{4,5},{5,4},{6,7},{7,6},{8,9},{9,8},{10,11... | collective-permute-start | bytes 786440 | tf_op jit(solution)/shard_map/ppermute | solution.py:466
  87.3 0.7 collective-permute-start.5
  87.9 16.2 %all_to_all.36.parts_ref = f32[32,8,128]{2,1,0:T(8,128)S(1)} all-to-all(f32[32,8,128]{2,1,0:T(8,128)S(1)} %get-tuple-element.47), channel_id=1, replica_groups=mesh['shot'=8,'brick'=32] {'brick'}, dimensions={0} | all-to-all | bytes 262144 | tf_op jit(solution)/shard_map/all_to_all | solution.py:461
  104.1 0.6 shard_map.124
  104.7 6.0 %all-to-all-start.6 = ((f32[8,1,128]{2,1,0:T(1,128)}), f32[8,1,128]{2,1,0:T(1,128)S(1)}, u32[]{:S(2)}, u32[]{:S(2)}) async-start(f32[8,1,128]{2,1,0:T(1,128)} %shard_map.124), calls=%async_computation.6 | async-start | bytes 8192 | tf_op jit(solution)/shard_map/all_to_all | solution.py:461
  110.7 0.6 copy.17
  111.3 1.0 copy.16
  112.2 0.0 collective-permute-done.4.refs_4_
  112.3 0.0 collective-permute-done.5.refs_5_
  112.3 4.2 %shard_map.125.field_ref = f32[1024,256]{1,0:T(8,128)S(1)} custom-call(s32[1]{0:T(128)} %bitcast.odd_brick, s32[1,128]{1,0:T(1,128)S(1)} %copy-done.3, s32[1,128]{1,0:T(1,128)S(1)} %get-tuple-element.30.cell_vec, f32[1024,256]{1,0:T(8,128)S(1)} %get-tuple-element.46.refs_0_, f32[1024,256]{1,0:T(8,128)} %copy-done, f32[3,4,256,256]{3,2,1,0:T(8,128)} %refs_2_.5, ...), custom_call_target="tpu_custom_call" | custom-call | flops 16777216 | bytes 10485760 | tf_op jit(solution)/shard_map/pallas_call | solution.py:33
  116.5 1.3 %all-to-all-done.6.parts_ref = f32[8,1,128]{2,1,0:T(1,128)S(1)} async-done(((f32[8,1,128]{2,1,0:T(1,128)}), f32[8,1,128]{2,1,0:T(1,128)S(1)}, u32[]{:S(2)}, u32[]{:S(2)}) %all-to-all-start.6) | async-done | bytes 4128 | tf_op jit(solution)/shard_map/all_to_all | solution.py:461
  117.7 2.0 %shard_map.126 = f32[1024,256]{1,0:T(8,128)} custom-call(s32[1,128]{1,0:T(1,128)S(1)} %copy-done.2, s32[1,128]{1,0:T(1,128)S(1)} %get-tuple-element.27.cell_vec, f32[8,1,128]{2,1,0:T(1,128)S(1)} %all-to-all-done.6.parts_ref, f32[1024,256]{1,0:T(8,128)S(1)} %shard_map.125.field_ref), custom_call_target="tpu_custom_call" | custom-call | flops 1048576 | bytes 2097152 | tf_op jit(solution)/shard_map/pallas_call | solution.py:33
  (2 shorter events, 0.0 us)
Async XLA Ops:
  0.6 28.4 %copy-start.3 = (s32[1,128]{1,0:T(1,128)S(1)}, s32[1,128]{1,0:T(1,128)}, u32[]{:S(2)}) copy-start(s32[1,128]{1,0:T(1,128)} %cell_smem.10) | copy-start | bytes 1540
  2.9 17.6 %all-to-all-start = ((f32[8,16,128]{2,1,0:T(8,128)}), f32[8,16,128]{2,1,0:T(8,128)S(1)}, u32[]{:S(2)}, u32[]{:S(2)}) async-start(f32[8,16,128]{2,1,0:T(8,128)} %get-tuple-element.28), calls=%async_computation | async-start | bytes 131072 | tf_op jit(solution)/shard_map/all_to_all | solution.py:461
  12.9 16.1 %collective-permute-start = (f32[256,256]{1,0:T(8,128)}, f32[256,256]{1,0:T(8,128)S(1)}, u32[]{:S(2)}, u32[]{:S(2)}) collective-permute-start(f32[256,256]{1,0:T(8,128)} %get-tuple-element.31), channel_id=1, source_target_pairs={{0,1},{1,0},{2,3},{3,2},{4,5},{5,4},{6,7},{7,6},{8,9},{9,8},{10,11... | collective-permute-start | bytes 786440 | tf_op jit(solution)/shard_map/ppermute | solution.py:466
  13.6 15.4 %collective-permute-start.1 = (f32[256,256]{1,0:T(8,128)S(1)}, f32[256,256]{1,0:T(8,128)S(1)}, u32[]{:S(2)}, u32[]{:S(2)}) collective-permute-start(f32[256,256]{1,0:T(8,128)S(1)} %get-tuple-element.32), channel_id=1, source_target_pairs={{1,2},{2,1},{3,4},{4,3},{5,6},{6,5},{7,8},{8,7},{9,10},{10,9},{11,... | collective-permute-start | bytes 786440 | tf_op jit(solution)/shard_map/ppermute | solution.py:467
  14.3 1.2 %copy-start.1 = (bf16[1,4096,128]{2,1,0:T(8,128)(2,1)S(1)}, bf16[1,4096,128]{2,1,0:T(8,128)(2,1)}, u32[]{:S(2)}) copy-start(bf16[1,4096,128]{2,1,0:T(8,128)(2,1)} %param.13) | copy-start | bytes 3145732
  21.5 15.1 %all-to-all-start.1 = ((f32[32,8,128]{2,1,0:T(8,128)}), f32[32,8,128]{2,1,0:T(8,128)S(1)}, u32[]{:S(2)}, u32[]{:S(2)}) async-start(f32[32,8,128]{2,1,0:T(8,128)} %shard_map.114), calls=%async_computation.1 | async-start | bytes 262144 | tf_op jit(solution)/shard_map/all_to_all | solution.py:461
  29.0 24.0 %copy-start.2 = (s32[1,128]{1,0:T(1,128)S(1)}, s32[1,128]{1,0:T(1,128)}, u32[]{:S(2)}) copy-start(s32[1,128]{1,0:T(1,128)} %cell_smem.11) | copy-start | bytes 1540
  37.2 14.6 %all-to-all-start.2 = ((f32[8,16,128]{2,1,0:T(8,128)}), f32[8,16,128]{2,1,0:T(8,128)S(1)}, u32[]{:S(2)}, u32[]{:S(2)}) async-start(f32[8,16,128]{2,1,0:T(8,128)} %shard_map.116), calls=%async_computation.2 | async-start | bytes 131072 | tf_op jit(solution)/shard_map/all_to_all | solution.py:461
  54.1 15.8 %copy-start = (f32[1024,256]{1,0:T(8,128)}, f32[1024,256]{1,0:T(8,128)S(1)}, u32[]{:S(2)}) copy-start(f32[1024,256]{1,0:T(8,128)S(1)} %get-tuple-element.38.refs_0_.refs_1_) | copy-start | bytes 3145732
  54.1 9.2 %collective-permute-start.2 = (f32[256,256]{1,0:T(8,128)S(1)}, f32[256,256]{1,0:T(8,128)S(1)}, u32[]{:S(2)}, u32[]{:S(2)}) collective-permute-start(f32[256,256]{1,0:T(8,128)S(1)} %get-tuple-element.39), channel_id=1, source_target_pairs={{0,1},{1,0},{2,3},{3,2},{4,5},{5,4},{6,7},{7,6},{8,9},{9,8},{10,11... | collective-permute-start | bytes 786440 | tf_op jit(solution)/shard_map/ppermute | solution.py:466
  54.8 8.5 %collective-permute-start.3 = (f32[256,256]{1,0:T(8,128)S(1)}, f32[256,256]{1,0:T(8,128)S(1)}, u32[]{:S(2)}, u32[]{:S(2)}) collective-permute-start(f32[256,256]{1,0:T(8,128)S(1)} %get-tuple-element.40), channel_id=1, source_target_pairs={{1,2},{2,1},{3,4},{4,3},{5,6},{6,5},{7,8},{8,7},{9,10},{10,9},{11,... | collective-permute-start | bytes 786440 | tf_op jit(solution)/shard_map/ppermute | solution.py:467
  55.5 15.4 %all-to-all-start.3 = ((f32[32,8,128]{2,1,0:T(8,128)}), f32[32,8,128]{2,1,0:T(8,128)S(1)}, u32[]{:S(2)}, u32[]{:S(2)}) async-start(f32[32,8,128]{2,1,0:T(8,128)} %get-tuple-element.35), calls=%async_computation.3 | async-start | bytes 262144 | tf_op jit(solution)/shard_map/all_to_all | solution.py:461
  63.3 0.7 copy-start.4
  64.0 0.7 copy-start.5
  85.4 26.9 %collective-permute-start.4 = (f32[256,256]{1,0:T(8,128)S(1)}, f32[256,256]{1,0:T(8,128)S(1)}, u32[]{:S(2)}, u32[]{:S(2)}) collective-permute-start(f32[256,256]{1,0:T(8,128)S(1)} %get-tuple-element.48), channel_id=1, source_target_pairs={{0,1},{1,0},{2,3},{3,2},{4,5},{5,4},{6,7},{7,6},{8,9},{9,8},{10,11... | collective-permute-start | bytes 786440 | tf_op jit(solution)/shard_map/ppermute | solution.py:466
  87.3 25.0 %collective-permute-start.5 = (f32[256,256]{1,0:T(8,128)S(1)}, f32[256,256]{1,0:T(8,128)S(1)}, u32[]{:S(2)}, u32[]{:S(2)}) collective-permute-start(f32[256,256]{1,0:T(8,128)S(1)} %get-tuple-element.49), channel_id=1, source_target_pairs={{1,2},{2,1},{3,4},{4,3},{5,6},{6,5},{7,8},{8,7},{9,10},{10,9},{11,... | collective-permute-start | bytes 786440 | tf_op jit(solution)/shard_map/ppermute | solution.py:467
  104.7 13.0 %all-to-all-start.6 = ((f32[8,1,128]{2,1,0:T(1,128)}), f32[8,1,128]{2,1,0:T(1,128)S(1)}, u32[]{:S(2)}, u32[]{:S(2)}) async-start(f32[8,1,128]{2,1,0:T(1,128)} %shard_map.124), calls=%async_computation.6 | async-start | bytes 8192 | tf_op jit(solution)/shard_map/all_to_all | solution.py:461

commit v5 on v4

--- a/solution.py
+++ b/solution.py
@@ -11,7 +11,6 @@
 VMEM = pltpu.VMEM
 SMEM = pltpu.SMEM
 HBM = pltpu.HBM
-FAR = True
 DMA = pltpu.SemaphoreType.DMA
 f32 = jnp.float32
 
@@ -103,15 +102,19 @@
     for s in range(8):
         out_ref[s] = message
     edges(odd_brick, field_ref, even_ref, odd_ref)
+    cells = jnp.broadcast_to(emit_ref[...].astype(f32), (8, 128))
+    for ref in (even_ref, odd_ref):
+        ref[256:264, 0:128] = cells
+        ref[256:264, 128:256] = cells
 
 
 def edges(odd_brick, field_ref, even_ref, odd_ref):
-    even_ref[...] = field_ref[pl.ds(pl.multiple_of(768 - 768 * odd_brick[0], 256), 256), :]
-    odd_ref[...] = field_ref[pl.ds(pl.multiple_of(768 * odd_brick[0], 256), 256), :]
+    even_ref[0:256, :] = field_ref[pl.ds(pl.multiple_of(768 - 768 * odd_brick[0], 256), 256), :]
+    odd_ref[0:256, :] = field_ref[pl.ds(pl.multiple_of(768 * odd_brick[0], 256), 256), :]
 
 
 def first_message(rank, odd_brick, delays, rec_cell, emit_cell, past, field):
-    plane = VMEM((256, 256), f32)
+    plane = VMEM((264, 256), f32)
     row = VMEM((1, 128), jnp.int32)
     return call(
         first_kernel,
@@ -163,8 +166,20 @@
 
 def multiply(chosen, right_ref, out_ref):
     product = jnp.dot(chosen.astype(jnp.bfloat16), right_ref[...], preferred_element_type=f32)
+    wide = out_ref.shape[1] == 24
     for b in range(32):
-        out_ref[b] = product[:, b * 128 : (b + 1) * 128]
+        block = product[:, b * 128 : (b + 1) * 128]
+        if not wide:
+            out_ref[b] = block
+            continue
+        out_ref[b, 8:16, :] = block
+        if b < 31:
+            out_ref[b + 1, 0:8, :] = block
+        if b > 0:
+            out_ref[b - 1, 16:24, :] = block
+    if wide:
+        out_ref[0, 0:8, :] = jnp.zeros((8, 128), f32)
+        out_ref[31, 16:24, :] = jnp.zeros((8, 128), f32)
 
 
 def old_samples(first_ref, where):
@@ -180,15 +195,19 @@
 
 
 def emission_start(first, delay, right):
-    out = VMEM((32, 8, 128), f32)
+    out = VMEM((32, 24, 128), f32)
     return call(start_kernel, out, (8 << 20, 1 << 20), arrays=[first, delay, right])
 
 
 def samples_kernel(moment, message_ref, first_ref, old_ref, delay_ref, own_ref, *refs):
-    *newer_refs, right_ref, out_ref, mine_ref, sample_ref = refs
+    *newer_refs, right_ref, out_ref, mine_ref, near_ref, sample_ref = refs
     total = message_ref[0, 0:8, :]
     for lag in range(1, 8):
         total = total + message_ref[lag, 0:8, :]
+    near = message_ref[0, 8:16, :]
+    for lag in range(1, 8):
+        near = near + message_ref[lag, 8:16, :]
+    near_ref[...] = near
     values = jnp.concatenate([message_ref[s, 8:9, :] for s in range(8)], axis=0)
     wide = jnp.concatenate([total] * 8, axis=1)
     block = lax.broadcasted_iota(jnp.int32, (8, 1024), 1) >> 7
@@ -214,15 +233,31 @@
 def samples_and_emission(moment, message, first, old, delay, own, newer, right):
     return call(
         functools.partial(samples_kernel, moment),
-        (VMEM((32, 8, 128), f32), VMEM((1, 128), f32), VMEM((8, 128), f32)),
+        (VMEM((32, 24 if moment == 1 else 8, 128), f32), VMEM((1, 128), f32), VMEM((8, 128), f32), VMEM((8, 128), f32)),
         (8 << 20, 1 << 20),
         arrays=[message, first, old, delay, own, *newer, right],
     )
 
 
+def spots(values, cells, plane):
+    cells = cells.astype(jnp.int32)
+    values = jnp.where((cells >> 16) == plane, values, 0.0)
+    column = sheet_of(((cells >> 8) & 255).astype(f32), 256).astype(jnp.int32)
+    rows = jnp.where(lax.broadcasted_iota(jnp.int32, (128, 256), 1) == column, 1.0, 0.0).astype(jnp.bfloat16)
+    rest = jnp.where(lanes_of(cells), sheet_of(values, 256), 0.0)
+    terms = []
+    for _ in range(3):
+        term = rest.astype(jnp.bfloat16)
+        rest = rest - term.astype(f32)
+        terms.append(lax.dot_general(rows, term, (((0,), (0,)), ((), ())), preferred_element_type=f32))
+    return (terms[2] + terms[1]) + terms[0]
+
+
 def stencil_kernel(take, inside, odd_brick, cell_smem, cell_vec, *refs):
+    if inside:
+        near_ref, near_cells_ref, *refs = refs
     field_in, prev_any, diag_any, cross_any, even_any, odd_any, *refs = refs
-    *outs, field_ref, prev_ref, diag_ref, cross_ref, low_ref, high_ref, skew_ref, sum_ref, sems, edge_sems = refs
+    *outs, rows_ref, field_ref, prev_ref, diag_ref, cross_ref, low_ref, high_ref, skew_ref, sum_ref, sems, edge_sems = refs
     out_ref, *outs = outs
     order = (1, 2, 0, 3)
 
@@ -296,6 +331,12 @@
         if x == 0:
             for k in (0, 1):
                 pltpu.make_async_copy(odd_any, low_ref, edge_sems.at[k]).wait()
+            if inside:
+                low_ref[...] = low_ref[...] + spots(near_ref[1:2, :], near_cells_ref[0:1, :], 3)
+                high_ref[...] = high_ref[...] + spots(near_ref[2:3, :], near_cells_ref[1:2, :], 0)
+            else:
+                outs[-1][0:1, :] = low_ref[256:257, 0:128]
+                outs[-1][1:2, :] = high_ref[256:257, 0:128]
         for k in ready[x]:
             for copy in begun.get(k, ()):
                 copy.wait()
@@ -347,29 +388,31 @@
                 values.append((twice - prev[h]) + (second + 0.5 * mixed))
             put(out_ref, 256 * x + row, values)
     if take:
-        value_ref, rows_ref = outs
-        value_ref[...] = gather_row(out_ref, cell_smem, cell_vec[...], rows_ref)
-
-
-def stencil(take, inside, odd_brick, rec_cell, rec, field, prev, diag, cross, even, odd):
+        edges(odd_brick, out_ref, outs[1], outs[2])
+        outs[0][...] = gather_row(out_ref, cell_smem, cell_vec[...], rows_ref)
+
+
+def stencil(take, odd_brick, rec_cell, rec, field, prev, diag, cross, even, odd, near=()):
+    plane = VMEM((256, 256), f32)
+    inside = bool(near)
     out_shape = [VMEM((1024, 256), f32)]
-    scratch = []
     if take:
-        out_shape.append(VMEM((1, 128), f32))
-        scratch.append(VMEM((128, 256), f32))
-    plane = VMEM((256, 256), f32)
+        out_shape += [VMEM((1, 128), f32), plane, plane]
+    if not inside:
+        out_shape.append(VMEM((8, 128), f32))
     coef = VMEM((3, 4, 256, 256), f32)
     whole = VMEM((1024, 256), f32)
-    scratch += [VMEM((8, 128), f32) if inside else whole, whole, coef, coef, plane, plane]
+    edge = VMEM(even.shape, f32)
+    scratch = [VMEM((128, 256), f32), VMEM((8, 128), f32) if inside else whole, whole, coef, coef, edge, edge]
     scratch += [VMEM((1536, 256), f32), whole, DMA((4, 8)), DMA((2,))]
     return call(
         functools.partial(stencil_kernel, take, inside),
         tuple(out_shape),
         (16 << 20, 10 << 20),
         scalars=[odd_brick, rec_cell],
-        arrays=[rec] + [field] * inside,
-        far=[field] * (not inside) + [prev, diag, cross] + ([even, odd] if FAR and take and inside else []),
-        free=[] if FAR and take and inside else [even, odd],
+        arrays=[rec, *near] + [field] * inside,
+        far=[field] * (not inside) + [prev, diag, cross] + [even, odd] * (inside and take),
+        free=[even, odd] * (not inside or not take),
         scratch=scratch,
         room=14,
     )
@@ -382,13 +425,11 @@
         target_ref[pl.ds(row, 1), :] = target_ref[pl.ds(row, 1), :] + rows_ref[j : j + 1, :]
 
 
-def scatter_kernel(odd_brick, cell_smem, cell_vec, mine_ref, field_ref, *refs):
+def scatter_kernel(cell_smem, cell_vec, mine_ref, field_ref, *refs):
     *refs, rows_ref = refs
-    old = refs[: len(refs) - 4] if len(refs) > 3 else []
-    out_ref, even_ref, odd_ref = refs[len(old) : len(old) + 3]
     del field_ref
-    add_at(cell_smem, cell_vec, mine_ref[...], out_ref, rows_ref)
-    edges(odd_brick, out_ref, even_ref, odd_ref)
+    old = refs[:-2]
+    add_at(cell_smem, cell_vec, mine_ref[...], refs[-2] if old else refs[-1], rows_ref)
     if old:
         own_ref, first_ref, *sample_refs = old
         own = own_ref[...] > 0.5
@@ -398,19 +439,18 @@
         refs[-1][...] = jnp.concatenate(series, axis=0).astype(jnp.bfloat16)
 
 
-def scatter(odd_brick, emit_cell, emit, mine, field, old=()):
-    plane = VMEM((256, 256), f32)
-    outs = (VMEM((1024, 256), f32), plane, plane)
+def scatter(emit_cell, emit, mine, field, old=()):
+    outs = [VMEM((1024, 256), f32)]
     if old:
-        outs += (VMEM((3, 128), jnp.bfloat16),)
+        outs.append(VMEM((3, 128), jnp.bfloat16))
     return call(
         scatter_kernel,
-        outs,
+        tuple(outs),
         (1 << 20, 1 << 19),
-        scalars=[odd_brick, emit_cell],
+        scalars=[emit_cell],
         arrays=[emit, mine, field, *old],
         scratch=[VMEM((128, 256), f32)],
-        aliases={4: 0},
+        aliases={3: 0},
     )
 
 
@@ -442,14 +482,13 @@
     for b in range(4, 32):
         sums[b % 4] = sums[b % 4] + parts_ref[b]
     total = (sums[0] + sums[1]) + (sums[2] + sums[3])
-    if not value_refs:
-        for s in range(8):
+    for s in range(8):
+        if not value_refs:
             out_ref[s] = total[s : s + 1, :]
-        return
-    value = jnp.broadcast_to(value_refs[0][...], (8, 128))
-    for s in range(8):
-        out_ref[s, 0:8, :] = total
-        out_ref[s, 8:16, :] = value
+            continue
+        out_ref[s, 0:8, :] = total[8:16]
+        rows = [value_refs[0][...], total[s : s + 1], total[16 + s : 17 + s], jnp.zeros((5, 128), f32)]
+        out_ref[s, 8:16, :] = jnp.concatenate(rows, axis=0)
 
 
 def spread(parts, *value):
@@ -479,30 +518,34 @@
     first = exchange(message, "shot")
     even, odd = halos(*planes)
     right = turn(green[0])
-    following, value = stencil(True, False, odd_brick, rec_cell, rec, current, before, diag, cross, even, odd)
+    following, value, *planes, cells = stencil(True, odd_brick, rec_cell, rec, current, before, diag, cross, even, odd)
     partial = emission_start(first, delay, right)
     parts = exchange(partial, "brick")
     old = older(first, delay)
     message = spread(parts, value)
 
     answer = exchange(message, "shot")
-    partial, mine, sample1 = samples_and_emission(1, answer, first, old, delay, own, [], right)
-    earlier = current
-    current, *planes = scatter(odd_brick, emit_cell, emit, mine, following)
     even, odd = halos(*planes)
-    parts = exchange(partial, "brick")
-    following, value = stencil(True, True, odd_brick, rec_cell, rec, current, earlier, diag, cross, even, odd)
-    message = spread(parts, value)
-
-    answer = exchange(message, "shot")
-    partial, mine, sample2 = samples_and_emission(2, answer, first, old, delay, own, [sample1], right)
+    partial, mine, near, sample1 = samples_and_emission(1, answer, first, old, delay, own, [], right)
     parts = exchange(partial, "brick")
     earlier = current
-    current, *planes, recorded = scatter(odd_brick, emit_cell, emit, mine, following, (own, first, sample1, sample2))
+    (current,) = scatter(emit_cell, emit, mine, following)
+    following, value, *planes = stencil(
+        True, odd_brick, rec_cell, rec, current, earlier, diag, cross, even, odd, (near, cells)
+    )
+    message = spread(parts, value)
+
+    answer = exchange(message, "shot")
     even, odd = halos(*planes)
-    (following,) = stencil(False, True, odd_brick, rec_cell, rec, current, earlier, diag, cross, even, odd)
+    partial, mine, near, sample2 = samples_and_emission(2, answer, first, old, delay, own, [sample1], right)
+    parts = exchange(partial, "brick")
+    earlier = current
+    current, recorded = scatter(emit_cell, emit, mine, following, (own, first, sample1, sample2))
     message = spread(parts)
     parts = exchange(message, "shot")
+    (following,) = stencil(
+        False, odd_brick, rec_cell, rec, current, earlier, diag, cross, even, odd, (near, cells)
+    )
     after = last_scatter(emit_cell, emit, parts, following)
     shape = field_now.shape
     return current.reshape(shape), after.reshape(shape), recorded[:, None]

time: 121 us -> 144 us (1.19)
  starting transfers between devices: 43.7 us -> 58.8 us
  waiting for transfers between devices: 17.1 us -> 31.6 us
  blocking collectives: 29 us -> 19 us
  Pallas kernels: 24.9 us -> 27.7 us
  local copies, waits for them, and re-layouts: 4.17 us -> 5.69 us
    ppermute x3, waiting for transfers between devices: 0.01 us -> 16.5 us  [halos(): even = lax.ppermute(even_plane, 'brick', [(i, i ^ 1) for i in range(size)])]
    all_to_all x5 -> x6, starting transfers between devices: 38.3 us -> 49.1 us  [exchange(): return lax.all_to_all(array, axis, 0, 0, tiled=True)]
    all_to_all x2 -> x1, blocking collectives: 29 us -> 19 us  [exchange(): return lax.all_to_all(array, axis, 0, 0, tiled=True)]
    ppermute x3, starting transfers between devices: 3.34 us -> 7.71 us  [halos(): even = lax.ppermute(even_plane, 'brick', [(i, i ^ 1) for i in range(size)])]
    pallas_call x15, Pallas kernels: 24.9 us -> 27.7 us  [call(): pl.pallas_call(kernel, out_shape=out_shape, in_specs=[spec(SMEM)] * len(s...]
    all_to_all x5 -> x6, waiting for transfers between devices: 17.1 us -> 15.1 us  [exchange(): return lax.all_to_all(array, axis, 0, 0, tiled=True)]
    unnamed x14 -> x20, local copies, waits for them, and re-layouts: 4.17 us -> 5.69 us
  transfers between devices with their start and end apart: 11 -> 12, of which waited for: 5 -> 5; matrix products, arithmetic and copies ran while one was open for 1% -> 1% of each run, Pallas kernels for 13% -> 13%
where the time goes in v5:
time: 144 us
  starting transfers between devices  58.8 us (41%)
  waiting for transfers between devices  31.6 us (22%)
  Pallas kernels  27.7 us (19%)
  blocking collectives  19 us (13%)
  local copies, waits for them, and re-layouts  5.69 us (4%)
    all_to_all x6, starting transfers between devices, exchange(): return lax.all_to_all(array, axis, 0, 0, tiled=True)  49.1 us
    pallas_call x15, Pallas kernels, call(): pl.pallas_call(kernel, out_shape=out_shape, in_specs=[spec(SMEM)] * len(s...  27.7 us
    all_to_all x1, blocking collectives, exchange(): return lax.all_to_all(array, axis, 0, 0, tiled=True)  19 us
    ppermute x3, waiting for transfers between devices, halos(): even = lax.ppermute(even_plane, 'brick', [(i, i ^ 1) for i in range(size)])  16.5 us
    all_to_all x6, waiting for transfers between devices, exchange(): return lax.all_to_all(array, axis, 0, 0, tiled=True)  15.1 us
    ppermute x3, starting transfers between devices, halos(): even = lax.ppermute(even_plane, 'brick', [(i, i ^ 1) for i in range(size)])  7.71 us
    unnamed x20, local copies, waits for them, and re-layouts  5.69 us
  transfers between devices with their start and end apart: 12, of which 5 were waited for; matrix products, arithmetic and copies ran while one was open for 1% of the time, Pallas kernels for 13%

profile of v5, /device:TPU:1, one launch (start us, length us, event | category | flops | bytes accessed | tf_op | source)
XLA Modules:
  0.0 143.7 jit_solution(470502198233910577)
XLA Ops:
  0.6 0.0 copy-start.2
  0.6 2.3 %shard_map.112 = (f32[8,16,128]{2,1,0:T(8,128)}, f32[264,256]{1,0:T(8,128)S(1)}, f32[264,256]{1,0:T(8,128)S(1)}, s32[1,128]{1,0:T(1,128)S(1)}, s32[1,128]{1,0:T(...) custom-call(s32[1]{0:T(128)} %bitcast.rank, s32[1]{0:T(128)} %bitcast.1.odd_brick, f32[1024,256]{1,0:T(8,128)} %bitcast.12, ...), custom_call_target="tpu_custom_call" | custom-call | flops 1048576 | bytes 524288 | tf_op jit(solution)/shard_map/pallas_call | solution.py:32
  2.9 10.0 %all-to-all-start = ((f32[8,16,128]{2,1,0:T(8,128)}), f32[8,16,128]{2,1,0:T(8,128)S(1)}, u32[]{:S(2)}, u32[]{:S(2)}) async-start(f32[8,16,128]{2,1,0:T(8,128)} %get-tuple-element.30), calls=%async_computation | async-start | bytes 131072 | tf_op jit(solution)/shard_map/all_to_all | solution.py:500
  12.9 0.0 copy-start.1
  12.9 1.2 copy-done.1
  14.1 0.3 shard_map.113.right_ref.refs_0_.refs_1_
  14.4 6.0 %all-to-all-done.first_ref.refs_1_ = f32[8,16,128]{2,1,0:T(8,128)S(1)} async-done(((f32[8,16,128]{2,1,0:T(8,128)}), f32[8,16,128]{2,1,0:T(8,128)S(1)}, u32[]{:S(2)}, u32[]{:S(2)}) %all-to-all-start) | async-done | bytes 65568 | tf_op jit(solution)/shard_map/all_to_all | solution.py:500
  20.5 1.0 shard_map.114
  21.5 7.2 %all-to-all-start.1 = ((f32[32,24,128]{2,1,0:T(8,128)}), f32[32,24,128]{2,1,0:T(8,128)S(1)}, u32[]{:S(2)}, u32[]{:S(2)}) async-start(f32[32,24,128]{2,1,0:T(8,128)} %shard_map.114), calls=%async_computation.1 | async-start | bytes 786432 | tf_op jit(solution)/shard_map/all_to_all | solution.py:500
  28.7 1.3 collective-permute-start
  30.0 0.7 collective-permute-start.1
  30.7 8.8 %collective-permute-done.refs_4_ = f32[264,256]{1,0:T(8,128)S(1)} collective-permute-done((f32[264,256]{1,0:T(8,128)S(1)}, f32[264,256]{1,0:T(8,128)S(1)}, u32[]{:S(2)}, u32[]{:S(2)}) %collective-permute-start) | collective-permute-done | bytes 270368 | tf_op jit(solution)/shard_map/ppermute | solution.py:505
  39.5 0.0 collective-permute-done.1.refs_5_
  39.5 0.0 copy-done.2
  39.5 0.0 copy-start.3
  39.5 4.8 %shard_map.115 = (f32[1024,256]{1,0:T(8,128)S(1)}, f32[1,128]{1,0:T(1,128)S(1)}, f32[256,256]{1,0:T(8,128)S(1)}, f32[256,256]{1,0:T(8,128)S(1)}, f32[8,128]{1,0:T(8,128)S(1)}) custom-call(s32[1]{0:T(128)} %bitcast.1.odd_brick, s32[1,128]{1,0:T(1,128)S(1)} %copy-done.2, s32[1,128]{1,0:T(1,128)S(1)} %get-tuple-element.32.cell_vec, f32[1024,256]{1,0:T(8,128)} %bitcast.13, ...), custom_call_target="tpu_custom_call" | custom-call | flops 16777216 | bytes 10485760 | tf_op jit(solution)/shard_map/pallas_call | solution.py:32
  44.3 0.0 copy-start.5
  44.3 0.7 copy-done.5
  45.0 0.0 copy-start.6
  45.0 0.7 copy-done.6
  45.7 0.0 all-to-all-done.1.parts_ref
  45.7 0.7 shard_map.116
  46.4 7.2 %all-to-all-start.2 = ((f32[8,16,128]{2,1,0:T(8,128)}), f32[8,16,128]{2,1,0:T(8,128)S(1)}, u32[]{:S(2)}, u32[]{:S(2)}) async-start(f32[8,16,128]{2,1,0:T(8,128)} %shard_map.116), calls=%async_computation.2 | async-start | bytes 131072 | tf_op jit(solution)/shard_map/all_to_all | solution.py:500
  53.7 7.4 %all-to-all-done.2.message_ref = f32[8,16,128]{2,1,0:T(8,128)S(1)} async-done(((f32[8,16,128]{2,1,0:T(8,128)}), f32[8,16,128]{2,1,0:T(8,128)S(1)}, u32[]{:S(2)}, u32[]{:S(2)}) %all-to-all-start.2) | async-done | bytes 65568 | tf_op jit(solution)/shard_map/all_to_all | solution.py:500
  61.1 1.3 shard_map.118
  62.4 11.4 %all-to-all-start.3 = ((f32[32,24,128]{2,1,0:T(8,128)}), f32[32,24,128]{2,1,0:T(8,128)}, u32[]{:S(2)}, u32[]{:S(2)}) async-start(f32[32,24,128]{2,1,0:T(8,128)} %get-tuple-element.37), calls=%async_computation.3 | async-start | bytes 786432 | tf_op jit(solution)/shard_map/all_to_all | solution.py:500
  73.8 1.3 collective-permute-start.2
  75.1 0.7 collective-permute-start.3
  75.7 0.0 copy-done.3
  75.8 1.0 shard_map.119.refs_2_.refs_3_
  76.8 0.0 copy-start
  76.8 7.7 %collective-permute-done.2.refs_6_ = f32[256,256]{1,0:T(8,128)S(1)} collective-permute-done((f32[256,256]{1,0:T(8,128)}, f32[256,256]{1,0:T(8,128)S(1)}, u32[]{:S(2)}, u32[]{:S(2)}) %collective-permute-start.2) | collective-permute-done | bytes 262176 | tf_op jit(solution)/shard_map/ppermute | solution.py:505
  84.5 0.0 copy-start.7
  84.5 0.0 collective-permute-done.3.refs_7_
  84.5 0.0 copy-start.8
  84.5 0.7 copy-done.7
  85.2 0.1 copy-done.8
  85.3 5.6 %shard_map.120 = (f32[1024,256]{1,0:T(8,128)S(1)}, f32[1,128]{1,0:T(1,128)S(1)}, f32[256,256]{1,0:T(8,128)S(1)}, f32[256,256]{1,0:T(8,128)S(1)}) custom-call(s32[1]{0:T(128)} %bitcast.1.odd_brick, s32[1,128]{1,0:T(1,128)S(1)} %copy-done.2, s32[1,128]{1,0:T(1,128)S(1)} %get-tuple-element.32.cell_vec, f32[8,128]{1,0:T(8,128)S(1)} %get-tuple-element.38.refs_0_, ...), custom_call_target="tpu_custom_call" | custom-call | flops 16777216 | bytes 10485760 | tf_op jit(solution)/shard_map/pallas_call | solution.py:32
  91.0 0.0 copy-done
  91.0 0.0 copy-start.4
  91.0 0.7 copy-done.4
  91.7 0.0 all-to-all-done.3.parts_ref
  91.7 1.7 %shard_map.121 = f32[8,16,128]{2,1,0:T(8,128)} custom-call(f32[32,24,128]{2,1,0:T(8,128)} %all-to-all-done.3.parts_ref, f32[1,128]{1,0:T(1,128)S(1)} %get-tuple-element.44.refs_0_), custom_call_target="tpu_custom_call" | custom-call | flops 32768 | bytes 131072 | tf_op jit(solution)/shard_map/pallas_call | solution.py:32
  93.3 6.9 %all-to-all-start.4 = ((f32[8,16,128]{2,1,0:T(8,128)}), f32[8,16,128]{2,1,0:T(8,128)S(1)}, u32[]{:S(2)}, u32[]{:S(2)}) async-start(f32[8,16,128]{2,1,0:T(8,128)} %shard_map.121), calls=%async_computation.4 | async-start | bytes 131072 | tf_op jit(solution)/shard_map/all_to_all | solution.py:500
  100.3 5.1 %collective-permute-start.4 = (f32[256,256]{1,0:T(8,128)}, f32[256,256]{1,0:T(8,128)S(1)}, u32[]{:S(2)}, u32[]{:S(2)}) collective-permute-start(f32[256,256]{1,0:T(8,128)} %copy-done.4), channel_id=1, source_target_pairs={{0,1},{1,0},{2,3},{3,2},{4,5},{5,4},{6,7},{7,6},{8,9},{9,8},{10,11... | collective-permute-start | bytes 786440 | tf_op jit(solution)/shard_map/ppermute | solution.py:505
  105.4 0.7 collective-permute-start.5
  106.1 1.6 %all-to-all-done.4.message_ref = f32[8,16,128]{2,1,0:T(8,128)S(1)} async-done(((f32[8,16,128]{2,1,0:T(8,128)}), f32[8,16,128]{2,1,0:T(8,128)S(1)}, u32[]{:S(2)}, u32[]{:S(2)}) %all-to-all-start.4) | async-done | bytes 65568 | tf_op jit(solution)/shard_map/all_to_all | solution.py:500
  107.7 0.5 shard_map.122
  108.3 19.0 %all_to_all.35.parts_ref = f32[32,8,128]{2,1,0:T(8,128)S(1)} all-to-all(f32[32,8,128]{2,1,0:T(8,128)S(1)} %get-tuple-element.50), channel_id=1, replica_groups=mesh['shot'=8,'brick'=32] {'brick'}, dimensions={0} | all-to-all | bytes 262144 | tf_op jit(solution)/shard_map/all_to_all | solution.py:500
  127.2 0.6 shard_map.124
  127.8 6.3 %all-to-all-start.6 = ((f32[8,1,128]{2,1,0:T(1,128)}), f32[8,1,128]{2,1,0:T(1,128)S(1)}, u32[]{:S(2)}, u32[]{:S(2)}) async-start(f32[8,1,128]{2,1,0:T(1,128)} %shard_map.124), calls=%async_computation.6 | async-start | bytes 8192 | tf_op jit(solution)/shard_map/all_to_all | solution.py:500
  134.2 1.2 shard_map.123
  135.3 0.6 copy.17
  135.9 1.0 copy.16
  136.9 0.0 collective-permute-done.4.refs_6_
  136.9 0.0 collective-permute-done.5.refs_7_
  136.9 4.6 %shard_map.125.field_ref = f32[1024,256]{1,0:T(8,128)S(1)} custom-call(s32[1]{0:T(128)} %bitcast.1.odd_brick, s32[1,128]{1,0:T(1,128)S(1)} %copy-done.2, s32[1,128]{1,0:T(1,128)S(1)} %get-tuple-element.32.cell_vec, f32[8,128]{1,0:T(8,128)S(1)} %get-tuple-element.51.refs_0_, f32[8,128]{1,0:T(8,128)S(1)} %get-tuple-element.39.refs_1_, ...), custom_call_target="tpu_custom_call" | custom-call | flops 16777216 | bytes 10485760 | tf_op jit(solution)/shard_map/pallas_call | solution.py:32
  141.5 0.0 all-to-all-done.6.parts_ref
  141.5 2.0 %shard_map.126 = f32[1024,256]{1,0:T(8,128)} custom-call(s32[1,128]{1,0:T(1,128)S(1)} %copy-done.3, s32[1,128]{1,0:T(1,128)S(1)} %get-tuple-element.29.cell_vec, f32[8,1,128]{2,1,0:T(1,128)S(1)} %all-to-all-done.6.parts_ref, f32[1024,256]{1,0:T(8,128)S(1)} %shard_map.125.field_ref), custom_call_target="tpu_custom_call" | custom-call | flops 1048576 | bytes 2097152 | tf_op jit(solution)/shard_map/pallas_call | solution.py:32
  (1 shorter events, 0.0 us)
Async XLA Ops:
  0.6 38.8 %copy-start.2 = (s32[1,128]{1,0:T(1,128)S(1)}, s32[1,128]{1,0:T(1,128)}, u32[]{:S(2)}) copy-start(s32[1,128]{1,0:T(1,128)} %cell_smem.10) | copy-start | bytes 1540
  2.9 17.5 %all-to-all-start = ((f32[8,16,128]{2,1,0:T(8,128)}), f32[8,16,128]{2,1,0:T(8,128)S(1)}, u32[]{:S(2)}, u32[]{:S(2)}) async-start(f32[8,16,128]{2,1,0:T(8,128)} %get-tuple-element.30), calls=%async_computation | async-start | bytes 131072 | tf_op jit(solution)/shard_map/all_to_all | solution.py:500
  12.9 1.2 copy-start.1
  21.5 24.3 %all-to-all-start.1 = ((f32[32,24,128]{2,1,0:T(8,128)}), f32[32,24,128]{2,1,0:T(8,128)S(1)}, u32[]{:S(2)}, u32[]{:S(2)}) async-start(f32[32,24,128]{2,1,0:T(8,128)} %shard_map.114), calls=%async_computation.1 | async-start | bytes 786432 | tf_op jit(solution)/shard_map/all_to_all | solution.py:500
  28.7 10.8 %collective-permute-start = (f32[264,256]{1,0:T(8,128)S(1)}, f32[264,256]{1,0:T(8,128)S(1)}, u32[]{:S(2)}, u32[]{:S(2)}) collective-permute-start(f32[264,256]{1,0:T(8,128)S(1)} %get-tuple-element.33), channel_id=1, source_target_pairs={{0,1},{1,0},{2,3},{3,2},{4,5},{5,4},{6,7},{7,6},{8,9},{9,8},{10,11... | collective-permute-start | bytes 811016 | tf_op jit(solution)/shard_map/ppermute | solution.py:505
  30.0 9.5 %collective-permute-start.1 = (f32[264,256]{1,0:T(8,128)S(1)}, f32[264,256]{1,0:T(8,128)S(1)}, u32[]{:S(2)}, u32[]{:S(2)}) collective-permute-start(f32[264,256]{1,0:T(8,128)S(1)} %get-tuple-element.34), channel_id=1, source_target_pairs={{1,2},{2,1},{3,4},{4,3},{5,6},{6,5},{7,8},{8,7},{9,10},{10,9},{11,... | collective-permute-start | bytes 811016 | tf_op jit(solution)/shard_map/ppermute | solution.py:506
  39.5 36.3 %copy-start.3 = (s32[1,128]{1,0:T(1,128)S(1)}, s32[1,128]{1,0:T(1,128)}, u32[]{:S(2)}) copy-start(s32[1,128]{1,0:T(1,128)} %cell_smem.11) | copy-start | bytes 1540
  44.3 0.7 copy-start.5
  45.0 0.7 copy-start.6
  46.4 14.7 %all-to-all-start.2 = ((f32[8,16,128]{2,1,0:T(8,128)}), f32[8,16,128]{2,1,0:T(8,128)S(1)}, u32[]{:S(2)}, u32[]{:S(2)}) async-start(f32[8,16,128]{2,1,0:T(8,128)} %shard_map.116), calls=%async_computation.2 | async-start | bytes 131072 | tf_op jit(solution)/shard_map/all_to_all | solution.py:500
  62.4 29.3 %all-to-all-start.3 = ((f32[32,24,128]{2,1,0:T(8,128)}), f32[32,24,128]{2,1,0:T(8,128)}, u32[]{:S(2)}, u32[]{:S(2)}) async-start(f32[32,24,128]{2,1,0:T(8,128)} %get-tuple-element.37), calls=%async_computation.3 | async-start | bytes 786432 | tf_op jit(solution)/shard_map/all_to_all | solution.py:500
  73.8 10.7 %collective-permute-start.2 = (f32[256,256]{1,0:T(8,128)}, f32[256,256]{1,0:T(8,128)S(1)}, u32[]{:S(2)}, u32[]{:S(2)}) collective-permute-start(f32[256,256]{1,0:T(8,128)} %copy-done.6), channel_id=1, source_target_pairs={{0,1},{1,0},{2,3},{3,2},{4,5},{5,4},{6,7},{7,6},{8,9},{9,8},{10,11... | collective-permute-start | bytes 786440 | tf_op jit(solution)/shard_map/ppermute | solution.py:505
  75.1 9.4 %collective-permute-start.3 = (f32[256,256]{1,0:T(8,128)}, f32[256,256]{1,0:T(8,128)S(1)}, u32[]{:S(2)}, u32[]{:S(2)}) collective-permute-start(f32[256,256]{1,0:T(8,128)} %copy-done.5), channel_id=1, source_target_pairs={{1,2},{2,1},{3,4},{4,3},{5,6},{6,5},{7,8},{8,7},{9,10},{10,9},{11,... | collective-permute-start | bytes 786440 | tf_op jit(solution)/shard_map/ppermute | solution.py:506
  76.8 14.2 %copy-start = (f32[1024,256]{1,0:T(8,128)}, f32[1024,256]{1,0:T(8,128)S(1)}, u32[]{:S(2)}) copy-start(f32[1024,256]{1,0:T(8,128)S(1)} %shard_map.119.refs_2_.refs_3_) | copy-start | bytes 3145732
  84.5 0.7 copy-start.7
  84.5 0.8 copy-start.8
  91.0 0.7 copy-start.4
  93.3 14.4 %all-to-all-start.4 = ((f32[8,16,128]{2,1,0:T(8,128)}), f32[8,16,128]{2,1,0:T(8,128)S(1)}, u32[]{:S(2)}, u32[]{:S(2)}) async-start(f32[8,16,128]{2,1,0:T(8,128)} %shard_map.121), calls=%async_computation.4 | async-start | bytes 131072 | tf_op jit(solution)/shard_map/all_to_all | solution.py:500
  100.3 36.6 %collective-permute-start.4 = (f32[256,256]{1,0:T(8,128)}, f32[256,256]{1,0:T(8,128)S(1)}, u32[]{:S(2)}, u32[]{:S(2)}) collective-permute-start(f32[256,256]{1,0:T(8,128)} %copy-done.4), channel_id=1, source_target_pairs={{0,1},{1,0},{2,3},{3,2},{4,5},{5,4},{6,7},{7,6},{8,9},{9,8},{10,11... | collective-permute-start | bytes 786440 | tf_op jit(solution)/shard_map/ppermute | solution.py:505
  105.4 31.5 %collective-permute-start.5 = (f32[256,256]{1,0:T(8,128)S(1)}, f32[256,256]{1,0:T(8,128)S(1)}, u32[]{:S(2)}, u32[]{:S(2)}) collective-permute-start(f32[256,256]{1,0:T(8,128)S(1)} %get-tuple-element.53), channel_id=1, source_target_pairs={{1,2},{2,1},{3,4},{4,3},{5,6},{6,5},{7,8},{8,7},{9,10},{10,9},{11,... | collective-permute-start | bytes 786440 | tf_op jit(solution)/shard_map/ppermute | solution.py:506
  127.8 13.7 %all-to-all-start.6 = ((f32[8,1,128]{2,1,0:T(1,128)}), f32[8,1,128]{2,1,0:T(1,128)S(1)}, u32[]{:S(2)}, u32[]{:S(2)}) async-start(f32[8,1,128]{2,1,0:T(1,128)} %shard_map.124), calls=%async_computation.6 | async-start | bytes 8192 | tf_op jit(solution)/shard_map/all_to_all | solution.py:500

commit v6 on v5

--- a/solution.py
+++ b/solution.py
@@ -27,13 +27,13 @@
     return pltpu.with_memory_space_constraint(array, pltpu.MemorySpace.HBM)
 
 
-def call(kernel, out_shape, work, scalars=(), arrays=(), far=(), free=(), scratch=(), aliases=None, room=2, result=VMEM):
+def call(kernel, out_shape, work, scalars=(), arrays=(), far=(), free=(), scratch=(), aliases=None, room=2):
     flops, moved = work
     return pl.pallas_call(
         kernel,
         out_shape=out_shape,
         in_specs=[spec(SMEM)] * len(scalars) + [spec(VMEM)] * len(arrays) + [spec(HBM)] * len(far) + [spec(pl.ANY)] * len(free),
-        out_specs=jax.tree.map(lambda _: spec(result), out_shape),
+        out_specs=jax.tree.map(lambda o: spec(HBM if o.memory_space == HBM else VMEM), out_shape),
         scratch_shapes=list(scratch),
         input_output_aliases=aliases or {},
         cost_estimate=pl.CostEstimate(flops=flops, bytes_accessed=moved, transcendentals=0),
@@ -74,6 +74,7 @@
     rec_any,
     emit_any,
     delays_any,
+    green_any,
     out_ref,
     even_ref,
     odd_ref,
@@ -81,6 +82,7 @@
     emit_ref,
     own_ref,
     delay_ref,
+    green_ref,
     field_ref,
     rows_ref,
     past_ref,
@@ -89,10 +91,10 @@
     sems,
 ):
     pairs = [(rec_any, cell_smem), (delays_any, delays), (field_any, field_ref), (past_any, past_ref)]
-    started = copies(pairs + [(rec_any, rec_ref), (emit_any, emit_ref)], sems)
+    started = copies(pairs + [(rec_any, rec_ref), (emit_any, emit_ref), (green_any, green_ref)], sems)
     own = lax.broadcasted_iota(jnp.int32, (8, 128), 0) == rank[0]
     own_ref[...] = jnp.where(own, 1.0, 0.0)
-    for copy in started:
+    for copy in started[:-1]:
         copy.wait()
     delay_ref[...] = jnp.full((8, 128), delays[rank[0]], jnp.int32)
     sample = gather_row(field_ref, cell_smem, rec_ref[...], rows_ref)
@@ -106,6 +108,7 @@
     for ref in (even_ref, odd_ref):
         ref[256:264, 0:128] = cells
         ref[256:264, 128:256] = cells
+    started[-1].wait()
 
 
 def edges(odd_brick, field_ref, even_ref, odd_ref):
@@ -113,22 +116,31 @@
     odd_ref[0:256, :] = field_ref[pl.ds(pl.multiple_of(768 * odd_brick[0], 256), 256), :]
 
 
-def first_message(rank, odd_brick, delays, rec_cell, emit_cell, past, field):
+def first_message(rank, odd_brick, delays, rec_cell, emit_cell, past, field, green):
     plane = VMEM((264, 256), f32)
     row = VMEM((1, 128), jnp.int32)
     return call(
         first_kernel,
-        (VMEM((8, 16, 128), f32), plane, plane, row, row, VMEM((8, 128), f32), VMEM((8, 128), jnp.int32)),
+        (
+            VMEM((8, 16, 128), f32),
+            plane,
+            plane,
+            row,
+            row,
+            VMEM((8, 128), f32),
+            VMEM((8, 128), jnp.int32),
+            VMEM((4096, 128), jnp.bfloat16),
+        ),
         (1 << 20, 1 << 19),
         scalars=[rank, odd_brick],
-        far=[field, past, rec_cell, emit_cell, delays],
+        far=[field, past, rec_cell, emit_cell, delays, green],
         scratch=[
             VMEM((1024, 256), f32),
             VMEM((128, 256), f32),
             VMEM((8, 128), jnp.bfloat16),
             SMEM((1, 128), jnp.int32),
             SMEM((8,), jnp.int32),
-            DMA((6,)),
+            DMA((7,)),
         ],
         room=3,
     )
@@ -166,20 +178,19 @@
 
 def multiply(chosen, right_ref, out_ref):
     product = jnp.dot(chosen.astype(jnp.bfloat16), right_ref[...], preferred_element_type=f32)
-    wide = out_ref.shape[1] == 24
+    if out_ref.shape[0] == 256:
+        for b in range(32):
+            out_ref[pl.ds(b, 8, stride=32), :] = product[:, b * 128 : (b + 1) * 128]
+        return
     for b in range(32):
         block = product[:, b * 128 : (b + 1) * 128]
-        if not wide:
-            out_ref[b] = block
-            continue
         out_ref[b, 8:16, :] = block
         if b < 31:
             out_ref[b + 1, 0:8, :] = block
         if b > 0:
             out_ref[b - 1, 16:24, :] = block
-    if wide:
-        out_ref[0, 0:8, :] = jnp.zeros((8, 128), f32)
-        out_ref[31, 16:24, :] = jnp.zeros((8, 128), f32)
+    out_ref[0, 0:8, :] = jnp.zeros((8, 128), f32)
+    out_ref[31, 16:24, :] = jnp.zeros((8, 128), f32)
 
 
 def old_samples(first_ref, where):
@@ -233,7 +244,7 @@
 def samples_and_emission(moment, message, first, old, delay, own, newer, right):
     return call(
         functools.partial(samples_kernel, moment),
-        (VMEM((32, 24 if moment == 1 else 8, 128), f32), VMEM((1, 128), f32), VMEM((8, 128), f32), VMEM((8, 128), f32)),
+        (VMEM((32, 24, 128) if moment == 1 else (256, 128), f32), VMEM((1, 128), f32), VMEM((8, 128), f32), VMEM((8, 128), f32)),
         (8 << 20, 1 << 20),
         arrays=[message, first, old, delay, own, *newer, right],
     )
@@ -253,23 +264,30 @@
     return (terms[2] + terms[1]) + terms[0]
 
 
-def stencil_kernel(take, inside, odd_brick, cell_smem, cell_vec, *refs):
-    if inside:
-        near_ref, near_cells_ref, *refs = refs
-    field_in, prev_any, diag_any, cross_any, even_any, odd_any, *refs = refs
-    *outs, rows_ref, field_ref, prev_ref, diag_ref, cross_ref, low_ref, high_ref, skew_ref, sum_ref, sems, edge_sems = refs
-    out_ref, *outs = outs
+def wave_kernel(step, odd_brick, rec_ref, *refs):
+    refs = list(refs)
+
+    def take(count):
+        taken = refs[:count]
+        del refs[:count]
+        return taken
+
+    emit_ref, mine_ref, near_ref, near_cells_ref = take(4) if step else [None] * 4
+    own_ref, start_ref, *sample_refs = take(4) if step == 2 else [None] * 4
+    rec_any, emit_any, field_any, prev_any, diag_any, cross_any, even_any, odd_any = take(8)
+    out_any, *outs = take(5 if step < 2 else 3)
+    field_ref, prev_ref, diag_ref, cross_ref, low_ref, high_ref, skew_ref, sum_ref = take(8)
+    rows_ref, rec_smem, emit_smem, sems, edge_sems, cell_sems, end_sems = take(7)
+    (out_ref,) = take(1) if step < 2 else [out_any]
     order = (1, 2, 0, 3)
 
     def part(x):
         return pl.ds(256 * x, 256)
 
+    listed = copies([(rec_any, rec_smem), (emit_any, emit_smem)], cell_sems)
     begun = {}
-    if inside:
-        field_ref = field_in
-    else:
-        for x in (0, 1, 2, 3):
-            begun[x] = copies([(field_in.at[part(x)], field_ref.at[part(x)])], sems.at[x, pl.ds(7, 1)])
+    for x in (0, 1, 2, 3):
+        begun[x] = copies([(field_any.at[part(x)], field_ref.at[part(x)])], sems.at[x, pl.ds(7, 1)])
     started = {}
     for x in order:
         pairs = [(diag_any.at[k, x], diag_ref.at[k, x]) for k in range(3)]
@@ -283,6 +301,21 @@
     @pl.when(odd_brick[0] == 1)
     def _():
         copies([(even_any, low_ref), (odd_any, high_ref)], edge_sems)
+
+    ending = []
+    for copy in listed:
+        copy.wait()
+    if step:
+        for x in (0, 1, 2, 3):
+            begun.pop(x)[0].wait()
+        add_at(emit_smem, emit_ref, mine_ref[...], field_ref, rows_ref)
+        ending += copies([(field_ref, outs[-1])], end_sems.at[pl.ds(4, 1)])
+    if step == 2:
+        own = own_ref[...] > 0.5
+        start = jnp.concatenate([start_ref[s, 8:9, :] for s in range(8)], axis=0)
+        series = [start] + [s[...] for s in sample_refs]
+        series = [jnp.sum(jnp.where(own, s, 0.0), axis=0, keepdims=True) for s in series]
+        outs[0][...] = jnp.concatenate(series, axis=0).astype(jnp.bfloat16)
 
     lane = lax.broadcasted_iota(jnp.int32, (8, 128), 1)
     sub = lax.broadcasted_iota(jnp.int32, (8, 128), 0)
@@ -331,12 +364,12 @@
         if x == 0:
             for k in (0, 1):
                 pltpu.make_async_copy(odd_any, low_ref, edge_sems.at[k]).wait()
-            if inside:
+            if step:
                 low_ref[...] = low_ref[...] + spots(near_ref[1:2, :], near_cells_ref[0:1, :], 3)
                 high_ref[...] = high_ref[...] + spots(near_ref[2:3, :], near_cells_ref[1:2, :], 0)
             else:
-                outs[-1][0:1, :] = low_ref[256:257, 0:128]
-                outs[-1][1:2, :] = high_ref[256:257, 0:128]
+                outs[3][0:1, :] = low_ref[256:257, 0:128]
+                outs[3][1:2, :] = high_ref[256:257, 0:128]
         for k in ready[x]:
             for copy in begun.get(k, ()):
                 copy.wait()
@@ -387,34 +420,44 @@
                 mixed = c0 * skew_xy[h] + c1 * skew_xz[h] + c2 * skew_yz[h]
                 values.append((twice - prev[h]) + (second + 0.5 * mixed))
             put(out_ref, 256 * x + row, values)
-    if take:
-        edges(odd_brick, out_ref, outs[1], outs[2])
-        outs[0][...] = gather_row(out_ref, cell_smem, cell_vec[...], rows_ref)
-
-
-def stencil(take, odd_brick, rec_cell, rec, field, prev, diag, cross, even, odd, near=()):
-    plane = VMEM((256, 256), f32)
-    inside = bool(near)
-    out_shape = [VMEM((1024, 256), f32)]
-    if take:
-        out_shape += [VMEM((1, 128), f32), plane, plane]
-    if not inside:
-        out_shape.append(VMEM((8, 128), f32))
+        if step < 2:
+            ending += copies([(out_ref.at[part(x)], out_any.at[part(x)])], end_sems.at[pl.ds(x, 1)])
+    if step < 2:
+        value_ref, even_out, odd_out = outs[:3]
+        even = out_ref.at[pl.ds(pl.multiple_of(768 - 768 * odd_brick[0], 256), 256)]
+        odd = out_ref.at[pl.ds(pl.multiple_of(768 * odd_brick[0], 256), 256)]
+        ending += copies([(even, even_out), (odd, odd_out)], end_sems.at[pl.ds(5, 2)])
+        value_ref[...] = gather_row(out_ref, rec_smem, rec_ref[...], rows_ref)
+    for copy in ending:
+        copy.wait()
+
+
+def wave(step, odd_brick, rec, cells, field, prev, diag, cross, edge_planes, added=(), record=()):
+    whole = (1024, 256)
+    out_shape = [HBM(whole, f32), VMEM((1, 128), f32), HBM((256, 256), f32), HBM((256, 256), f32)]
+    if step == 0:
+        out_shape += [VMEM((8, 128), f32)]
+    elif step == 1:
+        out_shape += [HBM(whole, f32)]
+    else:
+        out_shape = [VMEM(whole, f32), VMEM((3, 128), jnp.bfloat16), HBM(whole, f32)]
     coef = VMEM((3, 4, 256, 256), f32)
-    whole = VMEM((1024, 256), f32)
-    edge = VMEM(even.shape, f32)
-    scratch = [VMEM((128, 256), f32), VMEM((8, 128), f32) if inside else whole, whole, coef, coef, edge, edge]
-    scratch += [VMEM((1536, 256), f32), whole, DMA((4, 8)), DMA((2,))]
+    edge = VMEM(edge_planes[0].shape, f32)
+    listed = SMEM((1, 128), jnp.int32)
+    scratch = [VMEM(whole, f32), VMEM(whole, f32), coef, coef, edge, edge, VMEM((1536, 256), f32), VMEM(whole, f32)]
+    scratch += [VMEM((128, 256), f32), listed, listed, DMA((4, 8)), DMA((2,)), DMA((2,)), DMA((7,))]
+    if step < 2:
+        scratch.append(VMEM(whole, f32))
     return call(
-        functools.partial(stencil_kernel, take, inside),
+        functools.partial(wave_kernel, step),
         tuple(out_shape),
         (16 << 20, 10 << 20),
-        scalars=[odd_brick, rec_cell],
-        arrays=[rec, *near] + [field] * inside,
-        far=[field] * (not inside) + [prev, diag, cross] + [even, odd] * (inside and take),
-        free=[even, odd] * (not inside or not take),
+        scalars=[odd_brick],
+        arrays=[rec, *added, *record],
+        far=[*cells, field, prev, diag, cross],
+        free=edge_planes,
         scratch=scratch,
-        room=14,
+        room=16,
     )
 
 
@@ -425,39 +468,11 @@
         target_ref[pl.ds(row, 1), :] = target_ref[pl.ds(row, 1), :] + rows_ref[j : j + 1, :]
 
 
-def scatter_kernel(cell_smem, cell_vec, mine_ref, field_ref, *refs):
-    *refs, rows_ref = refs
-    del field_ref
-    old = refs[:-2]
-    add_at(cell_smem, cell_vec, mine_ref[...], refs[-2] if old else refs[-1], rows_ref)
-    if old:
-        own_ref, first_ref, *sample_refs = old
-        own = own_ref[...] > 0.5
-        start = jnp.concatenate([first_ref[s, 8:9, :] for s in range(8)], axis=0)
-        series = [start] + [s[...] for s in sample_refs]
-        series = [jnp.sum(jnp.where(own, s, 0.0), axis=0, keepdims=True) for s in series]
-        refs[-1][...] = jnp.concatenate(series, axis=0).astype(jnp.bfloat16)
-
-
-def scatter(emit_cell, emit, mine, field, old=()):
-    outs = [VMEM((1024, 256), f32)]
-    if old:
-        outs.append(VMEM((3, 128), jnp.bfloat16))
-    return call(
-        scatter_kernel,
-        tuple(outs),
-        (1 << 20, 1 << 19),
-        scalars=[emit_cell],
-        arrays=[emit, mine, field, *old],
-        scratch=[VMEM((128, 256), f32)],
-        aliases={3: 0},
-    )
-
-
 def last_kernel(cell_smem, cell_vec, parts_ref, field_ref, out_any, rows_ref, sem):
-    value = parts_ref[0]
-    for lag in range(1, 8):
-        value = value + parts_ref[lag]
+    sums = [parts_ref[8 * k : 8 * k + 8, :] for k in range(4)]
+    for k in range(4, 32):
+        sums[k % 4] = sums[k % 4] + parts_ref[8 * k : 8 * k + 8, :]
+    value = jnp.sum((sums[0] + sums[1]) + (sums[2] + sums[3]), axis=0, keepdims=True)
     add_at(cell_smem, cell_vec, value, field_ref, rows_ref)
     copy = pltpu.make_async_copy(field_ref, out_any, sem)
     copy.start()
@@ -467,33 +482,28 @@
 def last_scatter(emit_cell, emit, parts, field):
     return call(
         last_kernel,
-        jax.ShapeDtypeStruct((1024, 256), f32),
+        HBM((1024, 256), f32),
         (1 << 20, 2 << 20),
         scalars=[emit_cell],
         arrays=[emit, parts, field],
         scratch=[VMEM((128, 256), f32), DMA],
-        result=HBM,
-    )
-
-
-def spread_kernel(parts_ref, *refs):
-    *value_refs, out_ref = refs
+    )
+
+
+def spread_kernel(parts_ref, value_ref, out_ref):
     sums = [parts_ref[b] for b in range(4)]
     for b in range(4, 32):
         sums[b % 4] = sums[b % 4] + parts_ref[b]
     total = (sums[0] + sums[1]) + (sums[2] + sums[3])
     for s in range(8):
-        if not value_refs:
-            out_ref[s] = total[s : s + 1, :]
-            continue
         out_ref[s, 0:8, :] = total[8:16]
-        rows = [value_refs[0][...], total[s : s + 1], total[16 + s : 17 + s], jnp.zeros((5, 128), f32)]
+        rows = [value_ref[...], total[s : s + 1], total[16 + s : 17 + s], jnp.zeros((5, 128), f32)]
         out_ref[s, 8:16, :] = jnp.concatenate(rows, axis=0)
 
 
-def spread(parts, *value):
-    out = VMEM((8, 16 if value else 1, 128), f32)
-    return call(spread_kernel, out, (1 << 15, 1 << 17), arrays=[parts, *value])
+def spread(parts, value):
+    out = VMEM((8, 16, 128), f32)
+    return call(spread_kernel, out, (1 << 15, 1 << 17), arrays=[parts, value])
 
 
 def exchange(array, axis):
@@ -514,11 +524,14 @@
 
     current = field_now.reshape(1024, 256)
     before = field_prev.reshape(1024, 256)
-    message, *planes, rec, emit, own, delay = first_message(rank, odd_brick, delays, rec_cell, emit_cell, past, current)
+    message, *planes, rec, emit, own, delay, green = first_message(
+        rank, odd_brick, delays, rec_cell, emit_cell, past, current, green[0]
+    )
     first = exchange(message, "shot")
     even, odd = halos(*planes)
-    right = turn(green[0])
-    following, value, *planes, cells = stencil(True, odd_brick, rec_cell, rec, current, before, diag, cross, even, odd)
+    right = turn(green)
+    cells = (rec_cell, emit_cell)
+    following, value, *planes, near_cells = wave(0, odd_brick, rec, cells, current, before, diag, cross, (even, odd))
     partial = emission_start(first, delay, right)
     parts = exchange(partial, "brick")
     old = older(first, delay)
@@ -528,23 +541,22 @@
     even, odd = halos(*planes)
     partial, mine, near, sample1 = samples_and_emission(1, answer, first, old, delay, own, [], right)
     parts = exchange(partial, "brick")
+    added = (emit, mine, near, near_cells)
     earlier = current
-    (current,) = scatter(emit_cell, emit, mine, following)
-    following, value, *planes = stencil(
-        True, odd_brick, rec_cell, rec, current, earlier, diag, cross, even, odd, (near, cells)
+    following, value, *planes, current = wave(
+        1, odd_brick, rec, cells, following, earlier, diag, cross, (even, odd), added
     )
     message = spread(parts, value)
 
     answer = exchange(message, "shot")
     even, odd = halos(*planes)
     partial, mine, near, sample2 = samples_and_emission(2, answer, first, old, delay, own, [sample1], right)
-    parts = exchange(partial, "brick")
+    parts = exchange(partial.reshape(256, 1, 128), ("shot", "brick")).reshape(256, 128)
+    added = (emit, mine, near, near_cells)
+    record = (own, first, sample1, sample2)
     earlier = current
-    current, recorded = scatter(emit_cell, emit, mine, following, (own, first, sample1, sample2))
-    message = spread(parts)
-    parts = exchange(message, "shot")
-    (following,) = stencil(
-        False, odd_brick, rec_cell, rec, current, earlier, diag, cross, even, odd, (near, cells)
+    following, recorded, current = wave(
+        2, odd_brick, rec, cells, following, earlier, diag, cross, (even, odd), added, record
     )
     after = last_scatter(emit_cell, emit, parts, following)
     shape = field_now.shape

time: 144 us -> 136 us (0.944)
  blocking collectives: 19 us -> 0 us
  waiting for transfers between devices: 31.6 us -> 41.4 us
  starting transfers between devices: 58.8 us -> 66.8 us
  local copies, waits for them, and re-layouts: 5.69 us -> 0.57 us
  Pallas kernels: 27.7 us -> 25.8 us
    all_to_all x1 -> x0, blocking collectives: 19 us -> none  [exchange(): return lax.all_to_all(array, axis, 0, 0, tiled=True)]
    all_to_all x6, waiting for transfers between devices: 15.1 us -> 23.9 us  [exchange(): return lax.all_to_all(array, axis, 0, 0, tiled=True)]
    all_to_all x6, starting transfers between devices: 49.1 us -> 57.1 us  [exchange(): return lax.all_to_all(array, axis, 0, 0, tiled=True)]
    unnamed x20 -> x3, local copies, waits for them, and re-layouts: 5.69 us -> 0.57 us
    pallas_call x15 -> x12, Pallas kernels: 27.7 us -> 25.8 us  [call(): pl.pallas_call(kernel, out_shape=out_shape, in_specs=[spec(SMEM)] * len(s...]
  transfers between devices with their start and end apart: 12 -> 12, of which waited for: 5 -> 6; matrix products, arithmetic and copies ran while one was open for 1% -> 0% of each run, Pallas kernels for 13% -> 13%
where the time goes in v6:
time: 136 us
  starting transfers between devices  66.8 us (49%)
  waiting for transfers between devices  41.4 us (30%)
  Pallas kernels  25.8 us (19%)
    all_to_all x6, starting transfers between devices, exchange(): return lax.all_to_all(array, axis, 0, 0, tiled=True)  57.1 us
    pallas_call x12, Pallas kernels, call(): pl.pallas_call(kernel, out_shape=out_shape, in_specs=[spec(SMEM)] * len(s...  25.8 us
    all_to_all x6, waiting for transfers between devices, exchange(): return lax.all_to_all(array, axis, 0, 0, tiled=True)  23.9 us
    ppermute x3, waiting for transfers between devices, halos(): even = lax.ppermute(even_plane, 'brick', [(i, i ^ 1) for i in range(size)])  17.5 us
    ppermute x3, starting transfers between devices, halos(): even = lax.ppermute(even_plane, 'brick', [(i, i ^ 1) for i in range(size)])  7.74 us
  transfers between devices with their start and end apart: 12, of which 6 were waited for; matrix products, arithmetic and copies ran while one was open for 0% of the time, Pallas kernels for 13%

profile of v6, /device:TPU:1, one launch (start us, length us, event | category | flops | bytes accessed | tf_op | source)
XLA Modules:
  0.0 135.6 jit_solution(13740969409456136574)
XLA Ops:
  0.6 2.3 %shard_map.112 = (f32[8,16,128]{2,1,0:T(8,128)}, f32[264,256]{1,0:T(8,128)S(1)}, f32[264,256]{1,0:T(8,128)S(1)}, s32[1,128]{1,0:T(1,128)S(1)}, s32[1,128]{1,0:T(...) custom-call(s32[1]{0:T(128)} %bitcast.1.rank, s32[1]{0:T(128)} %bitcast.odd_brick, ...), custom_call_target="tpu_custom_call" | custom-call | flops 1048576 | bytes 524288 | tf_op jit(solution)/shard_map/pallas_call | solution.py:32
  2.9 10.0 %all-to-all-start = ((f32[8,16,128]{2,1,0:T(8,128)}), f32[8,16,128]{2,1,0:T(8,128)S(1)}, u32[]{:S(2)}, u32[]{:S(2)}) async-start(f32[8,16,128]{2,1,0:T(8,128)} %get-tuple-element.34), calls=%async_computation | async-start | bytes 131072 | tf_op jit(solution)/shard_map/all_to_all | solution.py:510
  12.9 0.3 shard_map.113.right_ref.refs_0_.refs_1_
  13.2 7.2 %all-to-all-done.first_ref.refs_5_ = f32[8,16,128]{2,1,0:T(8,128)S(1)} async-done(((f32[8,16,128]{2,1,0:T(8,128)}), f32[8,16,128]{2,1,0:T(8,128)S(1)}, u32[]{:S(2)}, u32[]{:S(2)}) %all-to-all-start) | async-done | bytes 65568 | tf_op jit(solution)/shard_map/all_to_all | solution.py:510
  20.5 1.0 shard_map.114
  21.5 7.2 %all-to-all-start.1 = ((f32[32,24,128]{2,1,0:T(8,128)}), f32[32,24,128]{2,1,0:T(8,128)S(1)}, u32[]{:S(2)}, u32[]{:S(2)}) async-start(f32[32,24,128]{2,1,0:T(8,128)} %shard_map.114), calls=%async_computation.1 | async-start | bytes 786432 | tf_op jit(solution)/shard_map/all_to_all | solution.py:510
  28.7 1.3 collective-permute-start
  30.0 0.7 collective-permute-start.1
  30.7 8.8 %collective-permute-done.refs_6_ = f32[264,256]{1,0:T(8,128)S(1)} collective-permute-done((f32[264,256]{1,0:T(8,128)S(1)}, f32[264,256]{1,0:T(8,128)S(1)}, u32[]{:S(2)}, u32[]{:S(2)}) %collective-permute-start) | collective-permute-done | bytes 270368 | tf_op jit(solution)/shard_map/ppermute | solution.py:515
  39.5 0.0 collective-permute-done.1.refs_7_
  39.5 5.2 %shard_map.115 = (f32[1024,256]{1,0:T(8,128)}, f32[1,128]{1,0:T(1,128)S(1)}, f32[256,256]{1,0:T(8,128)}, f32[256,256]{1,0:T(8,128)}, f32[8,128]{1,0:T(8,128)S(1)}) custom-call(s32[1]{0:T(128)} %bitcast.odd_brick, s32[1,128]{1,0:T(1,128)S(1)} %get-tuple-element.32.rec_ref, s32[1,128]{1,0:T(1,128)} %refs_8_.3, s32[1,128]{1,0:T(1,128)} %cell_smem.1, ...), custom_call_target="tpu_custom_call" | custom-call | flops 16777216 | bytes 10485760 | tf_op jit(solution)/shard_map/pallas_call | solution.py:32
  44.7 0.0 all-to-all-done.1.parts_ref
  44.7 0.7 shard_map.116
  45.4 7.2 %all-to-all-start.2 = ((f32[8,16,128]{2,1,0:T(8,128)}), f32[8,16,128]{2,1,0:T(8,128)S(1)}, u32[]{:S(2)}, u32[]{:S(2)}) async-start(f32[8,16,128]{2,1,0:T(8,128)} %shard_map.116), calls=%async_computation.2 | async-start | bytes 131072 | tf_op jit(solution)/shard_map/all_to_all | solution.py:510
  52.7 7.4 %all-to-all-done.2.message_ref = f32[8,16,128]{2,1,0:T(8,128)S(1)} async-done(((f32[8,16,128]{2,1,0:T(8,128)}), f32[8,16,128]{2,1,0:T(8,128)S(1)}, u32[]{:S(2)}, u32[]{:S(2)}) %all-to-all-start.2) | async-done | bytes 65568 | tf_op jit(solution)/shard_map/all_to_all | solution.py:510
  60.1 1.3 shard_map.118
  61.4 11.3 %all-to-all-start.3 = ((f32[32,24,128]{2,1,0:T(8,128)}), f32[32,24,128]{2,1,0:T(8,128)S(1)}, u32[]{:S(2)}, u32[]{:S(2)}) async-start(f32[32,24,128]{2,1,0:T(8,128)} %get-tuple-element.41), calls=%async_computation.3 | async-start | bytes 786432 | tf_op jit(solution)/shard_map/all_to_all | solution.py:510
  72.7 1.3 collective-permute-start.2
  74.0 0.7 collective-permute-start.3
  74.7 8.7 %collective-permute-done.2.refs_10_ = f32[256,256]{1,0:T(8,128)S(1)} collective-permute-done((f32[256,256]{1,0:T(8,128)}, f32[256,256]{1,0:T(8,128)S(1)}, u32[]{:S(2)}, u32[]{:S(2)}) %collective-permute-start.2) | collective-permute-done | bytes 262176 | tf_op jit(solution)/shard_map/ppermute | solution.py:515
  83.4 0.0 collective-permute-done.3.refs_11_
  83.4 6.2 %shard_map.119 = (f32[1024,256]{1,0:T(8,128)}, f32[1,128]{1,0:T(1,128)S(1)}, f32[256,256]{1,0:T(8,128)}, f32[256,256]{1,0:T(8,128)}, f32[1024,256]{1,0:T(8,128)}) custom-call(s32[1]{0:T(128)} %bitcast.odd_brick, s32[1,128]{1,0:T(1,128)S(1)} %get-tuple-element.32.rec_ref, s32[1,128]{1,0:T(1,128)S(1)} %get-tuple-element.33.refs_0_.cell_vec, ...), custom_call_target="tpu_custom_call" | custom-call | flops 16777216 | bytes 10485760 | tf_op jit(solution)/shard_map/pallas_call | solution.py:32
  89.7 0.0 all-to-all-done.3.parts_ref
  89.7 0.7 shard_map.120
  90.3 7.0 %all-to-all-start.4 = ((f32[8,16,128]{2,1,0:T(8,128)}), f32[8,16,128]{2,1,0:T(8,128)S(1)}, u32[]{:S(2)}, u32[]{:S(2)}) async-start(f32[8,16,128]{2,1,0:T(8,128)} %shard_map.120), calls=%async_computation.4 | async-start | bytes 131072 | tf_op jit(solution)/shard_map/all_to_all | solution.py:510
  97.4 5.1 %collective-permute-start.4 = (f32[256,256]{1,0:T(8,128)}, f32[256,256]{1,0:T(8,128)S(1)}, u32[]{:S(2)}, u32[]{:S(2)}) collective-permute-start(f32[256,256]{1,0:T(8,128)} %get-tuple-element.55), channel_id=1, source_target_pairs={{0,1},{1,0},{2,3},{3,2},{4,5},{5,4},{6,7},{7,6},{8,9},{9,8},{10,11... | collective-permute-start | bytes 786440 | tf_op jit(solution)/shard_map/ppermute | solution.py:515
  102.5 0.7 collective-permute-start.5
  103.1 1.7 %all-to-all-done.4.message_ref = f32[8,16,128]{2,1,0:T(8,128)S(1)} async-done(((f32[8,16,128]{2,1,0:T(8,128)}), f32[8,16,128]{2,1,0:T(8,128)S(1)}, u32[]{:S(2)}, u32[]{:S(2)}) %all-to-all-start.4) | async-done | bytes 65568 | tf_op jit(solution)/shard_map/all_to_all | solution.py:510
  104.8 1.2 shard_map.121
  106.0 14.3 %all-to-all-start.5 = ((f32[256,1,128]{2,1,0:T(1,128)}), f32[256,1,128]{2,1,0:T(1,128)S(1)}, u32[]{:S(2)}, u32[]{:S(2)}) async-start(f32[256,1,128]{2,1,0:T(1,128)} %bitcast.8), calls=%async_computation.5 | async-start | bytes 262144 | tf_op jit(solution)/shard_map/all_to_all | solution.py:510
  120.4 0.0 collective-permute-done.4.refs_14_
  120.4 0.0 collective-permute-done.5.refs_15_
  120.4 0.0 copy-start
  120.4 4.8 %shard_map.122 = (f32[1024,256]{1,0:T(8,128)S(1)}, bf16[3,128]{1,0:T(4,128)(2,1)S(1)}, f32[1024,256]{1,0:T(8,128)}) custom-call(s32[1]{0:T(128)} %bitcast.odd_brick, s32[1,128]{1,0:T(1,128)S(1)} %get-tuple-element.32.rec_ref, s32[1,128]{1,0:T(1,128)S(1)} %get-tuple-element.33.refs_0_.cell_vec, f32[1,128]{1,0:T(1,128)S(1)} %get-tuple-element.50.refs_1_, ...), custom_call_target="tpu_custom_call" | custom-call | flops 16777216 | bytes 10485760 | tf_op jit(solution)/shard_map/pallas_call | solution.py:32
  125.3 0.6 copy.13
  125.8 7.6 %all-to-all-done.5 = f32[256,1,128]{2,1,0:T(1,128)S(1)} async-done(((f32[256,1,128]{2,1,0:T(1,128)}), f32[256,1,128]{2,1,0:T(1,128)S(1)}, u32[]{:S(2)}, u32[]{:S(2)}) %all-to-all-start.5) | async-done | bytes 131104 | tf_op jit(solution)/shard_map/all_to_all | solution.py:510
  133.4 0.0 copy-done
  133.4 2.0 %shard_map.123 = f32[1024,256]{1,0:T(8,128)} custom-call(s32[1,128]{1,0:T(1,128)S(1)} %copy-done, s32[1,128]{1,0:T(1,128)S(1)} %get-tuple-element.33.refs_0_.cell_vec, f32[256,128]{1,0:T(8,128)S(1)} %bitcast.14, f32[1024,256]{1,0:T(8,128)S(1)} %get-tuple-element.59.field_ref), custom_call_target="tpu_custom_call" | custom-call | flops 1048576 | bytes 2097152 | tf_op jit(solution)/shard_map/pallas_call | solution.py:32
  (1 shorter events, 0.0 us)
Async XLA Ops:
  2.9 17.5 %all-to-all-start = ((f32[8,16,128]{2,1,0:T(8,128)}), f32[8,16,128]{2,1,0:T(8,128)S(1)}, u32[]{:S(2)}, u32[]{:S(2)}) async-start(f32[8,16,128]{2,1,0:T(8,128)} %get-tuple-element.34), calls=%async_computation | async-start | bytes 131072 | tf_op jit(solution)/shard_map/all_to_all | solution.py:510
  21.5 23.3 %all-to-all-start.1 = ((f32[32,24,128]{2,1,0:T(8,128)}), f32[32,24,128]{2,1,0:T(8,128)S(1)}, u32[]{:S(2)}, u32[]{:S(2)}) async-start(f32[32,24,128]{2,1,0:T(8,128)} %shard_map.114), calls=%async_computation.1 | async-start | bytes 786432 | tf_op jit(solution)/shard_map/all_to_all | solution.py:510
  28.7 10.8 %collective-permute-start = (f32[264,256]{1,0:T(8,128)S(1)}, f32[264,256]{1,0:T(8,128)S(1)}, u32[]{:S(2)}, u32[]{:S(2)}) collective-permute-start(f32[264,256]{1,0:T(8,128)S(1)} %get-tuple-element.37), channel_id=1, source_target_pairs={{0,1},{1,0},{2,3},{3,2},{4,5},{5,4},{6,7},{7,6},{8,9},{9,8},{10,11... | collective-permute-start | bytes 811016 | tf_op jit(solution)/shard_map/ppermute | solution.py:515
  30.0 9.5 %collective-permute-start.1 = (f32[264,256]{1,0:T(8,128)S(1)}, f32[264,256]{1,0:T(8,128)S(1)}, u32[]{:S(2)}, u32[]{:S(2)}) collective-permute-start(f32[264,256]{1,0:T(8,128)S(1)} %get-tuple-element.38), channel_id=1, source_target_pairs={{1,2},{2,1},{3,4},{4,3},{5,6},{6,5},{7,8},{8,7},{9,10},{10,9},{11,... | collective-permute-start | bytes 811016 | tf_op jit(solution)/shard_map/ppermute | solution.py:516
  45.4 14.7 %all-to-all-start.2 = ((f32[8,16,128]{2,1,0:T(8,128)}), f32[8,16,128]{2,1,0:T(8,128)S(1)}, u32[]{:S(2)}, u32[]{:S(2)}) async-start(f32[8,16,128]{2,1,0:T(8,128)} %shard_map.116), calls=%async_computation.2 | async-start | bytes 131072 | tf_op jit(solution)/shard_map/all_to_all | solution.py:510
  61.4 28.3 %all-to-all-start.3 = ((f32[32,24,128]{2,1,0:T(8,128)}), f32[32,24,128]{2,1,0:T(8,128)S(1)}, u32[]{:S(2)}, u32[]{:S(2)}) async-start(f32[32,24,128]{2,1,0:T(8,128)} %get-tuple-element.41), calls=%async_computation.3 | async-start | bytes 786432 | tf_op jit(solution)/shard_map/all_to_all | solution.py:510
  72.7 10.7 %collective-permute-start.2 = (f32[256,256]{1,0:T(8,128)}, f32[256,256]{1,0:T(8,128)S(1)}, u32[]{:S(2)}, u32[]{:S(2)}) collective-permute-start(f32[256,256]{1,0:T(8,128)} %get-tuple-element.46), channel_id=1, source_target_pairs={{0,1},{1,0},{2,3},{3,2},{4,5},{5,4},{6,7},{7,6},{8,9},{9,8},{10,11... | collective-permute-start | bytes 786440 | tf_op jit(solution)/shard_map/ppermute | solution.py:515
  74.0 9.4 %collective-permute-start.3 = (f32[256,256]{1,0:T(8,128)}, f32[256,256]{1,0:T(8,128)S(1)}, u32[]{:S(2)}, u32[]{:S(2)}) collective-permute-start(f32[256,256]{1,0:T(8,128)} %get-tuple-element.47), channel_id=1, source_target_pairs={{1,2},{2,1},{3,4},{4,3},{5,6},{6,5},{7,8},{8,7},{9,10},{10,9},{11,... | collective-permute-start | bytes 786440 | tf_op jit(solution)/shard_map/ppermute | solution.py:516
  90.3 14.5 %all-to-all-start.4 = ((f32[8,16,128]{2,1,0:T(8,128)}), f32[8,16,128]{2,1,0:T(8,128)S(1)}, u32[]{:S(2)}, u32[]{:S(2)}) async-start(f32[8,16,128]{2,1,0:T(8,128)} %shard_map.120), calls=%async_computation.4 | async-start | bytes 131072 | tf_op jit(solution)/shard_map/all_to_all | solution.py:510
  97.4 23.0 %collective-permute-start.4 = (f32[256,256]{1,0:T(8,128)}, f32[256,256]{1,0:T(8,128)S(1)}, u32[]{:S(2)}, u32[]{:S(2)}) collective-permute-start(f32[256,256]{1,0:T(8,128)} %get-tuple-element.55), channel_id=1, source_target_pairs={{0,1},{1,0},{2,3},{3,2},{4,5},{5,4},{6,7},{7,6},{8,9},{9,8},{10,11... | collective-permute-start | bytes 786440 | tf_op jit(solution)/shard_map/ppermute | solution.py:515
  102.5 17.9 %collective-permute-start.5 = (f32[256,256]{1,0:T(8,128)}, f32[256,256]{1,0:T(8,128)S(1)}, u32[]{:S(2)}, u32[]{:S(2)}) collective-permute-start(f32[256,256]{1,0:T(8,128)} %get-tuple-element.56), channel_id=1, source_target_pairs={{1,2},{2,1},{3,4},{4,3},{5,6},{6,5},{7,8},{8,7},{9,10},{10,9},{11,... | collective-permute-start | bytes 786440 | tf_op jit(solution)/shard_map/ppermute | solution.py:516
  106.0 27.3 %all-to-all-start.5 = ((f32[256,1,128]{2,1,0:T(1,128)}), f32[256,1,128]{2,1,0:T(1,128)S(1)}, u32[]{:S(2)}, u32[]{:S(2)}) async-start(f32[256,1,128]{2,1,0:T(1,128)} %bitcast.8), calls=%async_computation.5 | async-start | bytes 262144 | tf_op jit(solution)/shard_map/all_to_all | solution.py:510
  120.4 13.0 %copy-start = (s32[1,128]{1,0:T(1,128)S(1)}, s32[1,128]{1,0:T(1,128)}, u32[]{:S(2)}) copy-start(s32[1,128]{1,0:T(1,128)} %cell_smem.1) | copy-start | bytes 1540

commit v7 on v6

--- a/solution.py
+++ b/solution.py
@@ -264,6 +264,10 @@
     return (terms[2] + terms[1]) + terms[0]
 
 
+def base(x):
+    return 8 + 264 * (x + 1)
+
+
 def wave_kernel(step, odd_brick, rec_ref, *refs):
     refs = list(refs)
 
@@ -276,40 +280,68 @@
     own_ref, start_ref, *sample_refs = take(4) if step == 2 else [None] * 4
     rec_any, emit_any, field_any, prev_any, diag_any, cross_any, even_any, odd_any = take(8)
     out_any, *outs = take(5 if step < 2 else 3)
-    field_ref, prev_ref, diag_ref, cross_ref, low_ref, high_ref, skew_ref, sum_ref = take(8)
-    rows_ref, rec_smem, emit_smem, sems, edge_sems, cell_sems, end_sems = take(7)
+    left_ref, right_ref, prev_ref, diag_ref, cross_ref, left_skew, right_skew, left_sum, right_sum = take(9)
+    rows_ref, cells_ref, rec_smem, emit_smem, sems, edge_sems, cell_sems, end_sems = take(8)
     (out_ref,) = take(1) if step < 2 else [out_any]
     order = (1, 2, 0, 3)
+    fields, skews, sums = (left_ref, right_ref), (left_skew, right_skew), (left_sum, right_sum)
 
     def part(x):
         return pl.ds(256 * x, 256)
+
+    def lanes(h):
+        return pl.ds(128 * h, 128)
+
+    def plane(h, x):
+        return fields[h].at[pl.ds(base(x), 256)]
 
     listed = copies([(rec_any, rec_smem), (emit_any, emit_smem)], cell_sems)
     begun = {}
     for x in (0, 1, 2, 3):
-        begun[x] = copies([(field_any.at[part(x)], field_ref.at[part(x)])], sems.at[x, pl.ds(7, 1)])
+        begun[x] = copies([(field_any.at[part(x), lanes(h)], plane(h, x)) for h in (0, 1)], sems.at[x, pl.ds(7, 2)])
     started = {}
     for x in order:
         pairs = [(diag_any.at[k, x], diag_ref.at[k, x]) for k in range(3)]
         pairs += [(cross_any.at[k, x], cross_ref.at[k, x]) for k in range(3)]
         started[x] = copies([(prev_any.at[part(x)], prev_ref.at[part(x)])] + pairs, sems.at[x])
 
+    def bring(low, high):
+        pairs = [(low.at[pl.ds(0, 256), lanes(h)], plane(h, -1)) for h in (0, 1)]
+        pairs += [(high.at[pl.ds(0, 256), lanes(h)], plane(h, 4)) for h in (0, 1)]
+        if step == 0:
+            pairs += [(low.at[pl.ds(256, 8), lanes(0)], cells_ref.at[pl.ds(0, 8)])]
+            pairs += [(high.at[pl.ds(256, 8), lanes(0)], cells_ref.at[pl.ds(8, 8)])]
+        return [pltpu.make_async_copy(a, b, edge_sems.at[k]) for k, (a, b) in enumerate(pairs)]
+
     @pl.when(odd_brick[0] == 0)
     def _():
-        copies([(even_any, high_ref), (odd_any, low_ref)], edge_sems)
+        for copy in bring(odd_any, even_any):
+            copy.start()
 
     @pl.when(odd_brick[0] == 1)
     def _():
-        copies([(even_any, low_ref), (odd_any, high_ref)], edge_sems)
-
+        for copy in bring(even_any, odd_any):
+            copy.start()
+
+    for ref in fields + skews:
+        for x in range(-2, 5):
+            ref[base(x) + 256 : base(x) + 264, :] = jnp.zeros((8, 128), f32)
     ending = []
     for copy in listed:
         copy.wait()
     if step:
         for x in (0, 1, 2, 3):
-            begun.pop(x)[0].wait()
-        add_at(emit_smem, emit_ref, mine_ref[...], field_ref, rows_ref)
-        ending += copies([(field_ref, outs[-1])], end_sems.at[pl.ds(4, 1)])
+            for copy in begun.pop(x):
+                copy.wait()
+        rows_ref[...] = jnp.where(lanes_of(emit_ref[...]), sheet_of(mine_ref[...], 256), 0.0)
+        for j in range(128):
+            cell = emit_smem[0, j]
+            row = (cell >> 8) + 8 * (cell >> 16) + base(0)
+            for h in (0, 1):
+                spot = (pl.ds(row, 1), slice(None))
+                fields[h][spot] = fields[h][spot] + rows_ref[j : j + 1, 128 * h : 128 * h + 128]
+        pairs = [(plane(h, x), outs[-1].at[part(x), lanes(h)]) for x in (0, 1, 2, 3) for h in (0, 1)]
+        ending += copies(pairs, end_sems.at[pl.ds(6, 8)])
     if step == 2:
         own = own_ref[...] > 0.5
         start = jnp.concatenate([start_ref[s, 8:9, :] for s in range(8)], axis=0)
@@ -318,115 +350,72 @@
         outs[0][...] = jnp.concatenate(series, axis=0).astype(jnp.bfloat16)
 
     lane = lax.broadcasted_iota(jnp.int32, (8, 128), 1)
-    sub = lax.broadcasted_iota(jnp.int32, (8, 128), 0)
-    zero = jnp.zeros((8, 128), f32)
     first_lane, last_lane = lane == 0, lane == 127
-    first_sub, last_sub = sub == 0, sub == 7
-
-    def at(ref, where, row):
-        rows = slice(row, row + 8)
-        return ref[(*where, rows, slice(0, 128))], ref[(*where, rows, slice(128, 256))]
-
-    def put(ref, row, pair):
-        for h in range(2):
-            ref[row : row + 8, 128 * h : 128 * h + 128] = pair[h]
-
-    def each(f, *pairs):
-        return tuple(f(*vs) for vs in zip(*pairs))
-
-    def plus(a, b):
-        return each(lambda v, w: v + w, a, b)
-
-    def minus(a, b):
-        return each(lambda v, w: v - w, a, b)
-
-    def source(x):
-        if x < 0:
-            return low_ref, 0
-        if x > 3:
-            return high_ref, 0
-        return field_ref, 256 * x
 
     def along_z(x):
-        ref, base = source(x)
         for t in range(32):
-            a, b = at(ref, (), base + 8 * t)
+            rows = slice(base(x) + 8 * t, base(x) + 8 * t + 8)
+            a, b = left_ref[rows, :], right_ref[rows, :]
             up_a, up_b = pltpu.roll(a, 127, 1), pltpu.roll(b, 127, 1)
             down_a, down_b = pltpu.roll(a, 1, 1), pltpu.roll(b, 1, 1)
             ahead = (jnp.where(last_lane, up_b, up_a), jnp.where(last_lane, 0.0, up_b))
             behind = (jnp.where(first_lane, 0.0, down_a), jnp.where(first_lane, down_a, down_b))
-            put(skew_ref, 256 * (x + 1) + 8 * t, minus(ahead, behind))
-            if 0 <= x < 4:
-                put(sum_ref, 256 * x + 8 * t, plus(ahead, behind))
+            for h in (0, 1):
+                skews[h][rows, :] = ahead[h] - behind[h]
+                if 0 <= x < 4:
+                    sums[h][256 * x + 8 * t : 256 * x + 8 * t + 8, :] = ahead[h] + behind[h]
 
     ready = {1: (0, 1, 2), 2: (3,), 0: (-1,), 3: (4,)}
     for x in order:
         if x == 0:
-            for k in (0, 1):
-                pltpu.make_async_copy(odd_any, low_ref, edge_sems.at[k]).wait()
+            for copy in bring(odd_any, even_any):
+                copy.wait()
             if step:
-                low_ref[...] = low_ref[...] + spots(near_ref[1:2, :], near_cells_ref[0:1, :], 3)
-                high_ref[...] = high_ref[...] + spots(near_ref[2:3, :], near_cells_ref[1:2, :], 0)
+                for side, plane_of, row in ((-1, 3, 0), (4, 0, 1)):
+                    extra = spots(near_ref[1 + row : 2 + row, :], near_cells_ref[row : row + 1, :], plane_of)
+                    rows = slice(base(side), base(side) + 256)
+                    for h in (0, 1):
+                        fields[h][rows, :] = fields[h][rows, :] + extra[:, 128 * h : 128 * h + 128]
             else:
-                outs[3][0:1, :] = low_ref[256:257, 0:128]
-                outs[3][1:2, :] = high_ref[256:257, 0:128]
+                outs[3][0:1, :] = cells_ref[0:1, :]
+                outs[3][1:2, :] = cells_ref[8:9, :]
         for k in ready[x]:
             for copy in begun.get(k, ()):
                 copy.wait()
             along_z(k)
         for copy in started[x]:
             copy.wait()
-
-        def turned(pair):
-            return tuple(pltpu.roll(v, 7, 0) for v in pair), tuple(pltpu.roll(v, 1, 0) for v in pair)
-
-        edge = ((zero, zero), (zero, zero))
-        tiles = {}
-        turns = {-1: (edge, edge, edge), 32: (edge, edge, edge)}
-
-        def fetch(t):
-            mid, ahead, behind = (at(ref, (), base + 8 * t) for ref, base in map(source, (x, x + 1, x - 1)))
-            slope = minus(ahead, behind)
-            skew = at(skew_ref, (), 256 * (x + 1) + 8 * t)
-            tiles[t] = mid, plus(ahead, behind)
-            turns[t] = turned(mid), turned(slope), turned(skew)
-
-        def after_y(t, k):
-            return each(lambda a, b: jnp.where(last_sub, b, a), turns[t][k][0], turns[t + 1][k][0])
-
-        def before_y(t, k):
-            return each(lambda a, b: jnp.where(first_sub, b, a), turns[t][k][1], turns[t - 1][k][1])
-
-        fetch(0)
         for t in range(32):
-            if t < 31:
-                fetch(t + 1)
-            row = 8 * t
-            mid, sum_x = tiles.pop(t)
-            sum_y = plus(after_y(t, 0), before_y(t, 0))
-            sum_z = at(sum_ref, (), 256 * x + row)
-            skew_xy = minus(after_y(t, 1), before_y(t, 1))
-            skew_xz = minus(at(skew_ref, (), 256 * (x + 2) + row), at(skew_ref, (), 256 * x + row))
-            skew_yz = minus(after_y(t, 2), before_y(t, 2))
-            diag = [at(diag_ref, (k, x), row) for k in range(3)]
-            cross = [at(cross_ref, (k, x), row) for k in range(3)]
-            prev = at(prev_ref, (), 256 * x + row)
-            values = []
-            for h in range(2):
-                d0, d1, d2 = (d[h] for d in diag)
-                c0, c1, c2 = (c[h] for c in cross)
-                twice = mid[h] + mid[h]
-                second = d0 * (sum_x[h] - twice) + d1 * (sum_y[h] - twice) + d2 * (sum_z[h] - twice)
-                mixed = c0 * skew_xy[h] + c1 * skew_xz[h] + c2 * skew_yz[h]
-                values.append((twice - prev[h]) + (second + 0.5 * mixed))
-            put(out_ref, 256 * x + row, values)
+            near, up, down = (base(k) + 8 * t for k in (x, x + 1, x - 1))
+            row = 256 * x + 8 * t
+            rows = slice(row, row + 8)
+            for h in (0, 1):
+                field, skew = fields[h], skews[h]
+
+                def at(ref, first):
+                    return ref[first : first + 8, :]
+
+                def across(ref, first):
+                    return at(ref, first + 1) - at(ref, first - 1)
+
+                columns = slice(128 * h, 128 * h + 128)
+                d0, d1, d2 = (diag_ref[k, x, 8 * t : 8 * t + 8, columns] for k in range(3))
+                c0, c1, c2 = (cross_ref[k, x, 8 * t : 8 * t + 8, columns] for k in range(3))
+                mid = at(field, near)
+                twice = mid + mid
+                second = d0 * ((at(field, up) + at(field, down)) - twice)
+                second = second + d1 * ((at(field, near + 1) + at(field, near - 1)) - twice)
+                second = second + d2 * (sums[h][rows, :] - twice)
+                mixed = c0 * (across(field, up) - across(field, down))
+                mixed = mixed + c1 * (at(skew, up) - at(skew, down)) + c2 * across(skew, near)
+                out_ref[rows, columns] = (twice - prev_ref[rows, columns]) + (second + 0.5 * mixed)
         if step < 2:
             ending += copies([(out_ref.at[part(x)], out_any.at[part(x)])], end_sems.at[pl.ds(x, 1)])
     if step < 2:
         value_ref, even_out, odd_out = outs[:3]
         even = out_ref.at[pl.ds(pl.multiple_of(768 - 768 * odd_brick[0], 256), 256)]
         odd = out_ref.at[pl.ds(pl.multiple_of(768 * odd_brick[0], 256), 256)]
-        ending += copies([(even, even_out), (odd, odd_out)], end_sems.at[pl.ds(5, 2)])
+        ending += copies([(even, even_out), (odd, odd_out)], end_sems.at[pl.ds(4, 2)])
         value_ref[...] = gather_row(out_ref, rec_smem, rec_ref[...], rows_ref)
     for copy in ending:
         copy.wait()
@@ -442,10 +431,12 @@
     else:
         out_shape = [VMEM(whole, f32), VMEM((3, 128), jnp.bfloat16), HBM(whole, f32)]
     coef = VMEM((3, 4, 256, 256), f32)
-    edge = VMEM(edge_planes[0].shape, f32)
+    half = VMEM((1592, 128), f32)
+    inner = VMEM((1024, 128), f32)
     listed = SMEM((1, 128), jnp.int32)
-    scratch = [VMEM(whole, f32), VMEM(whole, f32), coef, coef, edge, edge, VMEM((1536, 256), f32), VMEM(whole, f32)]
-    scratch += [VMEM((128, 256), f32), listed, listed, DMA((4, 8)), DMA((2,)), DMA((2,)), DMA((7,))]
+    scratch = [half, half, VMEM(whole, f32), coef, coef, half, half, inner, inner]
+    scratch += [VMEM((128, 256), f32), VMEM((16, 128), f32), listed, listed]
+    scratch += [DMA((4, 9)), DMA((6,)), DMA((2,)), DMA((14,))]
     if step < 2:
         scratch.append(VMEM(whole, f32))
     return call(

time: 136 us -> 136 us (level)
  no operation moved by 1% of the time
where the time goes in v7:
time: 136 us; the launch traced here: 135 us
  starting transfers between devices  66.8 us (49%)
  waiting for transfers between devices  41.2 us (30%)
  Pallas kernels  25.8 us (19%)
    all_to_all x6, starting transfers between devices, exchange(): return lax.all_to_all(array, axis, 0, 0, tiled=True)  57.1 us
    pallas_call x12, Pallas kernels, call(): pl.pallas_call(kernel, out_shape=out_shape, in_specs=[spec(SMEM)] * len(s...  25.8 us
    all_to_all x6, waiting for transfers between devices, exchange(): return lax.all_to_all(array, axis, 0, 0, tiled=True)  23.7 us
    ppermute x3, waiting for transfers between devices, halos(): even = lax.ppermute(even_plane, 'brick', [(i, i ^ 1) for i in range(size)])  17.5 us
    ppermute x3, starting transfers between devices, halos(): even = lax.ppermute(even_plane, 'brick', [(i, i ^ 1) for i in range(size)])  7.74 us
  transfers between devices with their start and end apart: 12, of which 6 were waited for; matrix products, arithmetic and copies ran while one was open for 0% of the time, Pallas kernels for 13%

profile of v7, /device:TPU:1, one launch (start us, length us, event | category | flops | bytes accessed | tf_op | source)
XLA Modules:
  0.0 135.4 jit_solution(16171275222340584064)
XLA Ops:
  0.6 2.3 %shard_map.112 = (f32[8,16,128]{2,1,0:T(8,128)}, f32[264,256]{1,0:T(8,128)S(1)}, f32[264,256]{1,0:T(8,128)S(1)}, s32[1,128]{1,0:T(1,128)S(1)}, s32[1,128]{1,0:T(...) custom-call(s32[1]{0:T(128)} %bitcast.1.rank, s32[1]{0:T(128)} %bitcast.odd_brick, ...), custom_call_target="tpu_custom_call" | custom-call | flops 1048576 | bytes 524288 | tf_op jit(solution)/shard_map/pallas_call | solution.py:32
  2.9 10.0 %all-to-all-start = ((f32[8,16,128]{2,1,0:T(8,128)}), f32[8,16,128]{2,1,0:T(8,128)S(1)}, u32[]{:S(2)}, u32[]{:S(2)}) async-start(f32[8,16,128]{2,1,0:T(8,128)} %get-tuple-element.34), calls=%async_computation | async-start | bytes 131072 | tf_op jit(solution)/shard_map/all_to_all | solution.py:501
  12.9 0.3 shard_map.113.right_ref.refs_0_.refs_1_
  13.2 7.2 %all-to-all-done.first_ref.refs_5_ = f32[8,16,128]{2,1,0:T(8,128)S(1)} async-done(((f32[8,16,128]{2,1,0:T(8,128)}), f32[8,16,128]{2,1,0:T(8,128)S(1)}, u32[]{:S(2)}, u32[]{:S(2)}) %all-to-all-start) | async-done | bytes 65568 | tf_op jit(solution)/shard_map/all_to_all | solution.py:501
  20.5 1.0 shard_map.114
  21.5 7.2 %all-to-all-start.1 = ((f32[32,24,128]{2,1,0:T(8,128)}), f32[32,24,128]{2,1,0:T(8,128)S(1)}, u32[]{:S(2)}, u32[]{:S(2)}) async-start(f32[32,24,128]{2,1,0:T(8,128)} %shard_map.114), calls=%async_computation.1 | async-start | bytes 786432 | tf_op jit(solution)/shard_map/all_to_all | solution.py:501
  28.7 1.3 collective-permute-start
  30.0 0.7 collective-permute-start.1
  30.7 8.8 %collective-permute-done.refs_6_ = f32[264,256]{1,0:T(8,128)S(1)} collective-permute-done((f32[264,256]{1,0:T(8,128)S(1)}, f32[264,256]{1,0:T(8,128)S(1)}, u32[]{:S(2)}, u32[]{:S(2)}) %collective-permute-start) | collective-permute-done | bytes 270368 | tf_op jit(solution)/shard_map/ppermute | solution.py:506
  39.5 0.0 collective-permute-done.1.refs_7_
  39.5 5.4 %shard_map.115 = (f32[1024,256]{1,0:T(8,128)}, f32[1,128]{1,0:T(1,128)S(1)}, f32[256,256]{1,0:T(8,128)}, f32[256,256]{1,0:T(8,128)}, f32[8,128]{1,0:T(8,128)S(1)}) custom-call(s32[1]{0:T(128)} %bitcast.odd_brick, s32[1,128]{1,0:T(1,128)S(1)} %get-tuple-element.32.rec_ref, s32[1,128]{1,0:T(1,128)} %refs_8_.3, s32[1,128]{1,0:T(1,128)} %cell_smem.1, ...), custom_call_target="tpu_custom_call" | custom-call | flops 16777216 | bytes 10485760 | tf_op jit(solution)/shard_map/pallas_call | solution.py:32
  44.9 0.0 all-to-all-done.1.parts_ref
  44.9 0.7 shard_map.116
  45.5 7.2 %all-to-all-start.2 = ((f32[8,16,128]{2,1,0:T(8,128)}), f32[8,16,128]{2,1,0:T(8,128)S(1)}, u32[]{:S(2)}, u32[]{:S(2)}) async-start(f32[8,16,128]{2,1,0:T(8,128)} %shard_map.116), calls=%async_computation.2 | async-start | bytes 131072 | tf_op jit(solution)/shard_map/all_to_all | solution.py:501
  52.8 7.4 %all-to-all-done.2.message_ref = f32[8,16,128]{2,1,0:T(8,128)S(1)} async-done(((f32[8,16,128]{2,1,0:T(8,128)}), f32[8,16,128]{2,1,0:T(8,128)S(1)}, u32[]{:S(2)}, u32[]{:S(2)}) %all-to-all-start.2) | async-done | bytes 65568 | tf_op jit(solution)/shard_map/all_to_all | solution.py:501
  60.2 1.3 shard_map.118
  61.5 11.3 %all-to-all-start.3 = ((f32[32,24,128]{2,1,0:T(8,128)}), f32[32,24,128]{2,1,0:T(8,128)S(1)}, u32[]{:S(2)}, u32[]{:S(2)}) async-start(f32[32,24,128]{2,1,0:T(8,128)} %get-tuple-element.41), calls=%async_computation.3 | async-start | bytes 786432 | tf_op jit(solution)/shard_map/all_to_all | solution.py:501
  72.8 1.3 collective-permute-start.2
  74.2 0.7 collective-permute-start.3
  74.8 8.7 %collective-permute-done.2.refs_10_ = f32[256,256]{1,0:T(8,128)S(1)} collective-permute-done((f32[256,256]{1,0:T(8,128)}, f32[256,256]{1,0:T(8,128)S(1)}, u32[]{:S(2)}, u32[]{:S(2)}) %collective-permute-start.2) | collective-permute-done | bytes 262176 | tf_op jit(solution)/shard_map/ppermute | solution.py:506
  83.6 0.0 collective-permute-done.3.refs_11_
  83.6 5.9 %shard_map.119 = (f32[1024,256]{1,0:T(8,128)}, f32[1,128]{1,0:T(1,128)S(1)}, f32[256,256]{1,0:T(8,128)}, f32[256,256]{1,0:T(8,128)}, f32[1024,256]{1,0:T(8,128)}) custom-call(s32[1]{0:T(128)} %bitcast.odd_brick, s32[1,128]{1,0:T(1,128)S(1)} %get-tuple-element.32.rec_ref, s32[1,128]{1,0:T(1,128)S(1)} %get-tuple-element.33.refs_0_.cell_vec, ...), custom_call_target="tpu_custom_call" | custom-call | flops 16777216 | bytes 10485760 | tf_op jit(solution)/shard_map/pallas_call | solution.py:32
  89.5 0.0 all-to-all-done.3.parts_ref
  89.5 0.7 shard_map.120
  90.2 7.0 %all-to-all-start.4 = ((f32[8,16,128]{2,1,0:T(8,128)}), f32[8,16,128]{2,1,0:T(8,128)S(1)}, u32[]{:S(2)}, u32[]{:S(2)}) async-start(f32[8,16,128]{2,1,0:T(8,128)} %shard_map.120), calls=%async_computation.4 | async-start | bytes 131072 | tf_op jit(solution)/shard_map/all_to_all | solution.py:501
  97.2 5.1 %collective-permute-start.4 = (f32[256,256]{1,0:T(8,128)}, f32[256,256]{1,0:T(8,128)S(1)}, u32[]{:S(2)}, u32[]{:S(2)}) collective-permute-start(f32[256,256]{1,0:T(8,128)} %get-tuple-element.55), channel_id=1, source_target_pairs={{0,1},{1,0},{2,3},{3,2},{4,5},{5,4},{6,7},{7,6},{8,9},{9,8},{10,11... | collective-permute-start | bytes 786440 | tf_op jit(solution)/shard_map/ppermute | solution.py:506
  102.3 0.7 collective-permute-start.5
  103.0 1.7 %all-to-all-done.4.message_ref = f32[8,16,128]{2,1,0:T(8,128)S(1)} async-done(((f32[8,16,128]{2,1,0:T(8,128)}), f32[8,16,128]{2,1,0:T(8,128)S(1)}, u32[]{:S(2)}, u32[]{:S(2)}) %all-to-all-start.4) | async-done | bytes 65568 | tf_op jit(solution)/shard_map/all_to_all | solution.py:501
  104.6 1.2 shard_map.121
  105.9 14.3 %all-to-all-start.5 = ((f32[256,1,128]{2,1,0:T(1,128)}), f32[256,1,128]{2,1,0:T(1,128)S(1)}, u32[]{:S(2)}, u32[]{:S(2)}) async-start(f32[256,1,128]{2,1,0:T(1,128)} %bitcast.8), calls=%async_computation.5 | async-start | bytes 262144 | tf_op jit(solution)/shard_map/all_to_all | solution.py:501
  120.2 0.0 collective-permute-done.4.refs_14_
  120.2 0.0 collective-permute-done.5.refs_15_
  120.2 0.0 copy-start
  120.3 5.0 %shard_map.122 = (f32[1024,256]{1,0:T(8,128)S(1)}, bf16[3,128]{1,0:T(4,128)(2,1)S(1)}, f32[1024,256]{1,0:T(8,128)}) custom-call(s32[1]{0:T(128)} %bitcast.odd_brick, s32[1,128]{1,0:T(1,128)S(1)} %get-tuple-element.32.rec_ref, s32[1,128]{1,0:T(1,128)S(1)} %get-tuple-element.33.refs_0_.cell_vec, f32[1,128]{1,0:T(1,128)S(1)} %get-tuple-element.50.refs_1_, ...), custom_call_target="tpu_custom_call" | custom-call | flops 16777216 | bytes 10485760 | tf_op jit(solution)/shard_map/pallas_call | solution.py:32
  125.2 0.6 copy.13
  125.8 7.4 %all-to-all-done.5 = f32[256,1,128]{2,1,0:T(1,128)S(1)} async-done(((f32[256,1,128]{2,1,0:T(1,128)}), f32[256,1,128]{2,1,0:T(1,128)S(1)}, u32[]{:S(2)}, u32[]{:S(2)}) %all-to-all-start.5) | async-done | bytes 131104 | tf_op jit(solution)/shard_map/all_to_all | solution.py:501
  133.2 0.0 copy-done
  133.2 2.0 %shard_map.123 = f32[1024,256]{1,0:T(8,128)} custom-call(s32[1,128]{1,0:T(1,128)S(1)} %copy-done, s32[1,128]{1,0:T(1,128)S(1)} %get-tuple-element.33.refs_0_.cell_vec, f32[256,128]{1,0:T(8,128)S(1)} %bitcast.14, f32[1024,256]{1,0:T(8,128)S(1)} %get-tuple-element.59.field_ref), custom_call_target="tpu_custom_call" | custom-call | flops 1048576 | bytes 2097152 | tf_op jit(solution)/shard_map/pallas_call | solution.py:32
  (1 shorter events, 0.0 us)
Async XLA Ops:
  2.9 17.5 %all-to-all-start = ((f32[8,16,128]{2,1,0:T(8,128)}), f32[8,16,128]{2,1,0:T(8,128)S(1)}, u32[]{:S(2)}, u32[]{:S(2)}) async-start(f32[8,16,128]{2,1,0:T(8,128)} %get-tuple-element.34), calls=%async_computation | async-start | bytes 131072 | tf_op jit(solution)/shard_map/all_to_all | solution.py:501
  21.5 23.4 %all-to-all-start.1 = ((f32[32,24,128]{2,1,0:T(8,128)}), f32[32,24,128]{2,1,0:T(8,128)S(1)}, u32[]{:S(2)}, u32[]{:S(2)}) async-start(f32[32,24,128]{2,1,0:T(8,128)} %shard_map.114), calls=%async_computation.1 | async-start | bytes 786432 | tf_op jit(solution)/shard_map/all_to_all | solution.py:501
  28.7 10.8 %collective-permute-start = (f32[264,256]{1,0:T(8,128)S(1)}, f32[264,256]{1,0:T(8,128)S(1)}, u32[]{:S(2)}, u32[]{:S(2)}) collective-permute-start(f32[264,256]{1,0:T(8,128)S(1)} %get-tuple-element.37), channel_id=1, source_target_pairs={{0,1},{1,0},{2,3},{3,2},{4,5},{5,4},{6,7},{7,6},{8,9},{9,8},{10,11... | collective-permute-start | bytes 811016 | tf_op jit(solution)/shard_map/ppermute | solution.py:506
  30.0 9.5 %collective-permute-start.1 = (f32[264,256]{1,0:T(8,128)S(1)}, f32[264,256]{1,0:T(8,128)S(1)}, u32[]{:S(2)}, u32[]{:S(2)}) collective-permute-start(f32[264,256]{1,0:T(8,128)S(1)} %get-tuple-element.38), channel_id=1, source_target_pairs={{1,2},{2,1},{3,4},{4,3},{5,6},{6,5},{7,8},{8,7},{9,10},{10,9},{11,... | collective-permute-start | bytes 811016 | tf_op jit(solution)/shard_map/ppermute | solution.py:507
  45.5 14.7 %all-to-all-start.2 = ((f32[8,16,128]{2,1,0:T(8,128)}), f32[8,16,128]{2,1,0:T(8,128)S(1)}, u32[]{:S(2)}, u32[]{:S(2)}) async-start(f32[8,16,128]{2,1,0:T(8,128)} %shard_map.116), calls=%async_computation.2 | async-start | bytes 131072 | tf_op jit(solution)/shard_map/all_to_all | solution.py:501
  61.5 28.0 %all-to-all-start.3 = ((f32[32,24,128]{2,1,0:T(8,128)}), f32[32,24,128]{2,1,0:T(8,128)S(1)}, u32[]{:S(2)}, u32[]{:S(2)}) async-start(f32[32,24,128]{2,1,0:T(8,128)} %get-tuple-element.41), calls=%async_computation.3 | async-start | bytes 786432 | tf_op jit(solution)/shard_map/all_to_all | solution.py:501
  72.8 10.7 %collective-permute-start.2 = (f32[256,256]{1,0:T(8,128)}, f32[256,256]{1,0:T(8,128)S(1)}, u32[]{:S(2)}, u32[]{:S(2)}) collective-permute-start(f32[256,256]{1,0:T(8,128)} %get-tuple-element.46), channel_id=1, source_target_pairs={{0,1},{1,0},{2,3},{3,2},{4,5},{5,4},{6,7},{7,6},{8,9},{9,8},{10,11... | collective-permute-start | bytes 786440 | tf_op jit(solution)/shard_map/ppermute | solution.py:506
  74.2 9.4 %collective-permute-start.3 = (f32[256,256]{1,0:T(8,128)}, f32[256,256]{1,0:T(8,128)S(1)}, u32[]{:S(2)}, u32[]{:S(2)}) collective-permute-start(f32[256,256]{1,0:T(8,128)} %get-tuple-element.47), channel_id=1, source_target_pairs={{1,2},{2,1},{3,4},{4,3},{5,6},{6,5},{7,8},{8,7},{9,10},{10,9},{11,... | collective-permute-start | bytes 786440 | tf_op jit(solution)/shard_map/ppermute | solution.py:507
  90.2 14.5 %all-to-all-start.4 = ((f32[8,16,128]{2,1,0:T(8,128)}), f32[8,16,128]{2,1,0:T(8,128)S(1)}, u32[]{:S(2)}, u32[]{:S(2)}) async-start(f32[8,16,128]{2,1,0:T(8,128)} %shard_map.120), calls=%async_computation.4 | async-start | bytes 131072 | tf_op jit(solution)/shard_map/all_to_all | solution.py:501
  97.2 23.0 %collective-permute-start.4 = (f32[256,256]{1,0:T(8,128)}, f32[256,256]{1,0:T(8,128)S(1)}, u32[]{:S(2)}, u32[]{:S(2)}) collective-permute-start(f32[256,256]{1,0:T(8,128)} %get-tuple-element.55), channel_id=1, source_target_pairs={{0,1},{1,0},{2,3},{3,2},{4,5},{5,4},{6,7},{7,6},{8,9},{9,8},{10,11... | collective-permute-start | bytes 786440 | tf_op jit(solution)/shard_map/ppermute | solution.py:506
  102.3 17.9 %collective-permute-start.5 = (f32[256,256]{1,0:T(8,128)}, f32[256,256]{1,0:T(8,128)S(1)}, u32[]{:S(2)}, u32[]{:S(2)}) collective-permute-start(f32[256,256]{1,0:T(8,128)} %get-tuple-element.56), channel_id=1, source_target_pairs={{1,2},{2,1},{3,4},{4,3},{5,6},{6,5},{7,8},{8,7},{9,10},{10,9},{11,... | collective-permute-start | bytes 786440 | tf_op jit(solution)/shard_map/ppermute | solution.py:507
  105.9 27.3 %all-to-all-start.5 = ((f32[256,1,128]{2,1,0:T(1,128)}), f32[256,1,128]{2,1,0:T(1,128)S(1)}, u32[]{:S(2)}, u32[]{:S(2)}) async-start(f32[256,1,128]{2,1,0:T(1,128)} %bitcast.8), calls=%async_computation.5 | async-start | bytes 262144 | tf_op jit(solution)/shard_map/all_to_all | solution.py:501
  120.2 13.0 %copy-start = (s32[1,128]{1,0:T(1,128)S(1)}, s32[1,128]{1,0:T(1,128)}, u32[]{:S(2)}) copy-start(s32[1,128]{1,0:T(1,128)} %cell_smem.1) | copy-start | bytes 1540

commit v8 on v7

--- a/solution.py
+++ b/solution.py
@@ -268,7 +268,7 @@
     return 8 + 264 * (x + 1)
 
 
-def wave_kernel(step, odd_brick, rec_ref, *refs):
+def wave_kernel(step, planes, odd_brick, rec_ref, *refs):
     refs = list(refs)
 
     def take(count):
@@ -278,12 +278,15 @@
 
     emit_ref, mine_ref, near_ref, near_cells_ref = take(4) if step else [None] * 4
     own_ref, start_ref, *sample_refs = take(4) if step == 2 else [None] * 4
-    rec_any, emit_any, field_any, prev_any, diag_any, cross_any, even_any, odd_any = take(8)
-    out_any, *outs = take(5 if step < 2 else 3)
+    inner, outer = planes == (1, 2), planes == (0, 3)
+    rec_any, emit_any, field_any, prev_any, diag_any, cross_any = take(6)
+    (done_any,) = take(1) if outer else [None]
+    even_any, odd_any = take(2) if not inner else [None] * 2
+    out_any, *outs = take(1 if inner else 5 if step < 2 else 3)
     left_ref, right_ref, prev_ref, diag_ref, cross_ref, left_skew, right_skew, left_sum, right_sum = take(9)
     rows_ref, cells_ref, rec_smem, emit_smem, sems, edge_sems, cell_sems, end_sems = take(8)
     (out_ref,) = take(1) if step < 2 else [out_any]
-    order = (1, 2, 0, 3)
+    order = planes
     fields, skews, sums = (left_ref, right_ref), (left_skew, right_skew), (left_sum, right_sum)
 
     def part(x):
@@ -313,16 +316,20 @@
             pairs += [(high.at[pl.ds(256, 8), lanes(0)], cells_ref.at[pl.ds(8, 8)])]
         return [pltpu.make_async_copy(a, b, edge_sems.at[k]) for k, (a, b) in enumerate(pairs)]
 
-    @pl.when(odd_brick[0] == 0)
-    def _():
-        for copy in bring(odd_any, even_any):
-            copy.start()
-
-    @pl.when(odd_brick[0] == 1)
-    def _():
-        for copy in bring(even_any, odd_any):
-            copy.start()
-
+    if not inner:
+
+        @pl.when(odd_brick[0] == 0)
+        def _():
+            for copy in bring(odd_any, even_any):
+                copy.start()
+
+        @pl.when(odd_brick[0] == 1)
+        def _():
+            for copy in bring(even_any, odd_any):
+                copy.start()
+
+    if outer:
+        brought = copies([(done_any.at[part(x)], out_ref.at[part(x)]) for x in (1, 2)], end_sems.at[pl.ds(6, 2)])
     for ref in fields + skews:
         for x in range(-2, 5):
             ref[base(x) + 256 : base(x) + 264, :] = jnp.zeros((8, 128), f32)
@@ -365,7 +372,7 @@
                 if 0 <= x < 4:
                     sums[h][256 * x + 8 * t : 256 * x + 8 * t + 8, :] = ahead[h] + behind[h]
 
-    ready = {1: (0, 1, 2), 2: (3,), 0: (-1,), 3: (4,)}
+    ready = {1: (0, 1, 2), 2: (3,), 0: (0, 1, 2, 3, -1) if outer else (-1,), 3: (4,)}
     for x in order:
         if x == 0:
             for copy in bring(odd_any, even_any):
@@ -411,7 +418,10 @@
                 out_ref[rows, columns] = (twice - prev_ref[rows, columns]) + (second + 0.5 * mixed)
         if step < 2:
             ending += copies([(out_ref.at[part(x)], out_any.at[part(x)])], end_sems.at[pl.ds(x, 1)])
-    if step < 2:
+    if outer:
+        for copy in brought:
+            copy.wait()
+    if step < 2 and not inner:
         value_ref, even_out, odd_out = outs[:3]
         even = out_ref.at[pl.ds(pl.multiple_of(768 - 768 * odd_brick[0], 256), 256)]
         odd = out_ref.at[pl.ds(pl.multiple_of(768 * odd_brick[0], 256), 256)]
@@ -421,7 +431,7 @@
         copy.wait()
 
 
-def wave(step, odd_brick, rec, cells, field, prev, diag, cross, edge_planes, added=(), record=()):
+def wave(step, odd_brick, rec, cells, field, prev, diag, cross, edge_planes, added=(), record=(), done=(), planes=None):
     whole = (1024, 256)
     out_shape = [HBM(whole, f32), VMEM((1, 128), f32), HBM((256, 256), f32), HBM((256, 256), f32)]
     if step == 0:
@@ -430,6 +440,8 @@
         out_shape += [HBM(whole, f32)]
     else:
         out_shape = [VMEM(whole, f32), VMEM((3, 128), jnp.bfloat16), HBM(whole, f32)]
+    if not edge_planes:
+        out_shape = out_shape[:1]
     coef = VMEM((3, 4, 256, 256), f32)
     half = VMEM((1592, 128), f32)
     inner = VMEM((1024, 128), f32)
@@ -440,14 +452,15 @@
     if step < 2:
         scratch.append(VMEM(whole, f32))
     return call(
-        functools.partial(wave_kernel, step),
+        functools.partial(wave_kernel, step, planes or (1, 2, 0, 3)),
         tuple(out_shape),
         (16 << 20, 10 << 20),
         scalars=[odd_brick],
         arrays=[rec, *added, *record],
-        far=[*cells, field, prev, diag, cross],
+        far=[*cells, field, prev, diag, cross, *done],
         free=edge_planes,
         scratch=scratch,
+        aliases={2 + len(added) + len(record) + 6: 0} if done else None,
         room=16,
     )
 
@@ -522,7 +535,10 @@
     even, odd = halos(*planes)
     right = turn(green)
     cells = (rec_cell, emit_cell)
-    following, value, *planes, near_cells = wave(0, odd_brick, rec, cells, current, before, diag, cross, (even, odd))
+    inner = wave(0, odd_brick, rec, cells, current, before, diag, cross, (), planes=(1, 2))
+    following, value, *planes, near_cells = wave(
+        0, odd_brick, rec, cells, current, before, diag, cross, (even, odd), done=inner, planes=(0, 3)
+    )
     partial = emission_start(first, delay, right)
     parts = exchange(partial, "brick")
     old = older(first, delay)

time: 136 us -> 135 us (level)
  waiting for transfers between devices: 41.2 us -> 37.4 us
  Pallas kernels: 25.8 us -> 28.5 us
    ppermute x3, waiting for transfers between devices: 17.5 us -> 13.6 us  [halos(): even = lax.ppermute(even_plane, 'brick', [(i, i ^ 1) for i in range(size)])]
    pallas_call x12 -> x13, Pallas kernels: 25.8 us -> 28.5 us  [call(): pl.pallas_call(kernel, out_shape=out_shape, in_specs=[spec(SMEM)] * len(s...]
  transfers between devices with their start and end apart: 12 -> 12, of which waited for: 6 -> 6; matrix products, arithmetic and copies ran while one was open for 0% -> 0% of each run, Pallas kernels for 13% -> 15%
where the time goes in v8:
time: 135 us; the launch traced here: 134 us
  starting transfers between devices  66.8 us (49%)
  waiting for transfers between devices  37.4 us (28%)
  Pallas kernels  28.5 us (21%)
    all_to_all x6, starting transfers between devices, exchange(): return lax.all_to_all(array, axis, 0, 0, tiled=True)  57.1 us
    pallas_call x13, Pallas kernels, call(): pl.pallas_call(kernel, out_shape=out_shape, in_specs=[spec(SMEM)] * len(s...  28.5 us
    all_to_all x6, waiting for transfers between devices, exchange(): return lax.all_to_all(array, axis, 0, 0, tiled=True)  23.7 us
    ppermute x3, waiting for transfers between devices, halos(): even = lax.ppermute(even_plane, 'brick', [(i, i ^ 1) for i in range(size)])  13.6 us
    ppermute x3, starting transfers between devices, halos(): even = lax.ppermute(even_plane, 'brick', [(i, i ^ 1) for i in range(size)])  7.74 us
  transfers between devices with their start and end apart: 12, of which 6 were waited for; matrix products, arithmetic and copies ran while one was open for 0% of the time, Pallas kernels for 15%

profile of v8, /device:TPU:1, one launch (start us, length us, event | category | flops | bytes accessed | tf_op | source)
XLA Modules:
  0.0 134.2 jit_solution(454764569565080132)
XLA Ops:
  0.6 2.3 %shard_map.112 = (f32[8,16,128]{2,1,0:T(8,128)}, f32[264,256]{1,0:T(8,128)S(1)}, f32[264,256]{1,0:T(8,128)S(1)}, s32[1,128]{1,0:T(1,128)S(1)}, s32[1,128]{1,0:T(...) custom-call(s32[1]{0:T(128)} %bitcast.1.rank, s32[1]{0:T(128)} %bitcast.odd_brick, ...), custom_call_target="tpu_custom_call" | custom-call | flops 1048576 | bytes 524288 | tf_op jit(solution)/shard_map/pallas_call | solution.py:32
  2.9 10.0 %all-to-all-start = ((f32[8,16,128]{2,1,0:T(8,128)}), f32[8,16,128]{2,1,0:T(8,128)S(1)}, u32[]{:S(2)}, u32[]{:S(2)}) async-start(f32[8,16,128]{2,1,0:T(8,128)} %get-tuple-element.34), calls=%async_computation | async-start | bytes 131072 | tf_op jit(solution)/shard_map/all_to_all | solution.py:514
  12.9 0.3 shard_map.113.right_ref.refs_0_.refs_1_
  13.2 7.2 %all-to-all-done.first_ref.refs_5_ = f32[8,16,128]{2,1,0:T(8,128)S(1)} async-done(((f32[8,16,128]{2,1,0:T(8,128)}), f32[8,16,128]{2,1,0:T(8,128)S(1)}, u32[]{:S(2)}, u32[]{:S(2)}) %all-to-all-start) | async-done | bytes 65568 | tf_op jit(solution)/shard_map/all_to_all | solution.py:514
  20.5 1.0 shard_map.114
  21.5 7.2 %all-to-all-start.1 = ((f32[32,24,128]{2,1,0:T(8,128)}), f32[32,24,128]{2,1,0:T(8,128)S(1)}, u32[]{:S(2)}, u32[]{:S(2)}) async-start(f32[32,24,128]{2,1,0:T(8,128)} %shard_map.114), calls=%async_computation.1 | async-start | bytes 786432 | tf_op jit(solution)/shard_map/all_to_all | solution.py:514
  28.7 1.3 collective-permute-start
  30.0 0.7 collective-permute-start.1
  30.7 3.9 %shard_map.115.refs_6_ = f32[1024,256]{1,0:T(8,128)} custom-call(s32[1]{0:T(128)} %bitcast.odd_brick, s32[1,128]{1,0:T(1,128)S(1)} %get-tuple-element.32.rec_ref, s32[1,128]{1,0:T(1,128)} %refs_8_.3, s32[1,128]{1,0:T(1,128)} %cell_smem.1, f32[1024,256]{1,0:T(8,128)} %bitcast.16, f32[1024,256]{1,0:T(8,128)} %bitcast.19, f32[3,4,256,256]{3,2,1,0:T(8,128)} %refs_12_.1, ...), custom_call_target="tpu_custom_call" | custom-call | flops 16777216 | bytes 10485760 | tf_op jit(solution)/shard_map/pallas_call | solution.py:32
  34.6 4.9 %collective-permute-done.refs_7_ = f32[264,256]{1,0:T(8,128)S(1)} collective-permute-done((f32[264,256]{1,0:T(8,128)S(1)}, f32[264,256]{1,0:T(8,128)S(1)}, u32[]{:S(2)}, u32[]{:S(2)}) %collective-permute-start) | collective-permute-done | bytes 270368 | tf_op jit(solution)/shard_map/ppermute | solution.py:519
  39.5 0.0 collective-permute-done.1.refs_8_
  39.5 4.2 %shard_map.116 = (f32[1024,256]{1,0:T(8,128)}, f32[1,128]{1,0:T(1,128)S(1)}, f32[256,256]{1,0:T(8,128)}, f32[256,256]{1,0:T(8,128)}, f32[8,128]{1,0:T(8,128)S(1)}) custom-call(s32[1]{0:T(128)} %bitcast.odd_brick, s32[1,128]{1,0:T(1,128)S(1)} %get-tuple-element.32.rec_ref, s32[1,128]{1,0:T(1,128)} %refs_8_.3, ...), custom_call_target="tpu_custom_call", output_to_operand_aliasing={{0}: (8, {})} | custom-call | flops 16777216 | bytes 10485760 | tf_op jit(solution)/shard_map/pallas_call | solution.py:32
  43.7 0.0 all-to-all-done.1.parts_ref
  43.7 0.7 shard_map.117
  44.3 7.2 %all-to-all-start.2 = ((f32[8,16,128]{2,1,0:T(8,128)}), f32[8,16,128]{2,1,0:T(8,128)S(1)}, u32[]{:S(2)}, u32[]{:S(2)}) async-start(f32[8,16,128]{2,1,0:T(8,128)} %shard_map.117), calls=%async_computation.2 | async-start | bytes 131072 | tf_op jit(solution)/shard_map/all_to_all | solution.py:514
  51.6 7.4 %all-to-all-done.2.message_ref = f32[8,16,128]{2,1,0:T(8,128)S(1)} async-done(((f32[8,16,128]{2,1,0:T(8,128)}), f32[8,16,128]{2,1,0:T(8,128)S(1)}, u32[]{:S(2)}, u32[]{:S(2)}) %all-to-all-start.2) | async-done | bytes 65568 | tf_op jit(solution)/shard_map/all_to_all | solution.py:514
  59.0 1.3 shard_map.119
  60.4 11.3 %all-to-all-start.3 = ((f32[32,24,128]{2,1,0:T(8,128)}), f32[32,24,128]{2,1,0:T(8,128)S(1)}, u32[]{:S(2)}, u32[]{:S(2)}) async-start(f32[32,24,128]{2,1,0:T(8,128)} %get-tuple-element.41), calls=%async_computation.3 | async-start | bytes 786432 | tf_op jit(solution)/shard_map/all_to_all | solution.py:514
  71.7 1.3 collective-permute-start.2
  73.0 0.7 collective-permute-start.3
  73.7 8.7 %collective-permute-done.2.refs_10_ = f32[256,256]{1,0:T(8,128)S(1)} collective-permute-done((f32[256,256]{1,0:T(8,128)}, f32[256,256]{1,0:T(8,128)S(1)}, u32[]{:S(2)}, u32[]{:S(2)}) %collective-permute-start.2) | collective-permute-done | bytes 262176 | tf_op jit(solution)/shard_map/ppermute | solution.py:519
  82.4 0.0 collective-permute-done.3.refs_11_
  82.4 5.9 %shard_map.120 = (f32[1024,256]{1,0:T(8,128)}, f32[1,128]{1,0:T(1,128)S(1)}, f32[256,256]{1,0:T(8,128)}, f32[256,256]{1,0:T(8,128)}, f32[1024,256]{1,0:T(8,128)}) custom-call(s32[1]{0:T(128)} %bitcast.odd_brick, s32[1,128]{1,0:T(1,128)S(1)} %get-tuple-element.32.rec_ref, s32[1,128]{1,0:T(1,128)S(1)} %get-tuple-element.33.refs_0_.cell_vec, ...), custom_call_target="tpu_custom_call" | custom-call | flops 16777216 | bytes 10485760 | tf_op jit(solution)/shard_map/pallas_call | solution.py:32
  88.3 0.0 all-to-all-done.3.parts_ref
  88.3 0.7 shard_map.121
  89.0 7.0 %all-to-all-start.4 = ((f32[8,16,128]{2,1,0:T(8,128)}), f32[8,16,128]{2,1,0:T(8,128)S(1)}, u32[]{:S(2)}, u32[]{:S(2)}) async-start(f32[8,16,128]{2,1,0:T(8,128)} %shard_map.121), calls=%async_computation.4 | async-start | bytes 131072 | tf_op jit(solution)/shard_map/all_to_all | solution.py:514
  96.0 5.1 %collective-permute-start.4 = (f32[256,256]{1,0:T(8,128)}, f32[256,256]{1,0:T(8,128)S(1)}, u32[]{:S(2)}, u32[]{:S(2)}) collective-permute-start(f32[256,256]{1,0:T(8,128)} %get-tuple-element.55), channel_id=1, source_target_pairs={{0,1},{1,0},{2,3},{3,2},{4,5},{5,4},{6,7},{7,6},{8,9},{9,8},{10,11... | collective-permute-start | bytes 786440 | tf_op jit(solution)/shard_map/ppermute | solution.py:519
  101.1 0.7 collective-permute-start.5
  101.8 1.7 %all-to-all-done.4.message_ref = f32[8,16,128]{2,1,0:T(8,128)S(1)} async-done(((f32[8,16,128]{2,1,0:T(8,128)}), f32[8,16,128]{2,1,0:T(8,128)S(1)}, u32[]{:S(2)}, u32[]{:S(2)}) %all-to-all-start.4) | async-done | bytes 65568 | tf_op jit(solution)/shard_map/all_to_all | solution.py:514
  103.5 1.2 shard_map.122
  104.7 14.3 %all-to-all-start.5 = ((f32[256,1,128]{2,1,0:T(1,128)}), f32[256,1,128]{2,1,0:T(1,128)S(1)}, u32[]{:S(2)}, u32[]{:S(2)}) async-start(f32[256,1,128]{2,1,0:T(1,128)} %bitcast.8), calls=%async_computation.5 | async-start | bytes 262144 | tf_op jit(solution)/shard_map/all_to_all | solution.py:514
  119.0 0.0 collective-permute-done.4.refs_14_
  119.0 0.0 collective-permute-done.5.refs_15_
  119.1 0.0 copy-start
  119.1 5.0 %shard_map.123 = (f32[1024,256]{1,0:T(8,128)S(1)}, bf16[3,128]{1,0:T(4,128)(2,1)S(1)}, f32[1024,256]{1,0:T(8,128)}) custom-call(s32[1]{0:T(128)} %bitcast.odd_brick, s32[1,128]{1,0:T(1,128)S(1)} %get-tuple-element.32.rec_ref, s32[1,128]{1,0:T(1,128)S(1)} %get-tuple-element.33.refs_0_.cell_vec, f32[1,128]{1,0:T(1,128)S(1)} %get-tuple-element.50.refs_1_, ...), custom_call_target="tpu_custom_call" | custom-call | flops 16777216 | bytes 10485760 | tf_op jit(solution)/shard_map/pallas_call | solution.py:32
  124.0 0.6 copy.15
  124.6 7.4 %all-to-all-done.5 = f32[256,1,128]{2,1,0:T(1,128)S(1)} async-done(((f32[256,1,128]{2,1,0:T(1,128)}), f32[256,1,128]{2,1,0:T(1,128)S(1)}, u32[]{:S(2)}, u32[]{:S(2)}) %all-to-all-start.5) | async-done | bytes 131104 | tf_op jit(solution)/shard_map/all_to_all | solution.py:514
  132.0 0.0 copy-done
  132.0 2.0 %shard_map.124 = f32[1024,256]{1,0:T(8,128)} custom-call(s32[1,128]{1,0:T(1,128)S(1)} %copy-done, s32[1,128]{1,0:T(1,128)S(1)} %get-tuple-element.33.refs_0_.cell_vec, f32[256,128]{1,0:T(8,128)S(1)} %bitcast.14, f32[1024,256]{1,0:T(8,128)S(1)} %get-tuple-element.59.field_ref), custom_call_target="tpu_custom_call" | custom-call | flops 1048576 | bytes 2097152 | tf_op jit(solution)/shard_map/pallas_call | solution.py:32
  (1 shorter events, 0.0 us)
Async XLA Ops:
  2.9 17.5 %all-to-all-start = ((f32[8,16,128]{2,1,0:T(8,128)}), f32[8,16,128]{2,1,0:T(8,128)S(1)}, u32[]{:S(2)}, u32[]{:S(2)}) async-start(f32[8,16,128]{2,1,0:T(8,128)} %get-tuple-element.34), calls=%async_computation | async-start | bytes 131072 | tf_op jit(solution)/shard_map/all_to_all | solution.py:514
  21.5 22.2 %all-to-all-start.1 = ((f32[32,24,128]{2,1,0:T(8,128)}), f32[32,24,128]{2,1,0:T(8,128)S(1)}, u32[]{:S(2)}, u32[]{:S(2)}) async-start(f32[32,24,128]{2,1,0:T(8,128)} %shard_map.114), calls=%async_computation.1 | async-start | bytes 786432 | tf_op jit(solution)/shard_map/all_to_all | solution.py:514
  28.7 10.8 %collective-permute-start = (f32[264,256]{1,0:T(8,128)S(1)}, f32[264,256]{1,0:T(8,128)S(1)}, u32[]{:S(2)}, u32[]{:S(2)}) collective-permute-start(f32[264,256]{1,0:T(8,128)S(1)} %get-tuple-element.37), channel_id=1, source_target_pairs={{0,1},{1,0},{2,3},{3,2},{4,5},{5,4},{6,7},{7,6},{8,9},{9,8},{10,11... | collective-permute-start | bytes 811016 | tf_op jit(solution)/shard_map/ppermute | solution.py:519
  30.0 9.5 %collective-permute-start.1 = (f32[264,256]{1,0:T(8,128)S(1)}, f32[264,256]{1,0:T(8,128)S(1)}, u32[]{:S(2)}, u32[]{:S(2)}) collective-permute-start(f32[264,256]{1,0:T(8,128)S(1)} %get-tuple-element.38), channel_id=1, source_target_pairs={{1,2},{2,1},{3,4},{4,3},{5,6},{6,5},{7,8},{8,7},{9,10},{10,9},{11,... | collective-permute-start | bytes 811016 | tf_op jit(solution)/shard_map/ppermute | solution.py:520
  44.3 14.7 %all-to-all-start.2 = ((f32[8,16,128]{2,1,0:T(8,128)}), f32[8,16,128]{2,1,0:T(8,128)S(1)}, u32[]{:S(2)}, u32[]{:S(2)}) async-start(f32[8,16,128]{2,1,0:T(8,128)} %shard_map.117), calls=%async_computation.2 | async-start | bytes 131072 | tf_op jit(solution)/shard_map/all_to_all | solution.py:514
  60.4 28.0 %all-to-all-start.3 = ((f32[32,24,128]{2,1,0:T(8,128)}), f32[32,24,128]{2,1,0:T(8,128)S(1)}, u32[]{:S(2)}, u32[]{:S(2)}) async-start(f32[32,24,128]{2,1,0:T(8,128)} %get-tuple-element.41), calls=%async_computation.3 | async-start | bytes 786432 | tf_op jit(solution)/shard_map/all_to_all | solution.py:514
  71.7 10.7 %collective-permute-start.2 = (f32[256,256]{1,0:T(8,128)}, f32[256,256]{1,0:T(8,128)S(1)}, u32[]{:S(2)}, u32[]{:S(2)}) collective-permute-start(f32[256,256]{1,0:T(8,128)} %get-tuple-element.46), channel_id=1, source_target_pairs={{0,1},{1,0},{2,3},{3,2},{4,5},{5,4},{6,7},{7,6},{8,9},{9,8},{10,11... | collective-permute-start | bytes 786440 | tf_op jit(solution)/shard_map/ppermute | solution.py:519
  73.0 9.4 %collective-permute-start.3 = (f32[256,256]{1,0:T(8,128)}, f32[256,256]{1,0:T(8,128)S(1)}, u32[]{:S(2)}, u32[]{:S(2)}) collective-permute-start(f32[256,256]{1,0:T(8,128)} %get-tuple-element.47), channel_id=1, source_target_pairs={{1,2},{2,1},{3,4},{4,3},{5,6},{6,5},{7,8},{8,7},{9,10},{10,9},{11,... | collective-permute-start | bytes 786440 | tf_op jit(solution)/shard_map/ppermute | solution.py:520
  89.0 14.5 %all-to-all-start.4 = ((f32[8,16,128]{2,1,0:T(8,128)}), f32[8,16,128]{2,1,0:T(8,128)S(1)}, u32[]{:S(2)}, u32[]{:S(2)}) async-start(f32[8,16,128]{2,1,0:T(8,128)} %shard_map.121), calls=%async_computation.4 | async-start | bytes 131072 | tf_op jit(solution)/shard_map/all_to_all | solution.py:514
  96.0 23.0 %collective-permute-start.4 = (f32[256,256]{1,0:T(8,128)}, f32[256,256]{1,0:T(8,128)S(1)}, u32[]{:S(2)}, u32[]{:S(2)}) collective-permute-start(f32[256,256]{1,0:T(8,128)} %get-tuple-element.55), channel_id=1, source_target_pairs={{0,1},{1,0},{2,3},{3,2},{4,5},{5,4},{6,7},{7,6},{8,9},{9,8},{10,11... | collective-permute-start | bytes 786440 | tf_op jit(solution)/shard_map/ppermute | solution.py:519
  101.1 17.9 %collective-permute-start.5 = (f32[256,256]{1,0:T(8,128)}, f32[256,256]{1,0:T(8,128)S(1)}, u32[]{:S(2)}, u32[]{:S(2)}) collective-permute-start(f32[256,256]{1,0:T(8,128)} %get-tuple-element.56), channel_id=1, source_target_pairs={{1,2},{2,1},{3,4},{4,3},{5,6},{6,5},{7,8},{8,7},{9,10},{10,9},{11,... | collective-permute-start | bytes 786440 | tf_op jit(solution)/shard_map/ppermute | solution.py:520
  104.7 27.3 %all-to-all-start.5 = ((f32[256,1,128]{2,1,0:T(1,128)}), f32[256,1,128]{2,1,0:T(1,128)S(1)}, u32[]{:S(2)}, u32[]{:S(2)}) async-start(f32[256,1,128]{2,1,0:T(1,128)} %bitcast.8), calls=%async_computation.5 | async-start | bytes 262144 | tf_op jit(solution)/shard_map/all_to_all | solution.py:514
  119.1 13.0 %copy-start = (s32[1,128]{1,0:T(1,128)S(1)}, s32[1,128]{1,0:T(1,128)}, u32[]{:S(2)}) copy-start(s32[1,128]{1,0:T(1,128)} %cell_smem.1) | copy-start | bytes 1540

commit v9 on v8

--- a/solution.py
+++ b/solution.py
@@ -282,7 +282,7 @@
     rec_any, emit_any, field_any, prev_any, diag_any, cross_any = take(6)
     (done_any,) = take(1) if outer else [None]
     even_any, odd_any = take(2) if not inner else [None] * 2
-    out_any, *outs = take(1 if inner else 5 if step < 2 else 3)
+    out_any, *outs = take(1 + step if inner else 5 - step if outer else 5 if step < 2 else 3)
     left_ref, right_ref, prev_ref, diag_ref, cross_ref, left_skew, right_skew, left_sum, right_sum = take(9)
     rows_ref, cells_ref, rec_smem, emit_smem, sems, edge_sems, cell_sems, end_sems = take(8)
     (out_ref,) = take(1) if step < 2 else [out_any]
@@ -336,7 +336,7 @@
     ending = []
     for copy in listed:
         copy.wait()
-    if step:
+    if step and not outer:
         for x in (0, 1, 2, 3):
             for copy in begun.pop(x):
                 copy.wait()
@@ -440,7 +440,9 @@
         out_shape += [HBM(whole, f32)]
     else:
         out_shape = [VMEM(whole, f32), VMEM((3, 128), jnp.bfloat16), HBM(whole, f32)]
-    if not edge_planes:
+    if step == 1 and planes:
+        out_shape = out_shape[:4] if edge_planes else out_shape[:1] + out_shape[4:]
+    elif not edge_planes:
         out_shape = out_shape[:1]
     coef = VMEM((3, 4, 256, 256), f32)
     half = VMEM((1592, 128), f32)
@@ -550,8 +552,9 @@
     parts = exchange(partial, "brick")
     added = (emit, mine, near, near_cells)
     earlier = current
-    following, value, *planes, current = wave(
-        1, odd_brick, rec, cells, following, earlier, diag, cross, (even, odd), added
+    inner, current = wave(1, odd_brick, rec, cells, following, earlier, diag, cross, (), added, planes=(1, 2))
+    following, value, *planes = wave(
+        1, odd_brick, rec, cells, current, earlier, diag, cross, (even, odd), added, done=(inner,), planes=(0, 3)
     )
     message = spread(parts, value)
 

time: 135 us -> 134 us (level)
  waiting for transfers between devices: 37.4 us -> 33.2 us
  Pallas kernels: 28.5 us -> 31.3 us
    ppermute x3, waiting for transfers between devices: 13.6 us -> 9.35 us  [halos(): even = lax.ppermute(even_plane, 'brick', [(i, i ^ 1) for i in range(size)])]
    pallas_call x13 -> x14, Pallas kernels: 28.5 us -> 31.3 us  [call(): pl.pallas_call(kernel, out_shape=out_shape, in_specs=[spec(SMEM)] * len(s...]
  transfers between devices with their start and end apart: 12 -> 12, of which waited for: 6 -> 6; matrix products, arithmetic and copies ran while one was open for 0% -> 0% of each run, Pallas kernels for 15% -> 18%
where the time goes in v9:
time: 134 us; the launch traced here: 133 us
  starting transfers between devices  66.8 us (50%)
  waiting for transfers between devices  33.2 us (25%)
  Pallas kernels  31.3 us (23%)
    all_to_all x6, starting transfers between devices, exchange(): return lax.all_to_all(array, axis, 0, 0, tiled=True)  57.1 us
    pallas_call x14, Pallas kernels, call(): pl.pallas_call(kernel, out_shape=out_shape, in_specs=[spec(SMEM)] * len(s...  31.3 us
    all_to_all x6, waiting for transfers between devices, exchange(): return lax.all_to_all(array, axis, 0, 0, tiled=True)  23.8 us
    ppermute x3, waiting for transfers between devices, halos(): even = lax.ppermute(even_plane, 'brick', [(i, i ^ 1) for i in range(size)])  9.35 us
    ppermute x3, starting transfers between devices, halos(): even = lax.ppermute(even_plane, 'brick', [(i, i ^ 1) for i in range(size)])  7.74 us
  transfers between devices with their start and end apart: 12, of which 6 were waited for; matrix products, arithmetic and copies ran while one was open for 0% of the time, Pallas kernels for 18%

profile of v9, /device:TPU:1, one launch (start us, length us, event | category | flops | bytes accessed | tf_op | source)
XLA Modules:
  0.0 132.8 jit_solution(12490328522095162786)
XLA Ops:
  0.6 2.3 %shard_map.112 = (f32[8,16,128]{2,1,0:T(8,128)}, f32[264,256]{1,0:T(8,128)S(1)}, f32[264,256]{1,0:T(8,128)S(1)}, s32[1,128]{1,0:T(1,128)S(1)}, s32[1,128]{1,0:T(...) custom-call(s32[1]{0:T(128)} %bitcast.1.rank, s32[1]{0:T(128)} %bitcast.odd_brick, ...), custom_call_target="tpu_custom_call" | custom-call | flops 1048576 | bytes 524288 | tf_op jit(solution)/shard_map/pallas_call | solution.py:32
  2.9 10.0 %all-to-all-start = ((f32[8,16,128]{2,1,0:T(8,128)}), f32[8,16,128]{2,1,0:T(8,128)S(1)}, u32[]{:S(2)}, u32[]{:S(2)}) async-start(f32[8,16,128]{2,1,0:T(8,128)} %get-tuple-element.35), calls=%async_computation | async-start | bytes 131072 | tf_op jit(solution)/shard_map/all_to_all | solution.py:516
  12.9 0.3 shard_map.113.right_ref.refs_0_.refs_1_
  13.2 7.2 %all-to-all-done.first_ref.refs_5_ = f32[8,16,128]{2,1,0:T(8,128)S(1)} async-done(((f32[8,16,128]{2,1,0:T(8,128)}), f32[8,16,128]{2,1,0:T(8,128)S(1)}, u32[]{:S(2)}, u32[]{:S(2)}) %all-to-all-start) | async-done | bytes 65568 | tf_op jit(solution)/shard_map/all_to_all | solution.py:516
  20.5 1.0 shard_map.114
  21.5 7.2 %all-to-all-start.1 = ((f32[32,24,128]{2,1,0:T(8,128)}), f32[32,24,128]{2,1,0:T(8,128)S(1)}, u32[]{:S(2)}, u32[]{:S(2)}) async-start(f32[32,24,128]{2,1,0:T(8,128)} %shard_map.114), calls=%async_computation.1 | async-start | bytes 786432 | tf_op jit(solution)/shard_map/all_to_all | solution.py:516
  28.7 1.3 collective-permute-start
  30.0 0.7 collective-permute-start.1
  30.7 3.9 %shard_map.115.refs_6_ = f32[1024,256]{1,0:T(8,128)} custom-call(s32[1]{0:T(128)} %bitcast.odd_brick, s32[1,128]{1,0:T(1,128)S(1)} %get-tuple-element.33.rec_ref, s32[1,128]{1,0:T(1,128)} %refs_8_.5, s32[1,128]{1,0:T(1,128)} %cell_smem.1, f32[1024,256]{1,0:T(8,128)} %bitcast.16, f32[1024,256]{1,0:T(8,128)} %bitcast.20, f32[3,4,256,256]{3,2,1,0:T(8,128)} %refs_12_.1, ...), custom_call_target="tpu_custom_call" | custom-call | flops 16777216 | bytes 10485760 | tf_op jit(solution)/shard_map/pallas_call | solution.py:32
  34.6 4.9 %collective-permute-done.refs_7_ = f32[264,256]{1,0:T(8,128)S(1)} collective-permute-done((f32[264,256]{1,0:T(8,128)S(1)}, f32[264,256]{1,0:T(8,128)S(1)}, u32[]{:S(2)}, u32[]{:S(2)}) %collective-permute-start) | collective-permute-done | bytes 270368 | tf_op jit(solution)/shard_map/ppermute | solution.py:521
  39.5 0.0 collective-permute-done.1.refs_8_
  39.5 4.2 %shard_map.116 = (f32[1024,256]{1,0:T(8,128)}, f32[1,128]{1,0:T(1,128)S(1)}, f32[256,256]{1,0:T(8,128)}, f32[256,256]{1,0:T(8,128)}, f32[8,128]{1,0:T(8,128)S(1)}) custom-call(s32[1]{0:T(128)} %bitcast.odd_brick, s32[1,128]{1,0:T(1,128)S(1)} %get-tuple-element.33.rec_ref, s32[1,128]{1,0:T(1,128)} %refs_8_.5, ...), custom_call_target="tpu_custom_call", output_to_operand_aliasing={{0}: (8, {})} | custom-call | flops 16777216 | bytes 10485760 | tf_op jit(solution)/shard_map/pallas_call | solution.py:32
  43.7 0.0 all-to-all-done.1.parts_ref
  43.7 0.7 shard_map.117
  44.3 7.2 %all-to-all-start.2 = ((f32[8,16,128]{2,1,0:T(8,128)}), f32[8,16,128]{2,1,0:T(8,128)S(1)}, u32[]{:S(2)}, u32[]{:S(2)}) async-start(f32[8,16,128]{2,1,0:T(8,128)} %shard_map.117), calls=%async_computation.2 | async-start | bytes 131072 | tf_op jit(solution)/shard_map/all_to_all | solution.py:516
  51.6 7.4 %all-to-all-done.2.message_ref = f32[8,16,128]{2,1,0:T(8,128)S(1)} async-done(((f32[8,16,128]{2,1,0:T(8,128)}), f32[8,16,128]{2,1,0:T(8,128)S(1)}, u32[]{:S(2)}, u32[]{:S(2)}) %all-to-all-start.2) | async-done | bytes 65568 | tf_op jit(solution)/shard_map/all_to_all | solution.py:516
  59.0 1.3 shard_map.119
  60.3 11.3 %all-to-all-start.3 = ((f32[32,24,128]{2,1,0:T(8,128)}), f32[32,24,128]{2,1,0:T(8,128)S(1)}, u32[]{:S(2)}, u32[]{:S(2)}) async-start(f32[32,24,128]{2,1,0:T(8,128)} %get-tuple-element.42), calls=%async_computation.3 | async-start | bytes 786432 | tf_op jit(solution)/shard_map/all_to_all | solution.py:516
  71.7 1.3 collective-permute-start.2
  73.0 0.7 collective-permute-start.3
  73.6 4.3 %shard_map.120 = (f32[1024,256]{1,0:T(8,128)}, f32[1024,256]{1,0:T(8,128)}) custom-call(s32[1]{0:T(128)} %bitcast.odd_brick, s32[1,128]{1,0:T(1,128)S(1)} %get-tuple-element.33.rec_ref, s32[1,128]{1,0:T(1,128)S(1)} %get-tuple-element.34.refs_0_.cell_vec, f32[1,128]{1,0:T(1,128)S(1)} %get-tuple-element.43.refs_1_, f32[8,128]{1,0:T(8,128)S(1)} %get-tuple-element.44.refs_2_, ...), custom_call_target="tpu_custom_call" | custom-call | flops 16777216 | bytes 10485760 | tf_op jit(solution)/shard_map/pallas_call | solution.py:32
  77.9 4.4 %collective-permute-done.2.refs_11_ = f32[256,256]{1,0:T(8,128)S(1)} collective-permute-done((f32[256,256]{1,0:T(8,128)}, f32[256,256]{1,0:T(8,128)S(1)}, u32[]{:S(2)}, u32[]{:S(2)}) %collective-permute-start.2) | collective-permute-done | bytes 262176 | tf_op jit(solution)/shard_map/ppermute | solution.py:521
  82.4 0.0 collective-permute-done.3.refs_12_
  82.4 4.5 %shard_map.121 = (f32[1024,256]{1,0:T(8,128)}, f32[1,128]{1,0:T(1,128)S(1)}, f32[256,256]{1,0:T(8,128)}, f32[256,256]{1,0:T(8,128)}) custom-call(s32[1]{0:T(128)} %bitcast.odd_brick, s32[1,128]{1,0:T(1,128)S(1)} %get-tuple-element.33.rec_ref, s32[1,128]{1,0:T(1,128)S(1)} %get-tuple-element.34.refs_0_.cell_vec, ...), custom_call_target="tpu_custom_call", output_to_operand_aliasing={{0}: (12, {})} | custom-call | flops 16777216 | bytes 10485760 | tf_op jit(solution)/shard_map/pallas_call | solution.py:32
  86.9 0.0 all-to-all-done.3.parts_ref
  86.9 0.7 shard_map.122
  87.5 7.0 %all-to-all-start.4 = ((f32[8,16,128]{2,1,0:T(8,128)}), f32[8,16,128]{2,1,0:T(8,128)S(1)}, u32[]{:S(2)}, u32[]{:S(2)}) async-start(f32[8,16,128]{2,1,0:T(8,128)} %shard_map.122), calls=%async_computation.4 | async-start | bytes 131072 | tf_op jit(solution)/shard_map/all_to_all | solution.py:516
  94.6 5.1 %collective-permute-start.4 = (f32[256,256]{1,0:T(8,128)}, f32[256,256]{1,0:T(8,128)S(1)}, u32[]{:S(2)}, u32[]{:S(2)}) collective-permute-start(f32[256,256]{1,0:T(8,128)} %get-tuple-element.57), channel_id=1, source_target_pairs={{0,1},{1,0},{2,3},{3,2},{4,5},{5,4},{6,7},{7,6},{8,9},{9,8},{10,11... | collective-permute-start | bytes 786440 | tf_op jit(solution)/shard_map/ppermute | solution.py:521
  99.7 0.7 collective-permute-start.5
  100.4 1.7 %all-to-all-done.4.message_ref = f32[8,16,128]{2,1,0:T(8,128)S(1)} async-done(((f32[8,16,128]{2,1,0:T(8,128)}), f32[8,16,128]{2,1,0:T(8,128)S(1)}, u32[]{:S(2)}, u32[]{:S(2)}) %all-to-all-start.4) | async-done | bytes 65568 | tf_op jit(solution)/shard_map/all_to_all | solution.py:516
  102.0 1.2 shard_map.123
  103.3 14.3 %all-to-all-start.5 = ((f32[256,1,128]{2,1,0:T(1,128)}), f32[256,1,128]{2,1,0:T(1,128)S(1)}, u32[]{:S(2)}, u32[]{:S(2)}) async-start(f32[256,1,128]{2,1,0:T(1,128)} %bitcast.8), calls=%async_computation.5 | async-start | bytes 262144 | tf_op jit(solution)/shard_map/all_to_all | solution.py:516
  117.6 0.0 collective-permute-done.4.refs_14_
  117.6 0.0 collective-permute-done.5.refs_15_
  117.6 0.0 copy-start
  117.6 5.0 %shard_map.124 = (f32[1024,256]{1,0:T(8,128)S(1)}, bf16[3,128]{1,0:T(4,128)(2,1)S(1)}, f32[1024,256]{1,0:T(8,128)}) custom-call(s32[1]{0:T(128)} %bitcast.odd_brick, s32[1,128]{1,0:T(1,128)S(1)} %get-tuple-element.33.rec_ref, s32[1,128]{1,0:T(1,128)S(1)} %get-tuple-element.34.refs_0_.cell_vec, f32[1,128]{1,0:T(1,128)S(1)} %get-tuple-element.53.refs_1_, ...), custom_call_target="tpu_custom_call" | custom-call | flops 16777216 | bytes 10485760 | tf_op jit(solution)/shard_map/pallas_call | solution.py:32
  122.6 0.6 copy.17
  123.2 7.5 %all-to-all-done.5 = f32[256,1,128]{2,1,0:T(1,128)S(1)} async-done(((f32[256,1,128]{2,1,0:T(1,128)}), f32[256,1,128]{2,1,0:T(1,128)S(1)}, u32[]{:S(2)}, u32[]{:S(2)}) %all-to-all-start.5) | async-done | bytes 131104 | tf_op jit(solution)/shard_map/all_to_all | solution.py:516
  130.7 0.0 copy-done
  130.7 2.0 %shard_map.125 = f32[1024,256]{1,0:T(8,128)} custom-call(s32[1,128]{1,0:T(1,128)S(1)} %copy-done, s32[1,128]{1,0:T(1,128)S(1)} %get-tuple-element.34.refs_0_.cell_vec, f32[256,128]{1,0:T(8,128)S(1)} %bitcast.14, f32[1024,256]{1,0:T(8,128)S(1)} %get-tuple-element.61.field_ref), custom_call_target="tpu_custom_call" | custom-call | flops 1048576 | bytes 2097152 | tf_op jit(solution)/shard_map/pallas_call | solution.py:32
  (1 shorter events, 0.0 us)
Async XLA Ops:
  2.9 17.5 %all-to-all-start = ((f32[8,16,128]{2,1,0:T(8,128)}), f32[8,16,128]{2,1,0:T(8,128)S(1)}, u32[]{:S(2)}, u32[]{:S(2)}) async-start(f32[8,16,128]{2,1,0:T(8,128)} %get-tuple-element.35), calls=%async_computation | async-start | bytes 131072 | tf_op jit(solution)/shard_map/all_to_all | solution.py:516
  21.5 22.2 %all-to-all-start.1 = ((f32[32,24,128]{2,1,0:T(8,128)}), f32[32,24,128]{2,1,0:T(8,128)S(1)}, u32[]{:S(2)}, u32[]{:S(2)}) async-start(f32[32,24,128]{2,1,0:T(8,128)} %shard_map.114), calls=%async_computation.1 | async-start | bytes 786432 | tf_op jit(solution)/shard_map/all_to_all | solution.py:516
  28.7 10.8 %collective-permute-start = (f32[264,256]{1,0:T(8,128)S(1)}, f32[264,256]{1,0:T(8,128)S(1)}, u32[]{:S(2)}, u32[]{:S(2)}) collective-permute-start(f32[264,256]{1,0:T(8,128)S(1)} %get-tuple-element.38), channel_id=1, source_target_pairs={{0,1},{1,0},{2,3},{3,2},{4,5},{5,4},{6,7},{7,6},{8,9},{9,8},{10,11... | collective-permute-start | bytes 811016 | tf_op jit(solution)/shard_map/ppermute | solution.py:521
  30.0 9.5 %collective-permute-start.1 = (f32[264,256]{1,0:T(8,128)S(1)}, f32[264,256]{1,0:T(8,128)S(1)}, u32[]{:S(2)}, u32[]{:S(2)}) collective-permute-start(f32[264,256]{1,0:T(8,128)S(1)} %get-tuple-element.39), channel_id=1, source_target_pairs={{1,2},{2,1},{3,4},{4,3},{5,6},{6,5},{7,8},{8,7},{9,10},{10,9},{11,... | collective-permute-start | bytes 811016 | tf_op jit(solution)/shard_map/ppermute | solution.py:522
  44.3 14.7 %all-to-all-start.2 = ((f32[8,16,128]{2,1,0:T(8,128)}), f32[8,16,128]{2,1,0:T(8,128)S(1)}, u32[]{:S(2)}, u32[]{:S(2)}) async-start(f32[8,16,128]{2,1,0:T(8,128)} %shard_map.117), calls=%async_computation.2 | async-start | bytes 131072 | tf_op jit(solution)/shard_map/all_to_all | solution.py:516
  60.3 26.5 %all-to-all-start.3 = ((f32[32,24,128]{2,1,0:T(8,128)}), f32[32,24,128]{2,1,0:T(8,128)S(1)}, u32[]{:S(2)}, u32[]{:S(2)}) async-start(f32[32,24,128]{2,1,0:T(8,128)} %get-tuple-element.42), calls=%async_computation.3 | async-start | bytes 786432 | tf_op jit(solution)/shard_map/all_to_all | solution.py:516
  71.7 10.7 %collective-permute-start.2 = (f32[256,256]{1,0:T(8,128)}, f32[256,256]{1,0:T(8,128)S(1)}, u32[]{:S(2)}, u32[]{:S(2)}) collective-permute-start(f32[256,256]{1,0:T(8,128)} %get-tuple-element.49), channel_id=1, source_target_pairs={{0,1},{1,0},{2,3},{3,2},{4,5},{5,4},{6,7},{7,6},{8,9},{9,8},{10,11... | collective-permute-start | bytes 786440 | tf_op jit(solution)/shard_map/ppermute | solution.py:521
  73.0 9.4 %collective-permute-start.3 = (f32[256,256]{1,0:T(8,128)}, f32[256,256]{1,0:T(8,128)S(1)}, u32[]{:S(2)}, u32[]{:S(2)}) collective-permute-start(f32[256,256]{1,0:T(8,128)} %get-tuple-element.50), channel_id=1, source_target_pairs={{1,2},{2,1},{3,4},{4,3},{5,6},{6,5},{7,8},{8,7},{9,10},{10,9},{11,... | collective-permute-start | bytes 786440 | tf_op jit(solution)/shard_map/ppermute | solution.py:522
  87.5 14.5 %all-to-all-start.4 = ((f32[8,16,128]{2,1,0:T(8,128)}), f32[8,16,128]{2,1,0:T(8,128)S(1)}, u32[]{:S(2)}, u32[]{:S(2)}) async-start(f32[8,16,128]{2,1,0:T(8,128)} %shard_map.122), calls=%async_computation.4 | async-start | bytes 131072 | tf_op jit(solution)/shard_map/all_to_all | solution.py:516
  94.6 23.0 %collective-permute-start.4 = (f32[256,256]{1,0:T(8,128)}, f32[256,256]{1,0:T(8,128)S(1)}, u32[]{:S(2)}, u32[]{:S(2)}) collective-permute-start(f32[256,256]{1,0:T(8,128)} %get-tuple-element.57), channel_id=1, source_target_pairs={{0,1},{1,0},{2,3},{3,2},{4,5},{5,4},{6,7},{7,6},{8,9},{9,8},{10,11... | collective-permute-start | bytes 786440 | tf_op jit(solution)/shard_map/ppermute | solution.py:521
  99.7 17.9 %collective-permute-start.5 = (f32[256,256]{1,0:T(8,128)}, f32[256,256]{1,0:T(8,128)S(1)}, u32[]{:S(2)}, u32[]{:S(2)}) collective-permute-start(f32[256,256]{1,0:T(8,128)} %get-tuple-element.58), channel_id=1, source_target_pairs={{1,2},{2,1},{3,4},{4,3},{5,6},{6,5},{7,8},{8,7},{9,10},{10,9},{11,... | collective-permute-start | bytes 786440 | tf_op jit(solution)/shard_map/ppermute | solution.py:522
  103.3 27.4 %all-to-all-start.5 = ((f32[256,1,128]{2,1,0:T(1,128)}), f32[256,1,128]{2,1,0:T(1,128)S(1)}, u32[]{:S(2)}, u32[]{:S(2)}) async-start(f32[256,1,128]{2,1,0:T(1,128)} %bitcast.8), calls=%async_computation.5 | async-start | bytes 262144 | tf_op jit(solution)/shard_map/all_to_all | solution.py:516
  117.6 13.0 %copy-start = (s32[1,128]{1,0:T(1,128)S(1)}, s32[1,128]{1,0:T(1,128)}, u32[]{:S(2)}) copy-start(s32[1,128]{1,0:T(1,128)} %cell_smem.1) | copy-start | bytes 1540
